TPU v7x, 32 devices: a whole 2x2x4 slice. The times are simulated.
32 devices in a mesh: fsdp: 32 (over z, y, x, core).
Axes of the slice: x: 2, y: 2, z: 4, core: 2. Of those that a mesh axis runs over, the one named last changes fastest.
Arguments:
- tokens: bfloat16 [8192, 2048], P('fsdp'), may hold values from -6 to 6
- seq_lengths: int32 [32, 2], P('fsdp'), may hold values from 0 to 256, as said below
- block_counts: int32 [32], P('fsdp'), may hold values from 1 to 2, as said below
- qkv_weight: bfloat16 [2048, 6144], P('fsdp'), may hold values from -0.125 to 0.125
- qkv_bias: bfloat16 [6144], P('fsdp'), may hold values from -3 to 3
- out_weight: bfloat16 [2048, 2048], P('fsdp'), may hold values from -0.5 to 0.5
- norm1_gain: bfloat16 [2048], P('fsdp'), may hold values from 0.5 to 1.5
- norm1_bias: bfloat16 [2048], P('fsdp'), may hold values from -2 to 2
- gate_weight: bfloat16 [2048, 5632], P('fsdp'), may hold values from -0.125 to 0.125
- up_weight: bfloat16 [2048, 5632], P('fsdp'), may hold values from -0.125 to 0.125
- down_weight: bfloat16 [2048, 5632], P('fsdp'), may hold values from -0.078125 to 0.078125
- norm2_gain: bfloat16 [2048], P('fsdp'), may hold values from 0.5 to 1.5
- norm2_bias: bfloat16 [2048], P('fsdp'), may hold values from -2 to 2
- out_grad: bfloat16 [8192, 2048], P('fsdp'), may hold values from -6 to 6
Outputs:
- layer_out: bfloat16 [8192, 2048], P('fsdp')
- tokens_grad: bfloat16 [8192, 2048], P('fsdp')
- qkv_weight_grad: float32 [2048, 6144], P('fsdp')
- qkv_bias_grad: float32 [6144], P('fsdp')
- out_weight_grad: float32 [2048, 2048], P('fsdp')
- norm1_gain_grad: float32 [2048], P('fsdp')
- norm1_bias_grad: float32 [2048], P('fsdp')
- gate_weight_grad: float32 [2048, 5632], P('fsdp')
- up_weight_grad: float32 [2048, 5632], P('fsdp')
- down_weight_grad: float32 [2048, 5632], P('fsdp')
- norm2_gain_grad: float32 [2048], P('fsdp')
- norm2_bias_grad: float32 [2048], P('fsdp')
Inputs may be any that keep to these rules, and one draw needn't show every extreme that they name: `seq_lengths`: entry j of a device's row is the length of the sequence that begins at its block j, or 0; block 0 always begins one; a sequence of length L fills ceil(L / 128) blocks and the next one begins right after them, up to the device's used blocks; some device holds one sequence of 256 tokens. `block_counts`: used blocks of each device, consistent with seq_lengths; some device uses all of its blocks.
All inputs are finite; a program needn't handle non-finite values.
Results may differ from a plain program's by a relative error of at most 0.014.
Values may be sent and summed in bfloat16 or wider, within the bound.
No kernel may reach another device: no remote copies, remote signals or barrier semaphores. Data moves between devices by JAX's collectives and lax.ppermute only.
A program may use at most 448 MiB of HBM per device.

v0:
```python
import jax
import jax.numpy as jnp
from jax import lax
from jax.sharding import PartitionSpec as P

HEAD = 64
ROT = 16
BLOCK = 128


eps_norm = 1e-05


def mat_rows(left, right):
    return lax.dot_general(
        left, right, (((0,), (0,)), ((), ())), preferred_element_type=jnp.float32
    )


def mat_cols(left, right):
    return lax.dot_general(
        left, right, (((1,), (1,)), ((), ())), preferred_element_type=jnp.float32
    )


def standardize(values):
    centre = values - jnp.mean(values, axis=1, keepdims=True)
    inverse = lax.rsqrt(jnp.mean(centre * centre, axis=1, keepdims=True) + eps_norm)
    return (centre * inverse, inverse)


def norm_back(grad_out, standard, inverse, gain):
    scaled = grad_out * gain
    inner = jnp.mean(scaled, axis=1, keepdims=True)
    along = jnp.mean(scaled * standard, axis=1, keepdims=True)
    return (
        inverse * (scaled - inner - standard * along),
        jnp.sum(grad_out * standard, axis=0),
        jnp.sum(grad_out, axis=0),
    )


def row_layout(lengths, used_blocks, row_count):
    block_index = jnp.arange(lengths.shape[0], dtype=jnp.int32)
    row_index = jnp.arange(row_count, dtype=jnp.int32)
    row_block = row_index // BLOCK
    began = jnp.max(
        jnp.where(
            (lengths[None, :] > 0) & (block_index[None, :] <= row_block[:, None]),
            block_index[None, :],
            0,
        ),
        axis=1,
    )
    position = row_index - began * BLOCK
    limit = jnp.sum(jnp.where(block_index[None, :] == began[:, None], lengths[None, :], 0), axis=1)
    valid = (position < limit) & (row_block < used_blocks)
    same = (began[:, None] == began[None, :]) & (row_index[None, :] <= row_index[:, None])
    allowed = same & valid[:, None] & valid[None, :] | (row_index[:, None] == row_index[None, :])
    return (position, valid, allowed)


def rotate(values, position, direction):
    half_rot = ROT // 2
    freqs = 10000.0 ** (-2.0 * jnp.arange(half_rot, dtype=jnp.float32) / ROT)
    angle = position.astype(jnp.float32)[:, None] * freqs[None, :]
    cosine = jnp.cos(angle)[:, None, :]
    sine = direction * jnp.sin(angle)[:, None, :]
    first = values[:, :, :half_rot]
    second = values[:, :, half_rot:ROT]
    return jnp.concatenate(
        [first * cosine - second * sine, second * cosine + first * sine, values[:, :, ROT:]], axis=2
    )


def masked_scores(query, key_rows, allowed, factor):
    scores = (
        jnp.einsum("qhd,khd->hqk", query, key_rows, preferred_element_type=jnp.float32) * factor
    )
    return jnp.where(allowed[None, :, :], scores, -1e30)


def per_device(
    tokens,
    seq_lengths,
    block_counts,
    qkv_weight,
    qkv_bias,
    out_weight,
    norm1_gain,
    norm1_bias,
    gate_weight,
    up_weight,
    down_weight,
    norm2_gain,
    norm2_bias,
    out_grad,
):
    row_count = tokens.shape[0]
    width = tokens.shape[1]
    heads = width // HEAD
    factor = HEAD ** (-0.5)
    position, valid, allowed = row_layout(seq_lengths[0], block_counts[0], row_count)
    attn_full = (
        lax.all_gather(qkv_weight, "fsdp", axis=0, tiled=True),
        lax.all_gather(out_weight, "fsdp", axis=0, tiled=True),
        lax.all_gather(norm1_gain, "fsdp", axis=0, tiled=True),
        lax.all_gather(norm1_bias, "fsdp", axis=0, tiled=True),
        lax.all_gather(qkv_bias, "fsdp", axis=0, tiled=True),
    )
    inputs = tokens.astype(jnp.float32)
    standard_one, inverse_one = standardize(inputs)
    gain_one = attn_full[2].astype(jnp.float32)
    normed_one = (standard_one * gain_one + attn_full[3].astype(jnp.float32)).astype(jnp.bfloat16)
    qkv = jnp.dot(normed_one, attn_full[0], preferred_element_type=jnp.float32) + attn_full[
        4
    ].astype(jnp.float32)
    query = rotate(qkv[:, :width].reshape(row_count, heads, HEAD), position, 1.0).astype(
        jnp.bfloat16
    )
    key_rows = rotate(
        qkv[:, width : 2 * width].reshape(row_count, heads, HEAD), position, 1.0
    ).astype(jnp.bfloat16)
    value = qkv[:, 2 * width :].reshape(row_count, heads, HEAD).astype(jnp.bfloat16)
    scores = masked_scores(query, key_rows, allowed, factor)
    top_score = jnp.max(scores, axis=2, keepdims=True)
    expo = jnp.exp(scores - top_score)
    total = jnp.sum(expo, axis=2, keepdims=True)
    log_total = top_score + jnp.log(total)
    probs_low = (expo / total).astype(jnp.bfloat16)
    mixed = (
        jnp.einsum("hqk,khd->qhd", probs_low, value, preferred_element_type=jnp.float32)
        .reshape(row_count, width)
        .astype(jnp.bfloat16)
    )
    middle = inputs + jnp.dot(mixed, attn_full[1], preferred_element_type=jnp.float32)
    mlp_full = (
        lax.all_gather(gate_weight, "fsdp", axis=0, tiled=True),
        lax.all_gather(up_weight, "fsdp", axis=0, tiled=True),
        lax.all_gather(down_weight, "fsdp", axis=0, tiled=True),
        lax.all_gather(norm2_gain, "fsdp", axis=0, tiled=True),
        lax.all_gather(norm2_bias, "fsdp", axis=0, tiled=True),
    )
    standard_two, inverse_two = standardize(middle)
    normed_two = (
        standard_two * mlp_full[3].astype(jnp.float32) + mlp_full[4].astype(jnp.float32)
    ).astype(jnp.bfloat16)
    gate = jnp.dot(normed_two, mlp_full[0], preferred_element_type=jnp.float32)
    upward = jnp.dot(normed_two, mlp_full[1], preferred_element_type=jnp.float32)
    sigma = jax.nn.sigmoid(gate)
    hidden = (gate * sigma * upward).astype(jnp.bfloat16)
    down = mat_cols(hidden, mlp_full[2])
    layer_out = jnp.where(valid[:, None], middle + down, 0.0).astype(jnp.bfloat16)
    mlp_back = (
        lax.all_gather(gate_weight, "fsdp", axis=0, tiled=True),
        lax.all_gather(up_weight, "fsdp", axis=0, tiled=True),
        lax.all_gather(down_weight, "fsdp", axis=0, tiled=True),
        lax.all_gather(norm2_gain, "fsdp", axis=0, tiled=True),
        lax.all_gather(norm2_bias, "fsdp", axis=0, tiled=True),
    )
    grad_top = jnp.where(valid[:, None], out_grad.astype(jnp.float32), 0.0)
    grad_low = grad_top.astype(jnp.bfloat16)
    down_grad = mat_rows(grad_low, hidden)
    grad_hidden = jnp.dot(grad_low, mlp_back[2], preferred_element_type=jnp.float32)
    grad_gate = (grad_hidden * upward * sigma * (1.0 + gate * (1.0 - sigma))).astype(jnp.bfloat16)
    grad_up = (grad_hidden * gate * sigma).astype(jnp.bfloat16)
    gate_grad = mat_rows(normed_two, grad_gate)
    up_grad = mat_rows(normed_two, grad_up)
    gate_share, up_share = (
        lax.psum_scatter(gate_grad, "fsdp", scatter_dimension=0, tiled=True),
        lax.psum_scatter(up_grad, "fsdp", scatter_dimension=0, tiled=True),
    )
    grad_normed_two = mat_cols(grad_gate, mlp_back[0]) + mat_cols(grad_up, mlp_back[1])
    grad_middle_norm, gain_two_grad, shift_two_grad = norm_back(
        grad_normed_two, standard_two, inverse_two, mlp_back[3].astype(jnp.float32)
    )
    down_shares = (
        lax.psum_scatter(down_grad, "fsdp", scatter_dimension=0, tiled=True),
        lax.psum_scatter(gain_two_grad, "fsdp", scatter_dimension=0, tiled=True),
        lax.psum_scatter(shift_two_grad, "fsdp", scatter_dimension=0, tiled=True),
    )
    grad_middle = grad_top + grad_middle_norm
    attn_back = (
        lax.all_gather(qkv_weight, "fsdp", axis=0, tiled=True),
        lax.all_gather(out_weight, "fsdp", axis=0, tiled=True),
        lax.all_gather(norm1_gain, "fsdp", axis=0, tiled=True),
        lax.all_gather(norm1_bias, "fsdp", axis=0, tiled=True),
        lax.all_gather(qkv_bias, "fsdp", axis=0, tiled=True),
    )
    grad_branch = grad_middle.astype(jnp.bfloat16)
    out_grad_weight = mat_rows(mixed, grad_branch)
    grad_mixed = (
        mat_cols(grad_branch, attn_back[1]).astype(jnp.bfloat16).reshape(row_count, heads, HEAD)
    )
    probs_full = jnp.exp(masked_scores(query, key_rows, allowed, factor) - log_total)
    grad_probs = jnp.einsum("qhd,khd->hqk", grad_mixed, value, preferred_element_type=jnp.float32)
    row_inner = jnp.sum(grad_probs * probs_full, axis=2, keepdims=True)
    grad_scores = (probs_full * (grad_probs - row_inner)).astype(jnp.bfloat16)
    grad_query = (
        jnp.einsum("hqk,khd->qhd", grad_scores, key_rows, preferred_element_type=jnp.float32)
        * factor
    )
    grad_key = (
        jnp.einsum("hqk,qhd->khd", grad_scores, query, preferred_element_type=jnp.float32) * factor
    )
    grad_value = jnp.einsum(
        "hqk,qhd->khd", probs_low, grad_mixed, preferred_element_type=jnp.float32
    )
    grad_qkv = jnp.concatenate(
        [
            rotate(grad_query, position, -1.0).reshape(row_count, width),
            rotate(grad_key, position, -1.0).reshape(row_count, width),
            grad_value.reshape(row_count, width),
        ],
        axis=1,
    ).astype(jnp.bfloat16)
    qkv_grad = mat_rows(normed_one, grad_qkv)
    qkv_bias_grad = jnp.sum(grad_qkv.astype(jnp.float32), axis=0)
    grad_normed_one = mat_cols(grad_qkv, attn_back[0])
    grad_input_norm, gain_one_grad, shift_one_grad = norm_back(
        grad_normed_one, standard_one, inverse_one, attn_back[2].astype(jnp.float32)
    )
    attn_shares = (
        lax.psum_scatter(qkv_grad, "fsdp", scatter_dimension=0, tiled=True),
        lax.psum_scatter(out_grad_weight, "fsdp", scatter_dimension=0, tiled=True),
        lax.psum_scatter(gain_one_grad, "fsdp", scatter_dimension=0, tiled=True),
        lax.psum_scatter(shift_one_grad, "fsdp", scatter_dimension=0, tiled=True),
        lax.psum_scatter(qkv_bias_grad, "fsdp", scatter_dimension=0, tiled=True),
    )
    tokens_grad = (grad_middle + grad_input_norm).astype(jnp.bfloat16)
    return (
        layer_out,
        tokens_grad,
        attn_shares[0],
        attn_shares[4],
        attn_shares[1],
        attn_shares[2],
        attn_shares[3],
        gate_share,
        up_share,
        down_shares[0],
        down_shares[1],
        down_shares[2],
    )


def solution(mesh):
    placed = (
        P("fsdp", None),
        P("fsdp", None),
        P("fsdp"),
        P("fsdp", None),
        P("fsdp"),
        P("fsdp", None),
        P("fsdp"),
        P("fsdp"),
        P("fsdp", None),
        P("fsdp", None),
        P("fsdp", None),
        P("fsdp"),
        P("fsdp"),
        P("fsdp", None),
    )
    return jax.shard_map(
        per_device,
        mesh=mesh,
        in_specs=placed,
        out_specs=(
            P("fsdp", None),
            P("fsdp", None),
            P("fsdp", None),
            P("fsdp"),
            P("fsdp", None),
            P("fsdp"),
            P("fsdp"),
            P("fsdp", None),
            P("fsdp", None),
            P("fsdp", None),
            P("fsdp"),
            P("fsdp"),
        ),
        check_vma=False,
    )
```

profile of v0, /device:TPU:0, one launch (start us, length us, event | category | flops | bytes accessed | tf_op | source)
XLA Modules:
  0.0 2851.1 jit_solution(1925470938448877919)
XLA Ops:
  12.6 43.5 %all-reduce.11 = (bf16[6144]{0:T(1024)(128)(2,1)S(1)}, bf16[2048]{0:T(1024)(128)(2,1)S(1)}, bf16[2048]{0:T(1024)(128)(2,1)S(1)}, bf16[2048]{0:T(1024)(128)(2,1)S(1)}, bf16[2048]{0:T(1024)(128)(2,1)S(1)}) all-reduce(bf16[6144]{0:T(1024)(128)(2,1)S(1)} %dynamic-update-slice.2, ...), channel_id=1, replica_groups=mesh['fsdp'=32] {'fsdp'}, use_global_device_ids=true, to_apply=%add.2 | all-reduce | flops 14336 | bytes 57344
  58.6 111.2 %all-gather.6.cloned.1.call-done = bf16[2048,6144]{1,0:T(8,128)(2,1)} async-done(((bf16[64,6144]{1,0:T(8,128)(2,1)}), bf16[2048,6144]{1,0:T(8,128)(2,1)}) %all-gather.6.cloned.1.call-update) | async-done | bytes 25165840 | tf_op jit(solution)/shard_map/all_gather | solution.py:105
  169.8 11.8 convolution_add_fusion
  189.6 3.3 copy.58
  200.7 2.4 divide_convert_fusion
  206.9 41.5 %all-gather.8.cloned.1.call-done = bf16[2048,2048]{1,0:T(8,128)(2,1)} async-done(((bf16[64,2048]{1,0:T(8,128)(2,1)}), bf16[2048,2048]{1,0:T(8,128)(2,1)}) %all-gather.8.cloned.1.call-update) | async-done | bytes 8388624 | tf_op jit(solution)/shard_map/all_gather | solution.py:106
  248.3 6.2 fusion.45
  257.2 137.2 %all-gather.12.cloned.1.call-done = bf16[2048,5632]{1,0:T(8,128)(2,1)} async-done(((bf16[64,5632]{1,0:T(8,128)(2,1)}), bf16[2048,5632]{1,0:T(8,128)(2,1)}) %all-gather.12.cloned.1.call-update) | async-done | bytes 23068688 | tf_op jit(solution)/shard_map/all_gather | solution.py:139
  394.4 12.6 fusion.47
  407.1 132.9 %all-gather.10.cloned.1.call-done = bf16[2048,5632]{1,0:T(8,128)(2,1)} async-done(((bf16[64,5632]{1,0:T(8,128)(2,1)}), bf16[2048,5632]{1,0:T(8,128)(2,1)}) %all-gather.10.cloned.1.call-update) | async-done | bytes 23068688 | tf_op jit(solution)/shard_map/all_gather | solution.py:138
  539.9 12.6 fusion.46
  552.5 132.9 %all-gather.14.cloned.1.call-done = bf16[2048,5632]{1,0:T(8,128)(2,1)} async-done(((bf16[64,5632]{1,0:T(8,128)(2,1)}), bf16[2048,5632]{1,0:T(8,128)(2,1)}) %all-gather.14.cloned.1.call-update) | async-done | bytes 23068688 | tf_op jit(solution)/shard_map/all_gather | solution.py:140
  685.4 17.1 multiply_convert_fusion.1
  702.6 12.9 fusion.48
  715.5 13.8 multiply_reduce_fusion.1
  730.0 2.8 multiply_add_fusion
  734.2 8.2 fusion.20
  744.0 7.1 convolution_convert_fusion
  752.8 5.9 multiply_reduce_fusion
  759.4 2.6 multiply_convert_fusion
  769.6 20.2 fusion.40
  791.1 20.3 fusion.24
  812.7 20.2 fusion.50
  832.9 20.4 fusion.49
  856.8 13.3 fusion.17
  870.1 41.2 %all-reduce.10 = (f32[6144]{0:T(1024)S(1)}, f32[2048]{0:T(1024)S(1)}, f32[2048]{0:T(1024)S(1)}, f32[2048]{0:T(1024)S(1)}, f32[2048]{0:T(1024)S(1)}) all-reduce(f32[6144]{0:T(1024)S(1)} %convert_reduce_fusion, f32[2048]{0:T(1024)S(1)} %get-tuple-element.14, ...), channel_id=3, replica_groups=mesh['fsdp'=32] {'fsdp'}, use_global_device_ids=true, to_apply=%region_15.16.clone | all-reduce | flops 14336 | bytes 114688
  914.2 4.2 fusion.16
  918.4 12.5 fusion.3
  930.9 434.2 %reduce-scatter.6.cloned.1.call-done = f32[64,6144]{1,0:T(8,128)} async-done(((f32[2048,6144]{1,0:T(8,128)}), f32[64,6144]{1,0:T(8,128)}) %reduce-scatter.6.cloned.1.call-update) | async-done | bytes 1572880 | tf_op jit(solution)/shard_map/reduce_scatter | solution.py:224
  1365.2 486.9 %reduce-scatter.14.cloned.1.call-done = f32[64,5632]{1,0:T(8,128)} async-done(((f32[2048,5632]{1,0:T(8,128)}), f32[64,5632]{1,0:T(8,128)}) %reduce-scatter.14.cloned.1.call-update) | async-done | bytes 1441808 | tf_op jit(solution)/shard_map/reduce_scatter | solution.py:178
  1852.1 496.0 %reduce-scatter.12.cloned.1.call-done = f32[64,5632]{1,0:T(8,128)} async-done(((f32[2048,5632]{1,0:T(8,128)}), f32[64,5632]{1,0:T(8,128)}) %reduce-scatter.12.cloned.1.call-update) | async-done | bytes 1441808 | tf_op jit(solution)/shard_map/reduce_scatter | solution.py:171
  2348.0 495.8 %reduce-scatter.10.cloned.1.call-done = f32[64,5632]{1,0:T(8,128)} async-done(((f32[2048,5632]{1,0:T(8,128)}), f32[64,5632]{1,0:T(8,128)}) %reduce-scatter.10.cloned.1.call-update) | async-done | bytes 1441808 | tf_op jit(solution)/shard_map/reduce_scatter | solution.py:170
  (185 shorter events, 51.3 us)
Async XLA Ops:
  7.2 4.4 copy-start.45
  7.2 4.7 copy-start.46
  7.2 4.9 copy-start.47
  7.2 5.1 copy-start.48
  7.2 49.6 %copy-start.43 = (s32[1,2]{1,0:T(1,128)S(1)}, s32[1,2]{1,0:T(1,128)}, u32[]{:S(2)}) copy-start(s32[1,2]{1,0:T(1,128)} %param.15) | copy-start | bytes 28
  7.2 49.8 %copy-start.5 = (bf16[256,2048]{1,0:T(8,128)(2,1)S(1)}, bf16[256,2048]{1,0:T(8,128)(2,1)}, u32[]{:S(2)}) copy-start(bf16[256,2048]{1,0:T(8,128)(2,1)} %param.14) | copy-start | bytes 3145732
  7.3 162.6 %all-gather.6.cloned.1.call-start = ((), (), s32[]{:S(2)}) async-start(), calls=%async_computation.5 | async-start | bytes 25952256 | tf_op jit(solution)/shard_map/all_gather | solution.py:105
  8.0 240.4 %all-gather.8.cloned.1.call-start = ((), (), s32[]{:S(2)}) async-start(), calls=%async_computation.6 | async-start | bytes 8650752 | tf_op jit(solution)/shard_map/all_gather | solution.py:106
  8.7 385.7 %all-gather.12.cloned.1.call-start = ((), (), s32[]{:S(2)}) async-start(), calls=%async_computation.8 | async-start | bytes 23789568 | tf_op jit(solution)/shard_map/all_gather | solution.py:139
  9.5 530.5 %all-gather.10.cloned.1.call-start = ((), (), s32[]{:S(2)}) async-start(), calls=%async_computation.7 | async-start | bytes 23789568 | tf_op jit(solution)/shard_map/all_gather | solution.py:138
  10.0 675.4 %all-gather.14.cloned.1.call-start = ((), (), s32[]{:S(2)}) async-start(), calls=%async_computation.9 | async-start | bytes 23789568 | tf_op jit(solution)/shard_map/all_gather | solution.py:140
  10.6 920.3 %reduce-scatter.8.cloned.1.call-start = ((), (), s32[]{:S(2)}) async-start(), calls=%async_computation.11 | async-start | bytes 17301504 | tf_op jit(solution)/shard_map/reduce_scatter | solution.py:225
  56.2 125.4 %copy-start.23 = (f32[2048]{0:T(1024)}, f32[2048]{0:T(1024)S(1)}, u32[]{:S(2)}) copy-start(f32[2048]{0:T(1024)S(1)} %convert_element_type.89) | copy-start | bytes 24580
  56.2 125.4 %copy-start.25 = (f32[2048]{0:T(1024)}, f32[2048]{0:T(1024)S(1)}, u32[]{:S(2)}) copy-start(f32[2048]{0:T(1024)S(1)} %convert_element_type.90) | copy-start | bytes 24580
  57.3 124.4 %copy-start.31 = (f32[256]{0:T(256)}, f32[256]{0:T(256)S(1)}, u32[]{:S(2)}) copy-start(f32[256]{0:T(256)S(1)} %broadcast_multiply_fusion.6) | copy-start | bytes 3076
  57.7 123.9 %copy-start.33 = (f32[256]{0:T(256)}, f32[256]{0:T(256)S(1)}, u32[]{:S(2)}) copy-start(f32[256]{0:T(256)S(1)} %add_rsqrt_fusion.1) | copy-start | bytes 3076
  57.7 123.9 %copy-start.37 = (pred[256]{0:T(512)(128)(4,1)}, pred[256]{0:T(512)(128)(4,1)S(1)}, u32[]{:S(2)}) copy-start(pred[256]{0:T(512)(128)(4,1)S(1)} %compare_and_fusion) | copy-start | bytes 772
  187.7 15.4 copy-start.14
  189.6 6.4 copy-start.21
  248.3 7.4 copy-start.36
  254.5 475.5 %copy-start.3 = (f32[256,2048]{1,0:T(8,128)}, f32[256,2048]{1,0:T(8,128)S(1)}, u32[]{:S(2)}) copy-start(f32[256,2048]{1,0:T(8,128)S(1)} %get-tuple-element.53) | copy-start | bytes 6291460
  730.0 4.2 copy-start.9
  742.4 622.8 %reduce-scatter.6.cloned.1.call-start = ((), (), s32[]{:S(2)}) async-start(), calls=%async_computation.10 | async-start | bytes 51904512 | tf_op jit(solution)/shard_map/reduce_scatter | solution.py:224
  752.8 6.0 copy-start.16
  752.8 6.0 slice-start
  752.8 6.6 slice-start.1
  789.9 1062.2 %reduce-scatter.14.cloned.1.call-start = ((), (), s32[]{:S(2)}) async-start(), calls=%async_computation.14 | async-start | bytes 47579136 | tf_op jit(solution)/shard_map/reduce_scatter | solution.py:178
  811.5 1536.6 %reduce-scatter.12.cloned.1.call-start = ((), (), s32[]{:S(2)}) async-start(), calls=%async_computation.13 | async-start | bytes 47579136 | tf_op jit(solution)/shard_map/reduce_scatter | solution.py:171
  832.9 2011.0 %reduce-scatter.10.cloned.1.call-start = ((), (), s32[]{:S(2)}) async-start(), calls=%async_computation.12 | async-start | bytes 47579136 | tf_op jit(solution)/shard_map/reduce_scatter | solution.py:170
  856.7 13.3 copy-start.41
  856.8 13.3 copy-start.42
  914.2 4.2 copy-start.4
  (29 other events, 55.9 us)
Sparse Core Ops, SparseCore 0:
  10.9 158.8 all-gather.5
  172.7 75.5 all-gather.7
  251.2 143.1 all-gather.11
  397.1 142.7 all-gather.9
  542.6 142.7 all-gather.13
  742.5 182.4 reduce-scatter.7
  932.0 433.1 reduce-scatter.5
  1368.1 483.9 reduce-scatter.13
  1855.0 493.0 reduce-scatter.11
  2350.8 493.0 reduce-scatter.9
where the time goes:
time: 2870 us; the launch traced here: 2850 us
  waiting for transfers between devices  2470 us (86%)
  matrix products  222 us (8%)
  blocking collectives  84.7 us (3%)
  local copies, waits for them, and re-layouts  33.3 us (1%)
    reduce_scatter x1, waiting for transfers between devices, per_device(): lax.psum_scatter(up_grad, 'fsdp', scatter_dimension=0, tiled=True)  496 us
    reduce_scatter x1, waiting for transfers between devices, per_device(): lax.psum_scatter(gate_grad, 'fsdp', scatter_dimension=0, tiled=True)  496 us
    reduce_scatter x1, waiting for transfers between devices, per_device(): lax.psum_scatter(down_grad, 'fsdp', scatter_dimension=0, tiled=True)  487 us
    reduce_scatter x1, waiting for transfers between devices, per_device(): lax.psum_scatter(qkv_grad, 'fsdp', scatter_dimension=0, tiled=True)  434 us
    all_gather x1, waiting for transfers between devices, per_device(): lax.all_gather(up_weight, 'fsdp', axis=0, tiled=True)  137 us
    all_gather x1, waiting for transfers between devices, per_device(): lax.all_gather(down_weight, 'fsdp', axis=0, tiled=True)  133 us
    all_gather x1, waiting for transfers between devices, per_device(): lax.all_gather(gate_weight, 'fsdp', axis=0, tiled=True)  133 us
    all_gather x1, waiting for transfers between devices, per_device(): lax.all_gather(qkv_weight, 'fsdp', axis=0, tiled=True)  111 us
  transfers between devices with their start and end apart: 10, of which 9 were waited for; matrix products, arithmetic and copies ran while one was open for 7% of the time, Pallas kernels for 0%

commit v1 on v0

v1 whole, which is shorter than its diff:
```python
import jax
import jax.numpy as jnp
from jax import lax
from jax.sharding import Mesh, PartitionSpec as P

HEAD = 64
ROT = 16
BLOCK = 128
PARTS = 8
LINE = 4

AXES = ("z", "y", "x", "c", "s")
PLANE = ("y", "x", "c")
SWAP = ((0, 1), (1, 0))
NEAR = ((0, 1), (1, 0), (2, 3), (3, 2))
FAR = ((0, 2), (1, 3), (2, 0), (3, 1))

eps_norm = 1e-05
f32 = jnp.float32
bf16 = jnp.bfloat16


def mat_rows(left, right, kind=f32):
    return lax.dot_general(
        left, right, (((0,), (0,)), ((), ())), preferred_element_type=f32
    ).astype(kind)


def mat_cols(left, right):
    return lax.dot_general(left, right, (((1,), (1,)), ((), ())), preferred_element_type=f32)


def mat(left, right):
    return jnp.dot(left, right, preferred_element_type=f32)


def over_x(values):
    return lax.ppermute(values, "x", SWAP)


def over_y(values):
    return lax.ppermute(values, "y", SWAP)


def over_c(values):
    return lax.ppermute(values, "c", SWAP)


def gather_plane(own):
    half = own.shape[0] // 2
    from_x = over_x(own)
    from_y = over_y(own)
    far_low = over_x(from_y[:half])
    far_high = over_y(from_x[half:])
    line = [own, from_x, from_y, far_low, far_high]
    return jnp.concatenate(line + [over_c(part) for part in line], axis=0)


def scatter_plane(kept, sent, rows):
    width = kept.shape[1]
    half = rows // 2
    joined = kept.reshape(4, rows, width) + over_c(sent).reshape(4, rows, width).astype(f32)
    far = joined[3].astype(bf16)
    low = over_x(far[:half]).astype(f32)
    high = over_y(far[half:]).astype(f32)
    for_x = jnp.concatenate([joined[1, :half], joined[1, half:] + high], axis=0).astype(bf16)
    for_y = jnp.concatenate([joined[2, :half] + low, joined[2, half:]], axis=0).astype(bf16)
    return joined[0] + over_x(for_x).astype(f32) + over_y(for_y).astype(f32)


def exchange(blocks, me):
    result = blocks
    for mask in range(1, PARTS):
        there = me ^ mask
        piece = lax.dynamic_index_in_dim(blocks, there, 0, keepdims=True)
        came = lax.ppermute(piece, PLANE, [(i, i ^ mask) for i in range(PARTS)])
        result = lax.dynamic_update_slice_in_dim(result, came, there, 0)
    return result


def doubled(values, axis, perm, upper):
    other = lax.ppermute(values, axis, perm)
    return jnp.where(
        upper,
        jnp.concatenate([other, values], axis=0),
        jnp.concatenate([values, other], axis=0),
    )


def halved(values, axis, perm, upper):
    half = values.shape[0] // 2
    low, high = values[:half], values[half:]
    came = lax.ppermute(jnp.where(upper, low, high), axis, perm)
    return jnp.where(upper, high, low) + came


def standardize(values):
    centre = values - jnp.mean(values, axis=1, keepdims=True)
    inverse = lax.rsqrt(jnp.mean(centre * centre, axis=1, keepdims=True) + eps_norm)
    return (centre * inverse, inverse)


def norm_back(grad_out, standard, inverse, gain):
    scaled = grad_out * gain
    inner = jnp.mean(scaled, axis=1, keepdims=True)
    along = jnp.mean(scaled * standard, axis=1, keepdims=True)
    return (
        inverse * (scaled - inner - standard * along),
        jnp.sum(grad_out * standard, axis=0),
        jnp.sum(grad_out, axis=0),
    )


def row_layout(lengths, used_blocks, row_count):
    block_index = jnp.arange(lengths.shape[0], dtype=jnp.int32)
    row_index = jnp.arange(row_count, dtype=jnp.int32)
    row_block = row_index // BLOCK
    began = jnp.max(
        jnp.where(
            (lengths[None, :] > 0) & (block_index[None, :] <= row_block[:, None]),
            block_index[None, :],
            0,
        ),
        axis=1,
    )
    position = row_index - began * BLOCK
    limit = jnp.sum(jnp.where(block_index[None, :] == began[:, None], lengths[None, :], 0), axis=1)
    valid = (position < limit) & (row_block < used_blocks)
    same = (began[:, None] == began[None, :]) & (row_index[None, :] <= row_index[:, None])
    allowed = same & valid[:, None] & valid[None, :] | (row_index[:, None] == row_index[None, :])
    return (position, valid, allowed)


def rotate(values, position, direction):
    half_rot = ROT // 2
    freqs = 10000.0 ** (-2.0 * jnp.arange(half_rot, dtype=f32) / ROT)
    angle = position.astype(f32)[..., None] * freqs
    cosine = jnp.cos(angle)[:, :, None, :]
    sine = direction * jnp.sin(angle)[:, :, None, :]
    first = values[..., :half_rot]
    second = values[..., half_rot:ROT]
    return jnp.concatenate(
        [first * cosine - second * sine, second * cosine + first * sine, values[..., ROT:]], axis=3
    )


def per_device(
    tokens,
    seq_lengths,
    block_counts,
    qkv_weight,
    qkv_bias,
    out_weight,
    norm1_gain,
    norm1_bias,
    gate_weight,
    up_weight,
    down_weight,
    norm2_gain,
    norm2_bias,
    out_grad,
):
    rows, width = tokens.shape
    share = norm1_gain.shape[0]
    bias_share = qkv_bias.shape[0]
    hidden_share = gate_weight.shape[1] // PARTS
    heads = width // HEAD // PARTS
    head_cols = heads * HEAD
    spread = lax.axis_size("s")
    factor = HEAD ** (-0.5)
    iz = lax.axis_index("z")
    iy = lax.axis_index("y")
    ix = lax.axis_index("x")
    ic = lax.axis_index("c")
    me = iy * 4 + ix * 2 + ic

    def spread_gather(values, axis):
        return lax.all_gather(values, "s", axis=axis, tiled=True) if spread > 1 else values

    def spread_scatter(values, axis):
        if spread == 1:
            return values
        return lax.psum_scatter(values, "s", scatter_dimension=axis, tiled=True)

    def line_gather(values):
        return lax.all_gather(values, "z", axis=0, tiled=True)

    def line_scatter(values):
        return lax.psum_scatter(values, "z", scatter_dimension=0, tiled=True)

    out_full = line_gather(spread_gather(out_weight, 0))

    position, valid, _ = row_layout(seq_lengths[0], block_counts[0], rows)
    packed = jnp.concatenate(
        [
            norm1_gain,
            norm1_bias,
            norm2_gain,
            norm2_bias,
            qkv_bias,
            seq_lengths[0].astype(bf16),
            block_counts.astype(bf16),
        ]
    )
    packed_size = packed.shape[0]
    packed = jnp.pad(packed, (0, -packed_size % 128))[None, :]

    qkv_blocks = (
        qkv_weight.reshape(share, 3 * heads, PARTS, HEAD)
        .transpose(2, 0, 1, 3)
        .reshape(PARTS, share, 3 * head_cols)
    )
    qkv_rows = spread_gather(exchange(qkv_blocks, me), 1)
    qkv_full = line_gather(qkv_rows.reshape(-1, 3 * head_cols))

    tokens_all = gather_plane(tokens)

    plane_pack = doubled(packed, "c", SWAP, ic == 1)
    plane_pack = doubled(plane_pack, "x", SWAP, ix == 1)
    plane_pack = doubled(plane_pack, "y", SWAP, iy == 1)
    all_pack = spread_gather(plane_pack[:, None], 1).reshape(PARTS * spread, -1)
    all_pack = doubled(all_pack, "z", NEAR, iz % 2 == 1)
    all_pack = doubled(all_pack, "z", FAR, iz >= 2)

    def vector(index):
        return all_pack[:, index * share : (index + 1) * share].reshape(width).astype(f32)

    gain_one, shift_one, gain_two, shift_two = (vector(index) for index in range(4))
    bias_full = all_pack[:, 4 * share : 4 * share + bias_share].reshape(3 * heads, PARTS, HEAD)
    bias_mine = lax.dynamic_index_in_dim(bias_full, me, 1, keepdims=False).reshape(3 * head_cols)

    relative = [core + 4 * dy + 2 * dx for core in (0, 1) for dy in (0, 1) for dx in (0, 1)]
    marks = plane_pack[:, 4 * share + bias_share : 4 * share + bias_share + 3].astype(jnp.int32)
    marks = jnp.stack(
        [lax.dynamic_index_in_dim(marks, me ^ mask, 0, keepdims=False) for mask in relative]
    )
    position_all, _, allowed_all = jax.vmap(lambda lengths, used: row_layout(lengths, used, rows))(
        marks[:, :2], marks[:, 2]
    )

    mlp_blocks = jnp.stack(
        [
            weight.reshape(share, PARTS, hidden_share).transpose(1, 0, 2)
            for weight in (gate_weight, up_weight, down_weight)
        ],
        axis=1,
    )
    mlp_rows = spread_gather(exchange(mlp_blocks, me), 2)
    gate_full, up_full, down_full = (
        line_gather(mlp_rows[:, index].reshape(-1, hidden_share)) for index in range(3)
    )

    standard_all, inverse_all = standardize(tokens_all.astype(f32))
    normed_one = (standard_all * gain_one + shift_one).astype(bf16)
    qkv = mat(normed_one, qkv_full) + bias_mine.astype(f32)

    def split_heads(values):
        return values.reshape(PARTS, rows, heads, HEAD)

    query = rotate(split_heads(qkv[:, :head_cols]), position_all, 1.0).astype(bf16)
    key_rows = rotate(
        split_heads(qkv[:, head_cols : 2 * head_cols]), position_all, 1.0
    ).astype(bf16)
    value = split_heads(qkv[:, 2 * head_cols :]).astype(bf16)
    scores = jnp.einsum("gqhd,gkhd->ghqk", query, key_rows, preferred_element_type=f32) * factor
    scores = jnp.where(allowed_all[:, None], scores, -1e30)
    expo = jnp.exp(scores - jnp.max(scores, axis=3, keepdims=True))
    probs = expo / jnp.sum(expo, axis=3, keepdims=True)
    probs_low = probs.astype(bf16)
    mixed = (
        jnp.einsum("ghqk,gkhd->gqhd", probs_low, value, preferred_element_type=f32)
        .reshape(PARTS * rows, head_cols)
        .astype(bf16)
    )
    half_rows = 4 * rows
    out_kept = mat(mixed[:half_rows], out_full)
    out_sent = mat(mixed[half_rows:], out_full).astype(bf16)
    middle = tokens.astype(f32) + scatter_plane(out_kept, out_sent, rows)

    standard_two, inverse_two = standardize(middle)
    normed_two = gather_plane((standard_two * gain_two + shift_two).astype(bf16))

    grad_top = jnp.where(valid[:, None], out_grad.astype(f32), 0.0)
    grad_low = gather_plane(grad_top.astype(bf16))

    gate = mat(normed_two, gate_full)
    upward = mat(normed_two, up_full)
    sigma = jax.nn.sigmoid(gate)
    hidden = (gate * sigma * upward).astype(bf16)
    down_grad = line_scatter(mat_rows(grad_low, hidden, bf16))
    grad_hidden = mat(grad_low, down_full)
    grad_gate = (grad_hidden * upward * sigma * (1.0 + gate * (1.0 - sigma))).astype(bf16)
    grad_up = (grad_hidden * gate * sigma).astype(bf16)

    def back_two(low, high):
        return mat_cols(grad_gate[low:high], gate_full) + mat_cols(grad_up[low:high], up_full)

    grad_normed_two = scatter_plane(
        back_two(0, half_rows), back_two(half_rows, 2 * half_rows).astype(bf16), rows
    )
    gate_grad = line_scatter(mat_rows(normed_two, grad_gate, bf16))
    up_grad = line_scatter(mat_rows(normed_two, grad_up, bf16))

    down = scatter_plane(
        mat_cols(hidden[:half_rows], down_full),
        mat_cols(hidden[half_rows:], down_full).astype(bf16),
        rows,
    )
    layer_out = jnp.where(valid[:, None], middle + down, 0.0).astype(bf16)

    grad_middle_norm, gain_two_grad, shift_two_grad = norm_back(
        grad_normed_two, standard_two, inverse_two, gain_two
    )
    grad_middle = grad_top + grad_middle_norm
    grad_branch = gather_plane(grad_middle.astype(bf16))
    out_grad_weight = line_scatter(mat_rows(mixed, grad_branch, bf16))

    grad_mixed = split_heads(mat_cols(grad_branch, out_full).astype(bf16))
    grad_probs = jnp.einsum("gqhd,gkhd->ghqk", grad_mixed, value, preferred_element_type=f32)
    row_inner = jnp.sum(grad_probs * probs, axis=3, keepdims=True)
    grad_scores = (probs * (grad_probs - row_inner)).astype(bf16)
    grad_query = (
        jnp.einsum("ghqk,gkhd->gqhd", grad_scores, key_rows, preferred_element_type=f32) * factor
    )
    grad_key = (
        jnp.einsum("ghqk,gqhd->gkhd", grad_scores, query, preferred_element_type=f32) * factor
    )
    grad_value = jnp.einsum("ghqk,gqhd->gkhd", probs_low, grad_mixed, preferred_element_type=f32)

    def join_heads(values):
        return values.reshape(PARTS * rows, head_cols)

    grad_qkv = jnp.concatenate(
        [
            join_heads(rotate(grad_query, position_all, -1.0)),
            join_heads(rotate(grad_key, position_all, -1.0)),
            join_heads(grad_value),
        ],
        axis=1,
    ).astype(bf16)
    qkv_grad = line_scatter(mat_rows(normed_one, grad_qkv, bf16))
    bias_part = jnp.sum(grad_qkv.astype(f32), axis=0).reshape(3 * heads, 1, HEAD)
    bias_grad = jnp.where(
        lax.broadcasted_iota(jnp.int32, (3 * heads, PARTS, HEAD), 1) == me, bias_part, 0.0
    )

    grad_normed_one = scatter_plane(
        mat_cols(grad_qkv[:half_rows], qkv_full),
        mat_cols(grad_qkv[half_rows:], qkv_full).astype(bf16),
        rows,
    )
    grad_input_norm, gain_one_grad, shift_one_grad = norm_back(
        grad_normed_one, standard_all[:rows], inverse_all[:rows], gain_one
    )
    tokens_grad = (grad_middle + grad_input_norm).astype(bf16)

    devices = LINE * PARTS * spread
    small = jnp.concatenate(
        [
            part.reshape(devices, -1)
            for part in (gain_one_grad, shift_one_grad, gain_two_grad, shift_two_grad, bias_grad)
        ],
        axis=1,
    )
    small = halved(small, "z", FAR, iz >= 2)
    small = halved(small, "z", NEAR, iz % 2 == 1)
    small = halved(small, "y", SWAP, iy == 1)
    small = halved(small, "x", SWAP, ix == 1)
    small = halved(small, "c", SWAP, ic == 1)
    small = spread_scatter(small, 0)[0]

    mlp_back = jnp.stack(
        [part.reshape(PARTS, -1, hidden_share) for part in (gate_grad, up_grad, down_grad)], axis=1
    )
    mlp_back = exchange(spread_scatter(mlp_back, 2), me)
    gate_share, up_share, down_share = (
        mlp_back[:, index].transpose(1, 0, 2).reshape(share, -1).astype(f32) for index in range(3)
    )
    qkv_back = exchange(spread_scatter(qkv_grad.reshape(PARTS, -1, 3 * head_cols), 1), me)
    qkv_share = (
        qkv_back.reshape(PARTS, share, 3 * heads, HEAD)
        .transpose(1, 2, 0, 3)
        .reshape(share, 3 * width)
        .astype(f32)
    )
    out_share = spread_scatter(out_grad_weight, 0).astype(f32)
    return (
        layer_out,
        tokens_grad,
        qkv_share,
        small[4 * share :],
        out_share,
        small[:share],
        small[share : 2 * share],
        gate_share,
        up_share,
        down_share,
        small[2 * share : 3 * share],
        small[3 * share : 4 * share],
    )


def solution(mesh):
    devices = mesh.devices.reshape(LINE, 2, 2, 2, -1)
    rows, flat = P(AXES, None), P(AXES)
    return jax.shard_map(
        per_device,
        mesh=Mesh(devices, AXES),
        in_specs=(
            rows,
            rows,
            flat,
            rows,
            flat,
            rows,
            flat,
            flat,
            rows,
            rows,
            rows,
            flat,
            flat,
            rows,
        ),
        out_specs=(rows, rows, rows, flat, rows, flat, flat, rows, rows, rows, flat, flat),
        check_vma=False,
    )
```

time: 2870 us -> 808 us (0.28)
  waiting for transfers between devices: 2470 us -> 227 us
  local copies, waits for them, and re-layouts: 33.3 us -> 207 us
  blocking collectives: 84.7 us -> 0 us
  starting transfers between devices: 0.39 us -> 77.6 us
  other arithmetic: 22.8 us -> 81.1 us
  matrix products: 222 us -> 189 us
    reduce_scatter x5, waiting for transfers between devices: 1910 us -> 1.11 us  [line_scatter(): return lax.psum_scatter(values, 'z', scatter_dimension=0, tiled=True)]
    all_gather x5, waiting for transfers between devices: 556 us -> 0.05 us  [line_gather(): return lax.all_gather(values, 'z', axis=0, tiled=True)]
    ppermute x0 -> x94, waiting for transfers between devices: none -> 226 us  [the longest x16 75.6 us: over_y(): return lax.ppermute(values, 'y', SWAP)]
    unnamed x2 -> x0, blocking collectives: 84.7 us -> none
    ppermute x0 -> x94, starting transfers between devices: none -> 76.8 us  [the longest x28 26.5 us: exchange(): came = lax.ppermute(piece, PLANE, [(i, i ^ mask) for i in range(PARTS)])]
    unnamed x117 -> x227, local copies, waits for them, and re-layouts: 18.7 us -> 80 us
    dot_general x5, matrix products: 89.4 us -> 46.7 us  [mat_rows(): lax.dot_general(left, right, (((0,), (0,)), ((), ())), preferred_element_...]
    dot_general x5 -> x9, matrix products: 59.7 us -> 59.2 us  [mat_cols(): lax.dot_general(left, right, (((1,), (1,)), ((), ())), preferred_element_...]
  transfers between devices with their start and end apart: 10 -> 104, of which waited for: 9 -> 30; matrix products, arithmetic and copies ran while one was open for 7% -> 53% of each run, Pallas kernels for 0% -> 0%
where the time goes in v1:
time: 808 us; the launch traced here: 799 us
  waiting for transfers between devices  227 us (28%)
  local copies, waits for them, and re-layouts  207 us (26%)
  matrix products  189 us (23%)
  other arithmetic  81.1 us (10%)
  starting transfers between devices  77.6 us (10%)
  between operations  17.2 us (2%)
    unnamed x227, local copies, waits for them, and re-layouts  80 us
    ppermute x16, waiting for transfers between devices, over_y(): return lax.ppermute(values, 'y', SWAP)  75.6 us
    ppermute x16, waiting for transfers between devices, over_x(): return lax.ppermute(values, 'x', SWAP)  65.7 us
    ppermute x28, waiting for transfers between devices, exchange(): came = lax.ppermute(piece, PLANE, [(i, i ^ mask) for i in range(PARTS)])  59.2 us
    dot_general x9, matrix products, mat_cols(): lax.dot_general(left, right, (((1,), (1,)), ((), ())), preferred_element_...  59.2 us
    dot_general x6, matrix products, mat(): return jnp.dot(left, right, preferred_element_type=f32)  58.3 us
    dot_general x5, matrix products, mat_rows(): lax.dot_general(left, right, (((0,), (0,)), ((), ())), preferred_element_...  46.7 us
    ppermute x28, starting transfers between devices, exchange(): came = lax.ppermute(piece, PLANE, [(i, i ^ mask) for i in range(PARTS)])  26.5 us
  transfers between devices with their start and end apart: 104, of which 30 were waited for; matrix products, arithmetic and copies ran while one was open for 53% of the time, Pallas kernels for 0%

profile of v1, /device:TPU:0, one launch (start us, length us, event | category | flops | bytes accessed | tf_op | source)
XLA Modules:
  0.0 798.6 jit_solution(6486742810277910676)
XLA Ops:
  44.7 11.3 %collective-permute-done.10 = bf16[2,512]{1,0:T(2,128)(2,1)S(1)} collective-permute-done((bf16[2,512]{1,0:T(2,128)(2,1)S(1)}, bf16[2,512]{1,0:T(2,128)(2,1)S(1)}, u32[]{:S(2)}, u32[]{:S(2)}) %collective-permute-start.10) | collective-permute-done | bytes 2080 | tf_op jit(solution)/shard_map/ppermute | solution.py:82
  95.7 13.7 %collective-permute-done.39 = bf16[1,3,64,704]{3,2,0,1:T(8,128)(2,1)S(1)} collective-permute-done((bf16[1,3,64,704]{3,2,0,1:T(8,128)(2,1)}, bf16[1,3,64,704]{3,2,0,1:T(8,128)(2,1)S(1)}, u32[]{:S(2)}, u32[]{:S(2)}) %collective-permute-start.39) | collective-permute-done | bytes 270368 | tf_op jit(solution)/shard_map/ppermute | solution.py:76
  147.6 11.1 %broadcast_add_fusion = f32[2048,768]{1,0:T(8,128)S(1)} fusion(f32[768]{0:T(1024)S(1)} %copy-done.67, bf16[2048,768]{1,0:T(8,128)(2,1)} %all-gather.6.cloned.1.call-done, f32[2048]{0:T(1024)S(1)} %reshape.471, f32[2048]{0:T(1024)S(1)} %reshape.470, bf16[2048,2048]{1,0:T(8,128)(2,1)} %constant_dynamic-update-slice_fusion, f32[2048]{0:T(1024)S(1)} %add_rsqrt_fusion, ...), kind=kOutput, calls=%fused_computation.33 | convolution fusion | flops 6469189632 | bytes 17861632 | tf_op jit(solution)/shard_map/dot_general | solution.py:34
  165.0 9.2 %fusion.81 = (f32[8,256,4,8]{3,2,1,0:T(4,128)}, f32[8,256,4,8]{3,2,1,0:T(4,128)}) fusion(f32[8,256,4,64]{3,2,1,0:T(4,128)} %reshape.484), kind=kLoop, calls=%fused_computation.341 | loop fusion | bytes 1048576 | tf_op jit(solution)/shard_map/slice | solution.py:141
  180.9 9.2 %fusion.82 = (f32[8,256,4,8]{3,2,1,0:T(4,128)}, f32[8,256,4,8]{3,2,1,0:T(4,128)}) fusion(f32[8,256,4,64]{3,2,1,0:T(4,128)} %reshape.485), kind=kLoop, calls=%fused_computation.342 | loop fusion | bytes 1048576 | tf_op jit(solution)/shard_map/slice | solution.py:141
  221.2 7.8 fusion.85
  241.1 6.1 collective-permute-done.21
  257.5 8.3 %collective-permute-done.22 = bf16[128,2048]{1,0:T(8,128)(2,1)S(1)} collective-permute-done((bf16[128,2048]{1,0:T(8,128)(2,1)S(1)}, bf16[128,2048]{1,0:T(8,128)(2,1)S(1)}, u32[]{:S(2)}, u32[]{:S(2)}) %collective-permute-start.22) | collective-permute-done | bytes 524320 | tf_op jit(solution)/shard_map/ppermute | solution.py:42
  269.9 18.4 %collective-permute-done.48 = bf16[256,2048]{1,0:T(8,128)(2,1)S(1)} collective-permute-done((bf16[256,2048]{1,0:T(8,128)(2,1)}, bf16[256,2048]{1,0:T(8,128)(2,1)S(1)}, u32[]{:S(2)}, u32[]{:S(2)}) %collective-permute-start.48) | collective-permute-done | bytes 1048608 | tf_op jit(solution)/shard_map/ppermute | solution.py:42
  292.7 29.4 %collective-permute-done.49 = bf16[128,2048]{1,0:T(8,128)(2,1)} collective-permute-done((bf16[128,2048]{1,0:T(8,128)(2,1)}, bf16[128,2048]{1,0:T(8,128)(2,1)}, u32[]{:S(2)}, u32[]{:S(2)}) %collective-permute-start.49) | collective-permute-done | bytes 524320 | tf_op jit(solution)/shard_map/ppermute | solution.py:38
  339.2 17.4 %collective-permute-done.27 = bf16[256,2048]{1,0:T(8,128)(2,1)S(1)} collective-permute-done((bf16[256,2048]{1,0:T(8,128)(2,1)}, bf16[256,2048]{1,0:T(8,128)(2,1)S(1)}, u32[]{:S(2)}, u32[]{:S(2)}) %collective-permute-start.27) | collective-permute-done | bytes 1048608 | tf_op jit(solution)/shard_map/ppermute | solution.py:42
  361.2 11.4 %fusion.87 = f32[2048,704]{0,1:T(8,128)} fusion(bf16[2048,2048]{1,0:T(8,128)(2,1)} %constant_dynamic-update-slice_fusion.20, bf16[2048,704]{1,0:T(8,128)(2,1)} %all-gather.14.cloned.1.call-done), kind=kOutput, calls=%fused_computation.347 | convolution fusion | flops 5905580032 | bytes 17039360 | tf_op jit(solution)/shard_map/dot_general | solution.py:34
  384.4 11.2 %fusion.86 = f32[2048,704]{0,1:T(8,128)} fusion(bf16[2048,2048]{1,0:T(8,128)(2,1)} %constant_dynamic-update-slice_fusion.10, bf16[2048,704]{1,0:T(8,128)(2,1)} %all-gather.12.cloned.1.call-done), kind=kOutput, calls=%fused_computation.346 | convolution fusion | flops 5905580032 | bytes 17039360 | tf_op jit(solution)/shard_map/dot_general | solution.py:34
  395.6 16.4 %multiply_convert_fusion.2 = (bf16[2048,704]{0,1:T(8,128)(2,1)}, bf16[2048,704]{0,1:T(8,128)(2,1)S(1)}, bf16[2048,704]{0,1:T(8,128)(2,1)}) fusion(f32[2048,704]{0,1:T(8,128)} %fusion.87, f32[2048,704]{0,1:T(8,128)} %fusion.86, bf16[2048,2048]{1,0:T(8,128)(2,1)} %constant_dynamic-update-slice_fusion.10, bf16[2048,704]{1,0:T(8,128)(2,1)} %all-gather.10.cloned.1.call-done), kind=kOutput, calls=%fused_computation.19 | convolution fusion | flops 5928648704 | bytes 31457280 | tf_op jit(solution)/shard_map/dot_general | solution.py:34
  412.0 5.6 convolution_convert_fusion
  421.2 6.7 add_convert_fusion.1
  428.4 9.3 %convolution_convert_fusion.6 = bf16[2048,704]{0,1:T(8,128)(2,1)} fusion(bf16[2048,704]{0,1:T(8,128)(2,1)} %get-tuple-element.31, bf16[2048,2048]{1,0:T(8,128)(2,1)S(1)} %bitcast.265), kind=kOutput, calls=%fused_computation.32 | convolution fusion | flops 5907021824 | bytes 14155776 | tf_op jit(solution)/shard_map/dot_general | solution.py:24
  437.8 9.3 %fusion.32 = f32[1024,2048]{1,0:T(8,128)} fusion(bf16[2048,704]{1,0:T(8,128)(2,1)} %all-gather.12.cloned.1.call-done, bf16[2048,704]{0,1:T(8,128)(2,1)} %get-tuple-element.33), kind=kOutput, calls=%fused_computation.88 | convolution fusion | flops 2952790016 | bytes 12976128 | tf_op jit(solution)/shard_map/dot_general | solution.py:30
  447.1 5.6 convert_add_fusion.2
  455.9 9.6 %convert_add_fusion.1 = f32[1024,2048]{1,0:T(8,128)S(1)} fusion(bf16[1024,2048]{1,0:T(8,128)(2,1)} %collective-permute-done.56, f32[1024,2048]{1,0:T(8,128)} %fusion.32, bf16[2048,704]{1,0:T(8,128)(2,1)} %all-gather.10.cloned.1.call-done, bf16[2048,704]{0,1:T(8,128)(2,1)} %get-tuple-element.31), kind=kOutput, calls=%fused_computation.10 | convolution fusion | flops 2959081472 | bytes 25559040 | tf_op jit(solution)/shard_map/dot_general | solution.py:30
  475.6 6.5 collective-permute-done.57
  489.3 7.5 convolution_convert_fusion.5
  496.9 8.9 %collective-permute-done.44 = bf16[256,2048]{1,0:T(8,128)(2,1)} collective-permute-done((bf16[256,2048]{1,0:T(8,128)(2,1)}, bf16[256,2048]{1,0:T(8,128)(2,1)}, u32[]{:S(2)}, u32[]{:S(2)}) %collective-permute-start.44) | collective-permute-done | bytes 1048608 | tf_op jit(solution)/shard_map/ppermute | solution.py:38
  505.7 20.7 %collective-permute-done.58 = bf16[256,2048]{1,0:T(8,128)(2,1)} collective-permute-done((bf16[256,2048]{1,0:T(8,128)(2,1)}, bf16[256,2048]{1,0:T(8,128)(2,1)}, u32[]{:S(2)}, u32[]{:S(2)}) %collective-permute-start.58) | collective-permute-done | bytes 1048608 | tf_op jit(solution)/shard_map/ppermute | solution.py:38
  537.1 21.6 %collective-permute-done.62 = bf16[256,2048]{1,0:T(8,128)(2,1)S(1)} collective-permute-done((bf16[256,2048]{1,0:T(8,128)(2,1)}, bf16[256,2048]{1,0:T(8,128)(2,1)S(1)}, u32[]{:S(2)}, u32[]{:S(2)}) %collective-permute-start.62) | collective-permute-done | bytes 1048608 | tf_op jit(solution)/shard_map/ppermute | solution.py:42
  562.3 10.9 %convolution_convert_fusion.4 = bf16[2048,704]{0,1:T(8,128)(2,1)} fusion(bf16[2048,704]{0,1:T(8,128)(2,1)S(1)} %copy-done.81, bf16[2048,2048]{1,0:T(8,128)(2,1)} %constant_dynamic-update-slice_fusion.20), kind=kOutput, calls=%fused_computation.30 | convolution fusion | flops 5907021824 | bytes 14155776 | tf_op jit(solution)/shard_map/dot_general | solution.py:24
  585.3 6.7 convolution_convert_fusion.8
  636.2 11.0 %fusion.1 = f32[2048,2048]{1,0:T(8,128)} fusion(bf16[2048,2048]{1,0:T(8,128)(2,1)} %constant_dynamic-update-slice_fusion, f32[2048]{0:T(1024)S(1)} %copy-done.54, f32[2048]{0:T(1024)S(1)} %copy-done.50), kind=kLoop, calls=%fused_computation.3 | loop fusion | flops 12582912 | bytes 25182208 | tf_op jit(solution)/shard_map/mul | solution.py:100
  651.3 6.7 convolution_convert_fusion.7
  658.1 7.1 convert_add_fusion
  671.7 12.3 %convolution_convert_fusion.3 = bf16[2048,768]{1,0:T(8,128)(2,1)} fusion(bf16[2048,768]{0,1:T(8,128)(2,1)S(1)} %copy-done.13, f32[2048]{0:T(1024)S(1)} %copy-done.64, f32[2048]{0:T(1024)S(1)} %copy-done.48, bf16[2048,2048]{1,0:T(8,128)(2,1)} %constant_dynamic-update-slice_fusion, f32[2048]{0:T(1024)S(1)} %copy-done.54, f32[2048]{0:T(1024)S(1)} %copy-done.50), kind=kOutput, calls=%fused_computation.29 | convolution fusion | flops 6469189632 | bytes 14712832 | tf_op jit(solution)/shard_map/dot_general | solution.py:24
  699.2 25.9 %collective-permute-done.93 = bf16[1,3,64,704]{3,2,0,1:T(8,128)(2,1)S(1)} collective-permute-done((bf16[1,3,64,704]{3,2,0,1:T(8,128)(2,1)S(1)}, bf16[1,3,64,704]{3,2,0,1:T(8,128)(2,1)S(1)}, u32[]{:S(2)}, u32[]{:S(2)}) %collective-permute-start.93) | collective-permute-done | bytes 270368 | tf_op jit(solution)/shard_map/ppermute | solution.py:76
  (648 shorter events, 408.6 us)
Async XLA Ops:
  7.2 139.8 %all-gather.6.cloned.1.call-start = ((), (), s32[]{:S(2)}) async-start(), calls=%async_computation.5 | async-start | bytes 3932160 | tf_op jit(solution)/shard_map/all_gather | solution.py:186
  30.2 204.8 %all-gather.8.cloned.1.call-start = ((), (), s32[]{:S(2)}) async-start(), calls=%async_computation.6 | async-start | bytes 1310720 | tf_op jit(solution)/shard_map/all_gather | solution.py:186
  30.2 82.6 %collective-permute-start = (bf16[256,2048]{1,0:T(8,128)(2,1)}, bf16[256,2048]{1,0:T(8,128)(2,1)}, u32[]{:S(2)}, u32[]{:S(2)}) collective-permute-start(bf16[256,2048]{1,0:T(8,128)(2,1)} %param.14), channel_id=1, source_target_pairs={{0,2},{2,0},{1,3},{3,1},{4,6},{6,4},{5,7},{7,5},{8,10},{10,8},{9,1... | collective-permute-start | bytes 3145736 | tf_op jit(solution)/shard_map/ppermute | solution.py:38
  32.2 77.7 %collective-permute-start.1 = (bf16[256,2048]{1,0:T(8,128)(2,1)}, bf16[256,2048]{1,0:T(8,128)(2,1)S(1)}, u32[]{:S(2)}, u32[]{:S(2)}) collective-permute-start(bf16[256,2048]{1,0:T(8,128)(2,1)} %param.14), channel_id=1, source_target_pairs={{0,4},{4,0},{1,5},{5,1},{2,6},{6,2},{3,7},{7,3},{8,12},{12,8},{9,1... | collective-permute-start | bytes 3145736 | tf_op jit(solution)/shard_map/ppermute | solution.py:42
  40.5 35.0 %collective-permute-start.35 = (bf16[1,3,64,704]{3,2,0,1:T(8,128)(2,1)}, bf16[1,3,64,704]{3,2,0,1:T(8,128)(2,1)}, u32[]{:S(2)}, u32[]{:S(2)}) collective-permute-start(bf16[1,3,64,704]{3,2,0,1:T(8,128)(2,1)} %constant_dynamic-slice_fusion.20), channel_id=1, source_target_pairs={{0,1},{1,0},{2,3},{3,2},{4,5},{5,4},{6,7},{7,6},{8,9},{9,8},{10,11... | collective-permute-start | bytes 811016 | tf_op jit(solution)/shard_map/ppermute | solution.py:76
  41.1 320.1 %all-gather.14.cloned.1.call-start = ((), (), s32[]{:S(2)}) async-start(), calls=%async_computation.9 | async-start | bytes 3932160 | tf_op jit(solution)/shard_map/all_gather | solution.py:186
  116.6 267.8 %all-gather.12.cloned.1.call-start = ((), (), s32[]{:S(2)}) async-start(), calls=%async_computation.8 | async-start | bytes 3932160 | tf_op jit(solution)/shard_map/all_gather | solution.py:186
  240.1 155.5 %all-gather.10.cloned.1.call-start = ((), (), s32[]{:S(2)}) async-start(), calls=%async_computation.7 | async-start | bytes 3932160 | tf_op jit(solution)/shard_map/all_gather | solution.py:186
  254.8 35.0 %collective-permute-start.47 = (bf16[256,2048]{1,0:T(8,128)(2,1)}, bf16[256,2048]{1,0:T(8,128)(2,1)S(1)}, u32[]{:S(2)}, u32[]{:S(2)}) collective-permute-start(bf16[256,2048]{1,0:T(8,128)(2,1)} %get-tuple-element.26), channel_id=1, source_target_pairs={{0,2},{2,0},{1,3},{3,1},{4,6},{6,4},{5,7},{7,5},{8,10},{10,8},{9,1... | collective-permute-start | bytes 3145736 | tf_op jit(solution)/shard_map/ppermute | solution.py:38
  255.7 32.7 %collective-permute-start.48 = (bf16[256,2048]{1,0:T(8,128)(2,1)}, bf16[256,2048]{1,0:T(8,128)(2,1)S(1)}, u32[]{:S(2)}, u32[]{:S(2)}) collective-permute-start(bf16[256,2048]{1,0:T(8,128)(2,1)} %get-tuple-element.26), channel_id=1, source_target_pairs={{0,4},{4,0},{1,5},{5,1},{2,6},{6,2},{3,7},{7,3},{8,12},{12,8},{9,1... | collective-permute-start | bytes 3145736 | tf_op jit(solution)/shard_map/ppermute | solution.py:42
  267.2 58.2 %collective-permute-start.23 = (bf16[256,2048]{1,0:T(8,128)(2,1)S(1)}, bf16[256,2048]{1,0:T(8,128)(2,1)}, u32[]{:S(2)}, u32[]{:S(2)}) collective-permute-start(bf16[256,2048]{1,0:T(8,128)(2,1)S(1)} %pad_maximum_fusion.4), channel_id=1, source_target_pairs={{0,2},{2,0},{1,3},{3,1},{4,6},{6,4},{5,7},{7,5},{8,10},{10,8},{9,1... | collective-permute-start | bytes 3145736 | tf_op jit(solution)/shard_map/ppermute | solution.py:38
  268.5 56.9 %collective-permute-start.25 = (bf16[256,2048]{1,0:T(8,128)(2,1)}, bf16[256,2048]{1,0:T(8,128)(2,1)}, u32[]{:S(2)}, u32[]{:S(2)}) collective-permute-start(bf16[256,2048]{1,0:T(8,128)(2,1)} %pad_maximum_fusion.5), channel_id=1, source_target_pairs={{0,4},{4,0},{1,5},{5,1},{2,6},{6,2},{3,7},{7,3},{8,12},{12,8},{9,1... | collective-permute-start | bytes 3145736 | tf_op jit(solution)/shard_map/ppermute | solution.py:42
  289.2 33.0 %collective-permute-start.49 = (bf16[128,2048]{1,0:T(8,128)(2,1)}, bf16[128,2048]{1,0:T(8,128)(2,1)}, u32[]{:S(2)}, u32[]{:S(2)}) collective-permute-start(bf16[128,2048]{1,0:T(8,128)(2,1)} %slice.515), channel_id=1, source_target_pairs={{0,2},{2,0},{1,3},{3,1},{4,6},{6,4},{5,7},{7,5},{8,10},{10,8},{9,1... | collective-permute-start | bytes 1572872 | tf_op jit(solution)/shard_map/ppermute | solution.py:38
  289.6 41.4 %collective-permute-start.51 = (bf16[256,2048]{1,0:T(8,128)(2,1)}, bf16[256,2048]{1,0:T(8,128)(2,1)}, u32[]{:S(2)}, u32[]{:S(2)}) collective-permute-start(bf16[256,2048]{1,0:T(8,128)(2,1)} %get-tuple-element.26), channel_id=1, source_target_pairs={{0,1},{1,0},{2,3},{3,2},{4,5},{5,4},{6,7},{7,6},{8,9},{9,8},{10,11... | collective-permute-start | bytes 3145736 | tf_op jit(solution)/shard_map/ppermute | solution.py:46
  289.8 333.3 %reduce-scatter.10.cloned.1.call-start = ((), (), s32[]{:S(2)}) async-start(), calls=%async_computation.12 | async-start | bytes 3604480 | tf_op jit(solution)/shard_map/reduce_scatter | solution.py:189
  289.9 34.1 %collective-permute-start.50 = (bf16[128,2048]{1,0:T(8,128)(2,1)S(1)}, bf16[128,2048]{1,0:T(8,128)(2,1)S(1)}, u32[]{:S(2)}, u32[]{:S(2)}) collective-permute-start(bf16[128,2048]{1,0:T(8,128)(2,1)S(1)} %slice.516), channel_id=1, source_target_pairs={{0,4},{4,0},{1,5},{5,1},{2,6},{6,2},{3,7},{7,3},{8,12},{12,8},{9,1... | collective-permute-start | bytes 1572872 | tf_op jit(solution)/shard_map/ppermute | solution.py:42
  338.7 40.9 %collective-permute-start.30 = (bf16[256,2048]{1,0:T(8,128)(2,1)}, bf16[256,2048]{1,0:T(8,128)(2,1)S(1)}, u32[]{:S(2)}, u32[]{:S(2)}) collective-permute-start(bf16[256,2048]{1,0:T(8,128)(2,1)} %get-tuple-element.28), channel_id=1, source_target_pairs={{0,1},{1,0},{2,3},{3,2},{4,5},{5,4},{6,7},{7,6},{8,9},{9,8},{10,11... | collective-permute-start | bytes 3145736 | tf_op jit(solution)/shard_map/ppermute | solution.py:46
  437.7 186.8 %reduce-scatter.12.cloned.1.call-start = ((), (), s32[]{:S(2)}) async-start(), calls=%async_computation.13 | async-start | bytes 3604480 | tf_op jit(solution)/shard_map/reduce_scatter | solution.py:189
  473.4 32.4 %collective-permute-start.44 = (bf16[256,2048]{1,0:T(8,128)(2,1)}, bf16[256,2048]{1,0:T(8,128)(2,1)}, u32[]{:S(2)}, u32[]{:S(2)}) collective-permute-start(bf16[256,2048]{1,0:T(8,128)(2,1)} %pad_maximum_fusion.6), channel_id=1, source_target_pairs={{0,2},{2,0},{1,3},{3,1},{4,6},{6,4},{5,7},{7,5},{8,10},{10,8},{9,1... | collective-permute-start | bytes 3145736 | tf_op jit(solution)/shard_map/ppermute | solution.py:38
  474.9 30.8 %collective-permute-start.46 = (bf16[256,2048]{1,0:T(8,128)(2,1)}, bf16[256,2048]{1,0:T(8,128)(2,1)}, u32[]{:S(2)}, u32[]{:S(2)}) collective-permute-start(bf16[256,2048]{1,0:T(8,128)(2,1)} %pad_maximum_fusion.7), channel_id=1, source_target_pairs={{0,4},{4,0},{1,5},{5,1},{2,6},{6,2},{3,7},{7,3},{8,12},{12,8},{9,1... | collective-permute-start | bytes 3145736 | tf_op jit(solution)/shard_map/ppermute | solution.py:42
  485.9 40.6 %collective-permute-start.58 = (bf16[256,2048]{1,0:T(8,128)(2,1)}, bf16[256,2048]{1,0:T(8,128)(2,1)}, u32[]{:S(2)}, u32[]{:S(2)}) collective-permute-start(bf16[256,2048]{1,0:T(8,128)(2,1)} %pad_maximum_fusion.8), channel_id=1, source_target_pairs={{0,2},{2,0},{1,3},{3,1},{4,6},{6,4},{5,7},{7,5},{8,10},{10,8},{9,1... | collective-permute-start | bytes 3145736 | tf_op jit(solution)/shard_map/ppermute | solution.py:38
  488.4 38.0 %collective-permute-start.60 = (bf16[256,2048]{1,0:T(8,128)(2,1)}, bf16[256,2048]{1,0:T(8,128)(2,1)}, u32[]{:S(2)}, u32[]{:S(2)}) collective-permute-start(bf16[256,2048]{1,0:T(8,128)(2,1)} %pad_maximum_fusion.9), channel_id=1, source_target_pairs={{0,4},{4,0},{1,5},{5,1},{2,6},{6,2},{3,7},{7,3},{8,12},{12,8},{9,1... | collective-permute-start | bytes 3145736 | tf_op jit(solution)/shard_map/ppermute | solution.py:42
  496.8 131.0 %reduce-scatter.14.cloned.1.call-start = ((), (), s32[]{:S(2)}) async-start(), calls=%async_computation.14 | async-start | bytes 3604480 | tf_op jit(solution)/shard_map/reduce_scatter | solution.py:189
  537.0 43.4 %collective-permute-start.65 = (bf16[256,2048]{1,0:T(8,128)(2,1)}, bf16[256,2048]{1,0:T(8,128)(2,1)S(1)}, u32[]{:S(2)}, u32[]{:S(2)}) collective-permute-start(bf16[256,2048]{1,0:T(8,128)(2,1)} %get-tuple-element.22), channel_id=1, source_target_pairs={{0,1},{1,0},{2,3},{3,2},{4,5},{5,4},{6,7},{7,6},{8,9},{9,8},{10,11... | collective-permute-start | bytes 3145736 | tf_op jit(solution)/shard_map/ppermute | solution.py:46
  573.3 173.9 %reduce-scatter.8.cloned.1.call-start = ((), (), s32[]{:S(2)}) async-start(), calls=%async_computation.11 | async-start | bytes 1310720 | tf_op jit(solution)/shard_map/reduce_scatter | solution.py:189
  623.0 35.0 %collective-permute-start.70 = (bf16[1024,2048]{1,0:T(8,128)(2,1)}, bf16[1024,2048]{1,0:T(8,128)(2,1)}, u32[]{:S(2)}, u32[]{:S(2)}) collective-permute-start(bf16[1024,2048]{1,0:T(8,128)(2,1)} %convolution_convert_fusion.2), channel_id=1, source_target_pairs={{0,1},{1,0},{2,3},{3,2},{4,5},{5,4},{6,7},{7,6},{8,9},{9,8},{10,11... | collective-permute-start | bytes 12582920 | tf_op jit(solution)/shard_map/ppermute | solution.py:46
  648.3 45.5 %collective-permute-start.89 = (bf16[1,3,64,704]{3,2,0,1:T(8,128)(2,1)}, bf16[1,3,64,704]{3,2,0,1:T(8,128)(2,1)}, u32[]{:S(2)}, u32[]{:S(2)}) collective-permute-start(bf16[1,3,64,704]{3,2,0,1:T(8,128)(2,1)} %get-tuple-element.63), channel_id=1, source_target_pairs={{0,3},{1,2},{2,1},{3,0},{4,7},{5,6},{6,5},{7,4},{8,11},{9,10},{10,... | collective-permute-start | bytes 811016 | tf_op jit(solution)/shard_map/ppermute | solution.py:76
  648.3 47.9 %collective-permute-start.90 = (bf16[1,3,64,704]{3,2,0,1:T(8,128)(2,1)}, bf16[1,3,64,704]{3,2,0,1:T(8,128)(2,1)}, u32[]{:S(2)}, u32[]{:S(2)}) collective-permute-start(bf16[1,3,64,704]{3,2,0,1:T(8,128)(2,1)} %get-tuple-element.62), channel_id=1, source_target_pairs={{0,4},{1,5},{2,6},{3,7},{4,0},{5,1},{6,2},{7,3},{8,12},{9,13},{10,... | collective-permute-start | bytes 811016 | tf_op jit(solution)/shard_map/ppermute | solution.py:76
  649.8 47.5 %collective-permute-start.91 = (bf16[1,3,64,704]{3,2,0,1:T(8,128)(2,1)}, bf16[1,3,64,704]{3,2,0,1:T(8,128)(2,1)}, u32[]{:S(2)}, u32[]{:S(2)}) collective-permute-start(bf16[1,3,64,704]{3,2,0,1:T(8,128)(2,1)} %get-tuple-element.61), channel_id=1, source_target_pairs={{0,5},{1,4},{2,7},{3,6},{4,1},{5,0},{6,3},{7,2},{8,13},{9,12},{10,... | collective-permute-start | bytes 811016 | tf_op jit(solution)/shard_map/ppermute | solution.py:76
  658.0 103.3 %reduce-scatter.6.cloned.1.call-start = ((), (), s32[]{:S(2)}) async-start(), calls=%async_computation.10 | async-start | bytes 3932160 | tf_op jit(solution)/shard_map/reduce_scatter | solution.py:189
  691.7 34.2 %collective-permute-start.72 = (bf16[256,2048]{1,0:T(8,128)(2,1)S(1)}, bf16[256,2048]{1,0:T(8,128)(2,1)}, u32[]{:S(2)}, u32[]{:S(2)}) collective-permute-start(bf16[256,2048]{1,0:T(8,128)(2,1)S(1)} %pad_maximum_fusion.12), channel_id=1, source_target_pairs={{0,2},{2,0},{1,3},{3,1},{4,6},{6,4},{5,7},{7,5},{8,10},{10,8},{9,1... | collective-permute-start | bytes 3145736 | tf_op jit(solution)/shard_map/ppermute | solution.py:38
  693.8 32.1 %collective-permute-start.74 = (bf16[256,2048]{1,0:T(8,128)(2,1)}, bf16[256,2048]{1,0:T(8,128)(2,1)}, u32[]{:S(2)}, u32[]{:S(2)}) collective-permute-start(bf16[256,2048]{1,0:T(8,128)(2,1)} %pad_maximum_fusion.13), channel_id=1, source_target_pairs={{0,4},{4,0},{1,5},{5,1},{2,6},{6,2},{3,7},{7,3},{8,12},{12,8},{9,1... | collective-permute-start | bytes 3145736 | tf_op jit(solution)/shard_map/ppermute | solution.py:42
  (163 other events, 2154.2 us)
Sparse Core Ops, SparseCore 0:
  30.3 65.7 all-gather.5
  97.6 26.5 all-gather.7
  126.4 62.9 all-gather.13
  240.2 61.4 all-gather.11
  303.7 62.1 all-gather.9
  437.9 54.4 reduce-scatter.9
  496.9 54.1 reduce-scatter.11
  573.4 54.4 reduce-scatter.13
  658.1 26.9 reduce-scatter.7
  687.4 59.6 reduce-scatter.5

commit v2 on v1

v2 whole, which is shorter than its diff:
```python
import functools

import jax
import jax.numpy as jnp
from jax import lax
from jax.experimental import pallas as pl
from jax.experimental.pallas import tpu as pltpu
from jax.sharding import Mesh, PartitionSpec as P

HEAD = 64
ROT = 16
BLOCK = 128
PARTS = 8
LINE = 4
GROUPS = 4

AXES = ("z", "y", "x", "c", "s")
PLANE = ("y", "x", "c")
SWAP = ((0, 1), (1, 0))
NEAR = ((0, 1), (1, 0), (2, 3), (3, 2))
FAR = ((0, 2), (1, 3), (2, 0), (3, 1))
INNER = ((1, 2), (2, 1))
OUTWARD = ((2, 3), (1, 0))
INWARD = ((3, 2), (0, 1))

eps_norm = 1e-05
f32 = jnp.float32
bf16 = jnp.bfloat16
VMEM_BYTES = 56 * 1024 * 1024
ANYWHERE = pl.BlockSpec(memory_space=pl.ANY)


def mat_rows(left, right):
    return lax.dot_general(left, right, (((0,), (0,)), ((), ())), preferred_element_type=f32)


def mat_cols(left, right):
    return lax.dot_general(left, right, (((1,), (1,)), ((), ())), preferred_element_type=f32)


def mat(left, right):
    return jnp.dot(left, right, preferred_element_type=f32)


def over_x(values):
    return lax.ppermute(values, "x", SWAP)


def over_y(values):
    return lax.ppermute(values, "y", SWAP)


def over_c(values):
    return lax.ppermute(values, "c", SWAP)


def along_z(values, perm):
    return lax.ppermute(values, "z", perm)


def after(values, *earlier):
    return lax.optimization_barrier((values, *earlier))[0]


def gather_plane(own):
    half = own.shape[0] // 2
    from_x = over_x(own)
    from_y = over_y(own)
    line = [own, from_x, from_y, over_x(from_y[:half]), over_y(from_x[half:])]
    return line, [over_c(part) for part in line]


def scatter_plane(kept, sent, rows):
    half = rows // 2
    came = over_c(sent)

    def joined(low, high):
        return kept[low:high].astype(f32) + came[low:high].astype(f32)

    low = over_x(joined(3 * rows, 3 * rows + half).astype(bf16))
    high = over_y(joined(3 * rows + half, 4 * rows).astype(bf16))
    near_x = jnp.concatenate(
        [joined(rows, rows + half), joined(rows + half, 2 * rows) + high.astype(f32)], axis=0
    )
    near_y = jnp.concatenate(
        [joined(2 * rows, 2 * rows + half) + low.astype(f32), joined(2 * rows + half, 3 * rows)],
        axis=0,
    )
    return (
        joined(0, rows)
        + over_x(near_x.astype(bf16)).astype(f32)
        + over_y(near_y.astype(bf16)).astype(f32)
    )


def exchange(blocks, me):
    result = blocks
    for mask in range(1, PARTS):
        there = me ^ mask
        piece = lax.dynamic_index_in_dim(blocks, there, 0, keepdims=True)
        came = lax.ppermute(piece, PLANE, [(i, i ^ mask) for i in range(PARTS)])
        result = lax.dynamic_update_slice_in_dim(result, came, there, 0)
    return result


def gather_line(own):
    far = along_z(own, FAR)
    return (own, along_z(own, NEAR), far, along_z(own, INNER), along_z(far, OUTWARD))


def scatter_line(full, iz):
    blocks = full.reshape(LINE, -1, full.shape[1])

    def block(mask):
        return lax.dynamic_index_in_dim(blocks, iz ^ mask, 0, keepdims=False)

    last = block(3)
    inward = along_z(last, INWARD)
    inner = along_z(last, INNER)
    near = along_z(block(1), NEAR)
    far = along_z((block(2).astype(f32) + inward.astype(f32)).astype(bf16), FAR)
    return block(0).astype(f32) + inner.astype(f32) + near.astype(f32) + far.astype(f32)


def doubled(values, axis, perm, upper):
    other = lax.ppermute(values, axis, perm)
    return jnp.where(
        upper,
        jnp.concatenate([other, values], axis=0),
        jnp.concatenate([values, other], axis=0),
    )


def halved(values, axis, perm, upper):
    half = values.shape[0] // 2
    low, high = values[:half], values[half:]
    came = lax.ppermute(jnp.where(upper, low, high), axis, perm)
    return jnp.where(upper, high, low) + came


def standardize(values):
    centre = values - jnp.mean(values, axis=1, keepdims=True)
    inverse = lax.rsqrt(jnp.mean(centre * centre, axis=1, keepdims=True) + eps_norm)
    return (centre * inverse, inverse)


def norm_back(grad_out, standard, inverse, gain):
    scaled = grad_out * gain
    inner = jnp.mean(scaled, axis=1, keepdims=True)
    along = jnp.mean(scaled * standard, axis=1, keepdims=True)
    return (
        inverse * (scaled - inner - standard * along),
        jnp.sum(grad_out * standard, axis=0),
        jnp.sum(grad_out, axis=0),
    )


def block_marks(lengths, used_blocks):
    index = jnp.arange(lengths.shape[0], dtype=jnp.int32)
    began = jnp.max(
        jnp.where((lengths[None, :] > 0) & (index[None, :] <= index[:, None]), index[None, :], 0),
        axis=1,
    )
    limit = jnp.sum(jnp.where(index[None, :] == began[:, None], lengths[None, :], 0), axis=1)
    return jnp.stack([began, limit, (index < used_blocks).astype(jnp.int32)], axis=1).reshape(-1)


def valid_rows(marks, row_count):
    marks = marks.reshape(-1, 3)
    row = jnp.arange(row_count, dtype=jnp.int32)
    began, limit, used = (jnp.repeat(marks[:, index], BLOCK) for index in range(3))
    return (row - began * BLOCK < limit) & (used > 0)


def rotary_tables(row_count, heads):
    half_rot = ROT // 2
    freqs = 10000.0 ** (-2.0 * jnp.arange(half_rot, dtype=f32) / ROT)
    angle = jnp.arange(row_count, dtype=f32)[:, None] * freqs[None, :]
    cosine, sine = jnp.cos(angle), jnp.sin(angle)
    zero = jnp.zeros((row_count, HEAD - ROT), f32)
    none = jnp.zeros_like(sine)
    return tuple(
        jnp.tile(jnp.concatenate(parts, axis=1), (1, heads))
        for parts in (
            [cosine, cosine, zero + 1.0],
            [-sine, none, zero],
            [none, sine, zero],
        )
    )


def line_copies(pieces, target, sems):
    copies, offset = [], 0
    for index, piece in enumerate(pieces):
        size = piece.shape[0]
        copies.append(
            pltpu.make_async_copy(piece, target.at[pl.ds(offset, size)], sems.at[index])
        )
        offset += size
    return copies


def block_target(target, z, mask, size):
    return target.at[pl.ds(pl.multiple_of(jnp.bitwise_xor(z, mask) * size, size), size)]


def start_blocks(pieces, target, sems, z):
    size = pieces[0].shape[0]
    for mask in range(3):
        pltpu.make_async_copy(
            pieces[mask], block_target(target, z, mask, size), sems.at[mask]
        ).start()
    inner = jnp.logical_or(z == 1, z == 2)

    @pl.when(inner)
    def _():
        pltpu.make_async_copy(pieces[3], block_target(target, z, 3, size), sems.at[3]).start()

    @pl.when(jnp.logical_not(inner))
    def _():
        pltpu.make_async_copy(pieces[4], block_target(target, z, 3, size), sems.at[3]).start()


def wait_blocks(pieces, target, sems, z):
    size = pieces[0].shape[0]
    for mask in range(4):
        pltpu.make_async_copy(
            pieces[mask], block_target(target, z, mask, size), sems.at[mask]
        ).wait()


def begin_lines(step, lines):
    @pl.when(step == 0)
    def _():
        for copies in lines:
            for copy in copies:
                copy.start()


def await_lines(step, lines):
    for index in range(GROUPS):

        @pl.when(step == index)
        def _(index=index):
            for copies in lines:
                for copy in copies[index:] if index == GROUPS - 1 else copies[index : index + 1]:
                    copy.wait()


def row_marks(marks, group, shape, axis):
    place = lax.broadcasted_iota(jnp.int32, shape, axis)
    key = jnp.zeros(shape, jnp.int32)
    for index in range(shape[axis] // BLOCK):
        began = marks[group, 3 * index]
        limit = marks[group, 3 * index + 1]
        used = marks[group, 3 * index + 2]
        inside = jnp.logical_and(place >= index * BLOCK, place < (index + 1) * BLOCK)
        last = jnp.where(used > 0, began * BLOCK + limit, 0)
        seen = jnp.where(place < last, began, -1 - axis)
        key = jnp.where(inside, seen, key)
    return place, key


def allowed_pairs(marks, group, rows):
    row, row_key = row_marks(marks, group, (rows, 1), 0)
    column, column_key = row_marks(marks, group, (1, rows), 1)
    row = jnp.broadcast_to(row, (rows, rows))
    column = jnp.broadcast_to(column, (rows, rows))
    same = jnp.broadcast_to(row_key, (rows, rows)) == jnp.broadcast_to(column_key, (rows, rows))
    return jnp.logical_or(jnp.logical_and(same, column <= row), row == column)


def placed_table(table, marks, group, rows):
    parts = []
    for index in range(rows // BLOCK):
        start = pl.multiple_of((index - marks[group, 3 * index]) * BLOCK, BLOCK)
        parts.append(table[pl.ds(start, BLOCK), :])
    return jnp.concatenate(parts, axis=0)


def rotate(values, cosine, ahead, behind):
    width = values.shape[1]
    half_rot = ROT // 2
    return (
        values * cosine
        + pltpu.roll(values, width - half_rot, 1) * ahead
        + pltpu.roll(values, half_rot, 1) * behind
    )


def head_masks(shape, heads):
    lane = lax.broadcasted_iota(jnp.int32, shape, 1)
    return [
        jnp.logical_and(lane >= index * HEAD, lane < (index + 1) * HEAD) for index in range(heads)
    ]


def softmax_of(query, key_rows, allowed):
    scores = mat_cols(query, key_rows) * HEAD ** (-0.5)
    scores = jnp.where(allowed, scores, -1e30)
    expo = jnp.exp(scores - jnp.max(scores, axis=1, keepdims=True))
    return expo / jnp.sum(expo, axis=1, keepdims=True)


def attend_forward(first, heads, rows, half, z_ref, marks_ref, *refs):
    tokens, qkv_pieces, out_pieces = refs[0:5], refs[5:10], refs[10:15]
    gain, shift, bias, cos_ref, ahead_ref, behind_ref = refs[15:21]
    refs = refs[21 if first else 24 :]
    normed_ref, qkv_ref, mixed_ref, part_ref = refs[:4]
    token_rows, qkv_weight, out_weight, line_sems, qkv_sems, out_sems = refs[4:]
    step = pl.program_id(0)
    group = half * GROUPS + step
    z = z_ref[0]
    line = line_copies(tokens, token_rows, line_sems)
    begin_lines(step, [line])

    @pl.when(step == 0)
    def _():
        start_blocks(qkv_pieces, qkv_weight, qkv_sems, z)
        start_blocks(out_pieces, out_weight, out_sems, z)

    await_lines(step, [line])
    values = token_rows[pl.ds(pl.multiple_of(step * rows, rows), rows), :].astype(f32)
    centre = values - jnp.mean(values, axis=1, keepdims=True)
    inverse = lax.rsqrt(jnp.mean(centre * centre, axis=1, keepdims=True) + eps_norm)
    normed = (centre * inverse * gain[...] + shift[...]).astype(bf16)
    normed_ref[...] = normed

    @pl.when(step == 0)
    def _():
        wait_blocks(qkv_pieces, qkv_weight, qkv_sems, z)
        wait_blocks(out_pieces, out_weight, out_sems, z)

    width = heads * HEAD
    qkv = mat(normed, qkv_weight[...]) + bias[...]
    tables = [placed_table(ref, marks_ref, group, rows) for ref in (cos_ref, ahead_ref, behind_ref)]
    query = rotate(qkv[:, :width], *tables).astype(bf16)
    key_rows = rotate(qkv[:, width : 2 * width], *tables).astype(bf16)
    value = qkv[:, 2 * width :].astype(bf16)
    qkv_ref[:, :width] = query
    qkv_ref[:, width : 2 * width] = key_rows
    qkv_ref[:, 2 * width :] = value
    allowed = allowed_pairs(marks_ref, group, rows)
    mixed = jnp.zeros((rows, width), f32)
    for mask in head_masks((rows, width), heads):
        probs = softmax_of(jnp.where(mask, query, 0), key_rows, allowed).astype(bf16)
        mixed = jnp.where(mask, mat(probs, value), mixed)
    mixed = mixed.astype(bf16)
    mixed_ref[...] = mixed
    part_ref[...] = mat(mixed, out_weight[...]).astype(bf16)


def feed_both(first, rows, z_ref, *refs):
    normed, grads = refs[0:5], refs[5:10]
    gate_pieces, up_pieces, down_pieces = refs[10:15], refs[15:20], refs[20:25]
    refs = refs[25 if first else 30 :]
    normed_ref, grad_ref, hidden_ref, gate_ref, up_ref, back_ref, down_ref = refs[:7]
    normed_rows, grad_rows, gate_weight, up_weight, down_weight = refs[7:12]
    normed_sems, grad_sems, gate_sems, up_sems, down_sems = refs[12:]
    step = pl.program_id(0)
    z = z_ref[0]
    lines = [
        line_copies(normed, normed_rows, normed_sems),
        line_copies(grads, grad_rows, grad_sems),
    ]

    @pl.when(step == 0)
    def _():
        start_blocks(gate_pieces, gate_weight, gate_sems, z)

    begin_lines(step, lines)

    @pl.when(step == 0)
    def _():
        start_blocks(up_pieces, up_weight, up_sems, z)
        start_blocks(down_pieces, down_weight, down_sems, z)
        wait_blocks(gate_pieces, gate_weight, gate_sems, z)

    await_lines(step, lines)
    here = pl.ds(pl.multiple_of(step * rows, rows), rows)
    values = normed_rows[here, :]
    normed_ref[...] = values
    gate = mat(values, gate_weight[...])

    @pl.when(step == 0)
    def _():
        wait_blocks(up_pieces, up_weight, up_sems, z)
        wait_blocks(down_pieces, down_weight, down_sems, z)

    upward = mat(values, up_weight[...])
    sigma = jax.nn.sigmoid(gate)
    gated = gate * sigma
    hidden = (gated * upward).astype(bf16)
    hidden_ref[...] = hidden
    grad_low = grad_rows[here, :]
    grad_ref[...] = grad_low
    grad_hidden = mat(grad_low, down_weight[...])
    grad_gate = (grad_hidden * upward * sigma * (1.0 + gate * (1.0 - sigma))).astype(bf16)
    grad_up = (grad_hidden * gated).astype(bf16)
    gate_ref[...] = grad_gate
    up_ref[...] = grad_up
    back_ref[...] = (
        mat_cols(grad_gate, gate_weight[...]) + mat_cols(grad_up, up_weight[...])
    ).astype(bf16)
    down_ref[...] = mat_cols(hidden, down_weight[...]).astype(bf16)


def attend_backward(first, heads, rows, half, z_ref, marks_ref, *refs):
    branch, qkv_pieces, out_pieces = refs[0:5], refs[5:10], refs[10:15]
    saved, cos_ref, ahead_ref, behind_ref = refs[15:19]
    refs = refs[19 if first else 21 :]
    branch_ref, grad_ref, part_ref = refs[:3]
    branch_rows, qkv_weight, out_weight, line_sems, qkv_sems, out_sems = refs[3:]
    step = pl.program_id(0)
    group = half * GROUPS + step
    z = z_ref[0]
    line = line_copies(branch, branch_rows, line_sems)

    @pl.when(step == 0)
    def _():
        start_blocks(out_pieces, out_weight, out_sems, z)

    begin_lines(step, [line])

    @pl.when(step == 0)
    def _():
        start_blocks(qkv_pieces, qkv_weight, qkv_sems, z)
        wait_blocks(out_pieces, out_weight, out_sems, z)

    await_lines(step, [line])
    values = branch_rows[pl.ds(pl.multiple_of(step * rows, rows), rows), :]
    branch_ref[...] = values
    width = heads * HEAD
    factor = HEAD ** (-0.5)
    grad_mixed = mat_cols(values, out_weight[...]).astype(bf16)
    query = saved[:, :width]
    key_rows = saved[:, width : 2 * width]
    value = saved[:, 2 * width :]
    allowed = allowed_pairs(marks_ref, group, rows)
    zero = jnp.zeros((rows, width), f32)
    grad_query, grad_key, grad_value = zero, zero, zero
    for mask in head_masks((rows, width), heads):
        probs = softmax_of(jnp.where(mask, query, 0), key_rows, allowed)
        grad_probs = mat_cols(jnp.where(mask, grad_mixed, 0), value)
        inner = jnp.sum(grad_probs * probs, axis=1, keepdims=True)
        grad_scores = (probs * (grad_probs - inner)).astype(bf16)
        grad_query = jnp.where(mask, mat(grad_scores, key_rows), grad_query)
        grad_key = jnp.where(mask, mat_rows(grad_scores, query), grad_key)
        grad_value = jnp.where(mask, mat_rows(probs.astype(bf16), grad_mixed), grad_value)
    cosine, ahead, behind = (
        placed_table(ref, marks_ref, group, rows) for ref in (cos_ref, ahead_ref, behind_ref)
    )
    grads = jnp.concatenate(
        [
            rotate(grad_query * factor, cosine, -ahead, -behind),
            rotate(grad_key * factor, cosine, -ahead, -behind),
            grad_value,
        ],
        axis=1,
    ).astype(bf16)
    grad_ref[...] = grads

    @pl.when(step == 0)
    def _():
        wait_blocks(qkv_pieces, qkv_weight, qkv_sems, z)

    part_ref[...] = mat_cols(grads, qkv_weight[...]).astype(bf16)


def run_half(body, scalars, loose, blocked, whole, outputs, scratch, half, rows, prior, flops):
    loose, blocked, whole = list(loose), list(blocked), list(whole)
    kept = list(prior or [])
    out_shape, out_specs = [], []
    for width, shared in outputs:
        total = 2 * GROUPS if shared else GROUPS
        offset = half * GROUPS if shared else 0
        out_shape.append(jax.ShapeDtypeStruct((total * rows, width), bf16))
        out_specs.append(pl.BlockSpec((rows, width), lambda i, *_, offset=offset: (i + offset, 0)))
    in_specs = [ANYWHERE] * len(loose)
    for values in blocked:
        in_specs.append(
            pl.BlockSpec((rows, values.shape[1]), lambda i, *_: (i + half * GROUPS, 0))
        )
    for values in whole:
        in_specs.append(pl.BlockSpec(values.shape, lambda i, *_: (0, 0)))
    in_specs += [ANYWHERE] * len(kept)
    before = len(scalars) + len(loose) + len(blocked) + len(whole)
    moved = sum(values.size * values.dtype.itemsize for values in loose + blocked + whole)
    moved += sum(width * rows * GROUPS * 2 for width, _ in outputs)
    return pl.pallas_call(
        body,
        grid_spec=pltpu.PrefetchScalarGridSpec(
            num_scalar_prefetch=len(scalars),
            grid=(GROUPS,),
            in_specs=in_specs,
            out_specs=out_specs,
            scratch_shapes=scratch,
        ),
        out_shape=out_shape,
        input_output_aliases={before + index: index for index in range(len(kept))},
        compiler_params=pltpu.CompilerParams(
            dimension_semantics=("arbitrary",), vmem_limit_bytes=VMEM_BYTES
        ),
        cost_estimate=pl.CostEstimate(flops=flops, bytes_accessed=moved, transcendentals=0),
    )(*scalars, *loose, *blocked, *whole, *kept)


def per_device(
    tokens,
    seq_lengths,
    block_counts,
    qkv_weight,
    qkv_bias,
    out_weight,
    norm1_gain,
    norm1_bias,
    gate_weight,
    up_weight,
    down_weight,
    norm2_gain,
    norm2_bias,
    out_grad,
):
    rows, width = tokens.shape
    share = norm1_gain.shape[0]
    bias_share = qkv_bias.shape[0]
    hidden_share = gate_weight.shape[1] // PARTS
    heads = width // HEAD // PARTS
    head_cols = heads * HEAD
    spread = lax.axis_size("s")
    iz = lax.axis_index("z")
    iy = lax.axis_index("y")
    ix = lax.axis_index("x")
    ic = lax.axis_index("c")
    me = iy * 4 + ix * 2 + ic
    z_scalar = iz.astype(jnp.int32).reshape(1)

    def spread_gather(values, axis):
        return lax.all_gather(values, "s", axis=axis, tiled=True) if spread > 1 else values

    def spread_scatter(values, axis):
        if spread == 1:
            return values
        return lax.psum_scatter(values, "s", scatter_dimension=axis, tiled=True)

    out_blocks = gather_line(spread_gather(out_weight, 0))

    own_marks = block_marks(seq_lengths[0], block_counts[0])
    packed = jnp.concatenate(
        [
            norm1_gain,
            norm1_bias,
            norm2_gain,
            norm2_bias,
            qkv_bias,
            seq_lengths[0].astype(bf16),
            block_counts.astype(bf16),
        ]
    )
    packed = jnp.pad(packed, (0, -packed.shape[0] % 128))[None, :]

    qkv_parts = (
        qkv_weight.reshape(share, 3 * heads, PARTS, HEAD)
        .transpose(2, 0, 1, 3)
        .reshape(PARTS, share, 3 * head_cols)
    )
    qkv_rows = spread_gather(exchange(qkv_parts, me), 1).reshape(-1, 3 * head_cols)
    qkv_blocks = gather_line(qkv_rows)

    token_lines = gather_plane(tokens)

    plane_pack = doubled(packed, "c", SWAP, ic == 1)
    plane_pack = doubled(plane_pack, "x", SWAP, ix == 1)
    plane_pack = doubled(plane_pack, "y", SWAP, iy == 1)
    all_pack = spread_gather(plane_pack[:, None], 1).reshape(PARTS * spread, -1)
    all_pack = doubled(all_pack, "z", NEAR, iz % 2 == 1)
    all_pack = doubled(all_pack, "z", FAR, iz >= 2)

    def vector(index):
        return all_pack[:, index * share : (index + 1) * share].reshape(1, width).astype(f32)

    gain_one, shift_one, gain_two, shift_two = (vector(index) for index in range(4))
    bias_full = all_pack[:, 4 * share : 4 * share + bias_share].reshape(3 * heads, PARTS, HEAD)
    bias_mine = (
        lax.dynamic_index_in_dim(bias_full, me, 1, keepdims=False)
        .reshape(1, 3 * head_cols)
        .astype(f32)
    )

    relative = [core + 4 * dy + 2 * dx for core in (0, 1) for dy in (0, 1) for dx in (0, 1)]
    marks = plane_pack[:, 4 * share + bias_share : 4 * share + bias_share + 3].astype(jnp.int32)
    marks = jnp.stack(
        [lax.dynamic_index_in_dim(marks, me ^ mask, 0, keepdims=False) for mask in relative]
    )
    marks = jax.vmap(block_marks)(marks[:, :2], marks[:, 2])
    tables = rotary_tables(rows, heads)

    mlp_parts = jnp.stack(
        [
            weight.reshape(share, PARTS, hidden_share).transpose(1, 0, 2)
            for weight in (gate_weight, up_weight, down_weight)
        ],
        axis=1,
    )
    mlp_rows = spread_gather(exchange(mlp_parts, me), 2)
    gate_blocks, up_blocks, down_blocks = (
        gather_line(mlp_rows[:, index].reshape(-1, hidden_share)) for index in range(3)
    )

    dma = pltpu.SemaphoreType.DMA
    line_rows = GROUPS * rows

    def attention(half, prior):
        return run_half(
            functools.partial(attend_forward, prior is None, heads, rows, half),
            (z_scalar, marks),
            token_lines[half] + list(qkv_blocks) + list(out_blocks),
            (),
            (gain_one, shift_one, bias_mine) + tables,
            ((width, True), (3 * head_cols, True), (head_cols, True), (width, False)),
            [
                pltpu.VMEM((line_rows, width), bf16),
                pltpu.VMEM((width, 3 * head_cols), bf16),
                pltpu.VMEM((head_cols, width), bf16),
                dma((5,)),
                dma((4,)),
                dma((4,)),
            ],
            half,
            rows,
            prior,
            2 * line_rows * width * 4 * head_cols,
        )

    *shared, out_sent = attention(1, None)
    normed_one, saved, mixed, out_kept = attention(0, shared)
    inputs = tokens.astype(f32)
    middle = inputs + scatter_plane(out_kept, out_sent, rows)

    standard_two, inverse_two = standardize(middle)
    normed_lines = gather_plane((standard_two * gain_two + shift_two).astype(bf16))

    valid = valid_rows(own_marks, rows)[:, None]
    grad_top = jnp.where(valid, out_grad.astype(f32), 0.0)
    grad_lines = gather_plane(grad_top.astype(bf16))

    def feed(half, prior):
        return run_half(
            functools.partial(feed_both, prior is None, rows),
            (z_scalar,),
            normed_lines[half]
            + grad_lines[half]
            + list(gate_blocks)
            + list(up_blocks)
            + list(down_blocks),
            (),
            (),
            ((width, True),) * 2 + ((hidden_share, True),) * 3 + ((width, False),) * 2,
            [pltpu.VMEM((line_rows, width), bf16)] * 2
            + [pltpu.VMEM((width, hidden_share), bf16)] * 3
            + [dma((5,))] * 2
            + [dma((4,))] * 3,
            half,
            rows,
            prior,
            12 * line_rows * width * hidden_share,
        )

    *shared, back_sent, down_sent = feed(1, None)
    normed_two, grad_low, hidden, grad_gate, grad_up, back_kept, down_kept = feed(0, shared)
    grad_normed_two = scatter_plane(back_kept, back_sent, rows)
    down_grad = scatter_line(mat_rows(grad_low, hidden).astype(bf16), iz)
    gate_grad = scatter_line(mat_rows(normed_two, grad_gate).astype(bf16), iz)
    up_grad = scatter_line(mat_rows(normed_two, grad_up).astype(bf16), iz)

    grad_middle_norm, gain_two_grad, shift_two_grad = norm_back(
        grad_normed_two, standard_two, inverse_two, gain_two
    )
    grad_middle = grad_top + grad_middle_norm
    branch_lines = gather_plane(grad_middle.astype(bf16))

    down = scatter_plane(down_kept, down_sent, rows)
    layer_out = jnp.where(valid, middle + down, 0.0).astype(bf16)

    def attention_back(half, prior):
        return run_half(
            functools.partial(attend_backward, prior is None, heads, rows, half),
            (z_scalar, marks),
            branch_lines[half] + list(qkv_blocks) + list(out_blocks),
            (saved,),
            tables,
            ((width, True), (3 * head_cols, True), (width, False)),
            [
                pltpu.VMEM((line_rows, width), bf16),
                pltpu.VMEM((width, 3 * head_cols), bf16),
                pltpu.VMEM((head_cols, width), bf16),
                dma((5,)),
                dma((4,)),
                dma((4,)),
            ],
            half,
            rows,
            prior,
            2 * line_rows * width * 4 * head_cols,
        )

    *shared, input_sent = attention_back(1, None)
    grad_branch, grad_qkv, input_kept = attention_back(0, shared)
    qkv_grad = scatter_line(mat_rows(normed_one, grad_qkv).astype(bf16), iz)
    out_grad_weight = scatter_line(mat_rows(mixed, grad_branch).astype(bf16), iz)
    bias_part = jnp.sum(grad_qkv.astype(f32), axis=0).reshape(3 * heads, 1, HEAD)
    bias_grad = jnp.where(
        lax.broadcasted_iota(jnp.int32, (3 * heads, PARTS, HEAD), 1) == me, bias_part, 0.0
    )

    grad_normed_one = scatter_plane(input_kept, input_sent, rows)
    standard_one, inverse_one = standardize(inputs)
    grad_input_norm, gain_one_grad, shift_one_grad = norm_back(
        grad_normed_one, standard_one, inverse_one, gain_one
    )
    tokens_grad = (grad_middle + grad_input_norm).astype(bf16)

    devices = LINE * PARTS * spread
    small = jnp.concatenate(
        [
            part.reshape(devices, -1)
            for part in (gain_one_grad, shift_one_grad, gain_two_grad, shift_two_grad, bias_grad)
        ],
        axis=1,
    )
    small = halved(small, "z", FAR, iz >= 2)
    small = halved(small, "z", NEAR, iz % 2 == 1)
    small = halved(small, "y", SWAP, iy == 1)
    small = halved(small, "x", SWAP, ix == 1)
    small = halved(small, "c", SWAP, ic == 1)
    small = spread_scatter(small, 0)[0]

    mlp_back = jnp.stack(
        [part.reshape(PARTS, -1, hidden_share) for part in (gate_grad, up_grad, down_grad)], axis=1
    )
    mlp_back = exchange(spread_scatter(mlp_back, 2).astype(bf16), me)
    gate_share, up_share, down_share = (
        mlp_back[:, index].transpose(1, 0, 2).reshape(share, -1).astype(f32) for index in range(3)
    )
    qkv_back = spread_scatter(qkv_grad.reshape(PARTS, -1, 3 * head_cols), 1)
    qkv_back = exchange(qkv_back.astype(bf16), me)
    qkv_share = (
        qkv_back.reshape(PARTS, share, 3 * heads, HEAD)
        .transpose(1, 2, 0, 3)
        .reshape(share, 3 * width)
        .astype(f32)
    )
    out_share = spread_scatter(out_grad_weight, 0)
    return (
        layer_out,
        tokens_grad,
        qkv_share,
        small[4 * share :],
        out_share,
        small[:share],
        small[share : 2 * share],
        gate_share,
        up_share,
        down_share,
        small[2 * share : 3 * share],
        small[3 * share : 4 * share],
    )


def solution(mesh):
    devices = mesh.devices.reshape(LINE, 2, 2, 2, -1)
    rows, flat = P(AXES, None), P(AXES)
    return jax.shard_map(
        per_device,
        mesh=Mesh(devices, AXES),
        in_specs=(
            rows,
            rows,
            flat,
            rows,
            flat,
            rows,
            flat,
            flat,
            rows,
            rows,
            rows,
            flat,
            flat,
            rows,
        ),
        out_specs=(rows, rows, rows, flat, rows, flat, flat, rows, rows, rows, flat, flat),
        check_vma=False,
    )
```

time: 808 us -> 1070 us (1.32)
  waiting for transfers between devices: 227 us -> 444 us
  Pallas kernels: 0 us -> 149 us
  matrix products: 189 us -> 42.9 us
  starting transfers between devices: 77.6 us -> 214 us
  local copies, waits for them, and re-layouts: 207 us -> 152 us
  other arithmetic: 81.1 us -> 55.4 us
  between operations: 17.2 us -> 3.71 us
    ppermute x0 -> x40, waiting for transfers between devices: none -> 249 us  [along_z(): return lax.ppermute(values, 'z', perm)]
    pallas_call x0 -> x6, Pallas kernels: none -> 149 us  [run_half(): pl.pallas_call(body, grid_spec=pltpu.PrefetchScalarGridSpec(num_scalar_pr...]
    dot_general x20 -> x0, matrix products: 134 us -> none  [the longest x9 59.2 us: mat_cols(): lax.dot_general(left, right, (((1,), (1,)), ((), ())), preferred_element_...]
    ppermute x0 -> x40, starting transfers between devices: none -> 109 us  [along_z(): return lax.ppermute(values, 'z', perm)]
    unnamed x227 -> x150, local copies, waits for them, and re-layouts: 80 us -> 6.54 us
    ppermute x16, waiting for transfers between devices: 75.6 us -> 35.4 us  [over_y(): return lax.ppermute(values, 'y', SWAP)]
    ppermute x28, waiting for transfers between devices: 59.2 us -> 94.7 us  [exchange(): came = lax.ppermute(piece, PLANE, [(i, i ^ mask) for i in range(PARTS)])]
    ppermute x16, starting transfers between devices: 16.6 us -> 45.3 us  [over_x(): return lax.ppermute(values, 'x', SWAP)]
  transfers between devices with their start and end apart: 104 -> 134, of which waited for: 30 -> 53; matrix products, arithmetic and copies ran while one was open for 53% -> 21% of each run, Pallas kernels for 0% -> 4%
where the time goes in v2:
time: 1070 us; the launch traced here: 1060 us
  waiting for transfers between devices  444 us (41%)
  starting transfers between devices  214 us (20%)
  local copies, waits for them, and re-layouts  152 us (14%)
  Pallas kernels  149 us (14%)
  other arithmetic  55.4 us (5%)
  matrix products  42.9 us (4%)
    ppermute x40, waiting for transfers between devices, along_z(): return lax.ppermute(values, 'z', perm)  249 us
    pallas_call x6, Pallas kernels, run_half(): pl.pallas_call(body, grid_spec=pltpu.PrefetchScalarGridSpec(num_scalar_pr...  149 us
    ppermute x40, starting transfers between devices, along_z(): return lax.ppermute(values, 'z', perm)  109 us
    ppermute x28, waiting for transfers between devices, exchange(): came = lax.ppermute(piece, PLANE, [(i, i ^ mask) for i in range(PARTS)])  94.7 us
    ppermute x16, starting transfers between devices, over_x(): return lax.ppermute(values, 'x', SWAP)  45.3 us
    dot_general x5, matrix products, mat_rows(): lax.dot_general(left, right, (((0,), (0,)), ((), ())), preferred_element_...  42.9 us
    ppermute x16, waiting for transfers between devices, over_x(): return lax.ppermute(values, 'x', SWAP)  41.3 us
    ppermute x16, waiting for transfers between devices, over_y(): return lax.ppermute(values, 'y', SWAP)  35.4 us
  transfers between devices with their start and end apart: 134, of which 53 were waited for; matrix products, arithmetic and copies ran while one was open for 21% of the time, Pallas kernels for 4%

profile of v2, /device:TPU:0, one launch (start us, length us, event | category | flops | bytes accessed | tf_op | source)
XLA Modules:
  0.0 1060.9 jit_solution(6224779664277340358)
XLA Ops:
  18.3 10.3 collective-permute-done.1
  59.8 16.5 %collective-permute-done.19.refs_12_ = bf16[64,2048]{1,0:T(8,128)(2,1)S(1)} collective-permute-done((bf16[64,2048]{1,0:T(8,128)(2,1)}, bf16[64,2048]{1,0:T(8,128)(2,1)S(1)}, u32[]{:S(2)}, u32[]{:S(2)}) %collective-permute-start.19) | collective-permute-done | bytes 262176 | tf_op jit(solution)/shard_map/ppermute | solution.py:58
  99.9 30.0 %collective-permute-start.5 = (bf16[128,2048]{1,0:T(8,128)(2,1)}, bf16[128,2048]{1,0:T(8,128)(2,1)}, u32[]{:S(2)}, u32[]{:S(2)}) collective-permute-start(bf16[128,2048]{1,0:T(8,128)(2,1)} %slice.393), channel_id=1, source_target_pairs={{0,2},{2,0},{1,3},{3,1},{4,6},{6,4},{5,7},{7,5},{8,10},{10,8},{9,1... | collective-permute-start | bytes 1572872 | tf_op jit(solution)/shard_map/ppermute | solution.py:46
  153.5 20.7 %shard_map.229 = (bf16[2048,2048]{1,0:T(8,128)(2,1)}, bf16[2048,768]{1,0:T(8,128)(2,1)}, bf16[2048,256]{1,0:T(8,128)(2,1)}, bf16[1024,2048]{1,0:T(8,128)(2,1)}) custom-call(s32[1]{0:T(128)} %bitcast.6.z_ref, s32[8,6]{1,0:T(8,128)} %reshape.384.marks_ref, bf16[256,2048]{1,0:T(8,128)(2,1)} %collective-permute-done.24.refs_0_, ...), custom_call_target="tpu_custom_call" | custom-call | flops 4294967296 | bytes 20728832 | tf_op jit(solution)/shard_map/pallas_call | solution.py:490
  185.9 21.1 %shard_map.230 = (bf16[2048,2048]{1,0:T(8,128)(2,1)}, bf16[2048,768]{1,0:T(8,128)(2,1)}, bf16[2048,256]{1,0:T(8,128)(2,1)}, bf16[1024,2048]{1,0:T(8,128)(2,1)}) custom-call(s32[1]{0:T(128)} %bitcast.6.z_ref, s32[8,6]{1,0:T(8,128)} %reshape.384.marks_ref, bf16[256,2048]{1,0:T(8,128)(2,1)} %refs_0_.1, ...), custom_call_target="tpu_custom_call", output_to_operand_aliasing={{0}: (23, {}), {1}: (24, {}), {2}: (25, {})} | custom-call | flops 4294967296 | bytes 20728832 | tf_op jit(solution)/shard_map/pallas_call | solution.py:490
  215.6 16.0 %collective-permute-done.47 = bf16[1,3,64,704]{3,2,0,1:T(8,128)(2,1)S(1)} collective-permute-done((bf16[1,3,64,704]{3,2,0,1:T(8,128)(2,1)S(1)}, bf16[1,3,64,704]{3,2,0,1:T(8,128)(2,1)S(1)}, u32[]{:S(2)}, u32[]{:S(2)}) %collective-permute-start.47) | collective-permute-done | bytes 270368 | tf_op jit(solution)/shard_map/ppermute | solution.py:101
  238.0 22.6 %collective-permute-done.48 = bf16[1,3,64,704]{3,2,0,1:T(8,128)(2,1)S(1)} collective-permute-done((bf16[1,3,64,704]{3,2,0,1:T(8,128)(2,1)S(1)}, bf16[1,3,64,704]{3,2,0,1:T(8,128)(2,1)S(1)}, u32[]{:S(2)}, u32[]{:S(2)}) %collective-permute-start.48) | collective-permute-done | bytes 270368 | tf_op jit(solution)/shard_map/ppermute | solution.py:101
  281.8 23.5 %collective-permute-start.58 = (bf16[512,704]{0,1:T(8,128)(2,1)S(1)}, bf16[512,704]{0,1:T(8,128)(2,1)S(1)}, u32[]{:S(2)}, u32[]{:S(2)}) collective-permute-start(bf16[512,704]{0,1:T(8,128)(2,1)S(1)} %copy-done.44), channel_id=1, source_target_pairs={{0,16},{8,24},{16,0},{24,8},{1,17},{9,25},{17,1},{25,9},{2,18},{10... | collective-permute-start | bytes 2162696 | tf_op jit(solution)/shard_map/ppermute | solution.py:58
  309.6 22.5 %collective-permute-done.50 = bf16[512,704]{0,1:T(8,128)(2,1)S(1)} collective-permute-done((bf16[512,704]{0,1:T(8,128)(2,1)}, bf16[512,704]{0,1:T(8,128)(2,1)S(1)}, u32[]{:S(2)}, u32[]{:S(2)}) %collective-permute-start.50) | collective-permute-done | bytes 720928 | tf_op jit(solution)/shard_map/ppermute | solution.py:58
  334.9 28.6 %collective-permute-start.53 = (bf16[512,704]{0,1:T(8,128)(2,1)S(1)}, bf16[512,704]{0,1:T(8,128)(2,1)S(1)}, u32[]{:S(2)}, u32[]{:S(2)}) collective-permute-start(bf16[512,704]{0,1:T(8,128)(2,1)S(1)} %copy-done.43), channel_id=1, source_target_pairs={{0,8},{8,0},{16,24},{24,16},{1,9},{9,1},{17,25},{25,17},{2,10},{10... | collective-permute-start | bytes 2162696 | tf_op jit(solution)/shard_map/ppermute | solution.py:58
  363.6 14.9 %collective-permute-done.58 = bf16[512,704]{0,1:T(8,128)(2,1)S(1)} collective-permute-done((bf16[512,704]{0,1:T(8,128)(2,1)S(1)}, bf16[512,704]{0,1:T(8,128)(2,1)S(1)}, u32[]{:S(2)}, u32[]{:S(2)}) %collective-permute-start.58) | collective-permute-done | bytes 720928 | tf_op jit(solution)/shard_map/ppermute | solution.py:58
  382.3 26.4 %collective-permute-done.54 = bf16[512,704]{0,1:T(8,128)(2,1)S(1)} collective-permute-done((bf16[512,704]{0,1:T(8,128)(2,1)S(1)}, bf16[512,704]{0,1:T(8,128)(2,1)S(1)}, u32[]{:S(2)}, u32[]{:S(2)}) %collective-permute-start.54) | collective-permute-done | bytes 720928 | tf_op jit(solution)/shard_map/ppermute | solution.py:58
  424.1 15.3 %collective-permute-done.60 = bf16[512,704]{0,1:T(8,128)(2,1)S(1)} collective-permute-done((bf16[512,704]{0,1:T(8,128)(2,1)S(1)}, bf16[512,704]{0,1:T(8,128)(2,1)S(1)}, u32[]{:S(2)}, u32[]{:S(2)}) %collective-permute-start.60) | collective-permute-done | bytes 720928 | tf_op jit(solution)/shard_map/ppermute | solution.py:58
  443.6 15.8 %collective-permute-done.56 = bf16[512,704]{0,1:T(8,128)(2,1)S(1)} collective-permute-done((bf16[512,704]{0,1:T(8,128)(2,1)S(1)}, bf16[512,704]{0,1:T(8,128)(2,1)S(1)}, u32[]{:S(2)}, u32[]{:S(2)}) %collective-permute-start.56) | collective-permute-done | bytes 720928 | tf_op jit(solution)/shard_map/ppermute | solution.py:58
  463.3 10.6 %collective-permute-done.36.refs_3_ = bf16[128,2048]{1,0:T(8,128)(2,1)} collective-permute-done((bf16[128,2048]{1,0:T(8,128)(2,1)S(1)}, bf16[128,2048]{1,0:T(8,128)(2,1)}, u32[]{:S(2)}, u32[]{:S(2)}) %collective-permute-start.36) | collective-permute-done | bytes 524320 | tf_op jit(solution)/shard_map/ppermute | solution.py:46
  503.4 30.3 %shard_map.231 = (bf16[2048,2048]{1,0:T(8,128)(2,1)}, bf16[2048,2048]{1,0:T(8,128)(2,1)}, bf16[2048,704]{1,0:T(8,128)(2,1)}, bf16[2048,704]{1,0:T(8,128)(2,1)}, ...) custom-call(s32[1]{0:T(128)} %bitcast.6.z_ref, ...), custom_call_target="tpu_custom_call" | custom-call | flops 17716740096 | bytes 40304640 | tf_op jit(solution)/shard_map/pallas_call | solution.py:490
  533.8 30.5 %shard_map.232 = (bf16[2048,2048]{1,0:T(8,128)(2,1)}, bf16[2048,2048]{1,0:T(8,128)(2,1)}, bf16[2048,704]{1,0:T(8,128)(2,1)}, bf16[2048,704]{1,0:T(8,128)(2,1)}, ...) custom-call(s32[1]{0:T(128)} %bitcast.6.z_ref, ...), custom_call_target="tpu_custom_call", output_to_operand_aliasing={{0}: (26, {}), {1}: (27, {}), {2}: (28, {}), {3}: (29, {}),... | custom-call | flops 17716740096 | bytes 40304640 | tf_op jit(solution)/shard_map/pallas_call | solution.py:490
  564.3 10.9 %convolution_convert_fusion.3 = bf16[2048,704]{0,1:T(8,128)(2,1)} fusion(bf16[2048,2048]{1,0:T(8,128)(2,1)} %get-tuple-element.63, bf16[2048,704]{1,0:T(8,128)(2,1)} %get-tuple-element.64), kind=kOutput, calls=%fused_computation.4 | convolution fusion | flops 5907021824 | bytes 14155776 | tf_op jit(solution)/shard_map/dot_general | solution.py:34
  612.9 10.2 constant_dynamic-slice_fusion.10
  641.9 14.7 %collective-permute-done.117 = bf16[512,704]{0,1:T(8,128)(2,1)S(1)} collective-permute-done((bf16[512,704]{0,1:T(8,128)(2,1)S(1)}, bf16[512,704]{0,1:T(8,128)(2,1)S(1)}, u32[]{:S(2)}, u32[]{:S(2)}) %collective-permute-start.117) | collective-permute-done | bytes 720928 | tf_op jit(solution)/shard_map/ppermute | solution.py:58
  659.4 12.7 %collective-permute-done.121 = bf16[512,704]{0,1:T(8,128)(2,1)S(1)} collective-permute-done((bf16[512,704]{0,1:T(8,128)(2,1)S(1)}, bf16[512,704]{0,1:T(8,128)(2,1)S(1)}, u32[]{:S(2)}, u32[]{:S(2)}) %collective-permute-start.121) | collective-permute-done | bytes 720928 | tf_op jit(solution)/shard_map/ppermute | solution.py:58
  676.9 10.7 %collective-permute-done.124 = bf16[512,704]{0,1:T(8,128)(2,1)S(1)} collective-permute-done((bf16[512,704]{0,1:T(8,128)(2,1)S(1)}, bf16[512,704]{0,1:T(8,128)(2,1)S(1)}, u32[]{:S(2)}, u32[]{:S(2)}) %collective-permute-start.124) | collective-permute-done | bytes 720928 | tf_op jit(solution)/shard_map/ppermute | solution.py:58
  690.0 17.6 %collective-permute-done.126 = bf16[512,704]{0,1:T(8,128)(2,1)S(1)} collective-permute-done((bf16[512,704]{0,1:T(8,128)(2,1)S(1)}, bf16[512,704]{0,1:T(8,128)(2,1)S(1)}, u32[]{:S(2)}, u32[]{:S(2)}) %collective-permute-start.126) | collective-permute-done | bytes 720928 | tf_op jit(solution)/shard_map/ppermute | solution.py:58
  744.2 9.8 collective-permute-done.118
  770.5 10.6 collective-permute-done.75
  788.7 10.6 collective-permute-done.122
  859.6 23.1 %shard_map.233 = (bf16[2048,2048]{1,0:T(8,128)(2,1)}, bf16[2048,768]{1,0:T(8,128)(2,1)}, bf16[1024,2048]{1,0:T(8,128)(2,1)}) custom-call(s32[1]{0:T(128)} %bitcast.6.z_ref, s32[8,6]{1,0:T(8,128)} %reshape.384.marks_ref, bf16[256,2048]{1,0:T(8,128)(2,1)} %collective-permute-done.85.refs_0_, bf16[256,2048]{1,0:T(8,128)(2,1)} %collective-permute-done.86.refs_1_, ...), custom_call_target="tpu_custom_call" | custom-call | flops 4294967296 | bytes 23330816 | tf_op jit(solution)/shard_map/pallas_call | solution.py:490
  882.8 22.9 %shard_map.234 = (bf16[2048,2048]{1,0:T(8,128)(2,1)}, bf16[2048,768]{1,0:T(8,128)(2,1)}, bf16[1024,2048]{1,0:T(8,128)(2,1)}) custom-call(s32[1]{0:T(128)} %bitcast.6.z_ref, s32[8,6]{1,0:T(8,128)} %reshape.384.marks_ref, bf16[256,2048]{1,0:T(8,128)(2,1)} %get-tuple-element.77.refs_0_, ...), custom_call_target="tpu_custom_call", output_to_operand_aliasing={{0}: (21, {}), {1}: (22, {})} | custom-call | flops 4294967296 | bytes 23330816 | tf_op jit(solution)/shard_map/pallas_call | solution.py:490
  905.6 10.2 convolution_convert_fusion
  946.2 21.6 %collective-permute-done.96 = bf16[512,768]{1,0:T(8,128)(2,1)S(1)} collective-permute-done((bf16[512,768]{1,0:T(8,128)(2,1)S(1)}, bf16[512,768]{1,0:T(8,128)(2,1)S(1)}, u32[]{:S(2)}, u32[]{:S(2)}) %collective-permute-start.96) | collective-permute-done | bytes 786464 | tf_op jit(solution)/shard_map/ppermute | solution.py:58
  986.7 9.5 collective-permute-done.114
  999.7 12.9 %collective-permute-done.100 = bf16[1,64,768]{2,1,0:T(8,128)(2,1)S(1)} collective-permute-done((bf16[1,64,768]{2,1,0:T(8,128)(2,1)S(1)}, bf16[1,64,768]{2,1,0:T(8,128)(2,1)S(1)}, u32[]{:S(2)}, u32[]{:S(2)}) %collective-permute-start.100) | collective-permute-done | bytes 98336 | tf_op jit(solution)/shard_map/ppermute | solution.py:101
  (603 shorter events, 493.3 us)
Async XLA Ops:
  0.6 78.2 %collective-permute-start.4 = (bf16[256,2048]{1,0:T(8,128)(2,1)}, bf16[256,2048]{1,0:T(8,128)(2,1)}, u32[]{:S(2)}, u32[]{:S(2)}) collective-permute-start(bf16[256,2048]{1,0:T(8,128)(2,1)} %refs_0_.1), channel_id=1, source_target_pairs={{0,4},{4,0},{1,5},{5,1},{2,6},{6,2},{3,7},{7,3},{8,12},{12,8},{9,1... | collective-permute-start | bytes 3145736 | tf_op jit(solution)/shard_map/ppermute | solution.py:50
  3.7 83.7 %collective-permute-start.3 = (bf16[256,2048]{1,0:T(8,128)(2,1)}, bf16[256,2048]{1,0:T(8,128)(2,1)}, u32[]{:S(2)}, u32[]{:S(2)}) collective-permute-start(bf16[256,2048]{1,0:T(8,128)(2,1)} %refs_0_.1), channel_id=1, source_target_pairs={{0,2},{2,0},{1,3},{3,1},{4,6},{6,4},{5,7},{7,5},{8,10},{10,8},{9,1... | collective-permute-start | bytes 3145736 | tf_op jit(solution)/shard_map/ppermute | solution.py:46
  59.0 70.9 %collective-permute-start.16 = (bf16[512,768]{1,0:T(8,128)(2,1)S(1)}, bf16[512,768]{1,0:T(8,128)(2,1)S(1)}, u32[]{:S(2)}, u32[]{:S(2)}) collective-permute-start(bf16[512,768]{1,0:T(8,128)(2,1)S(1)} %bitcast.165), channel_id=1, source_target_pairs={{8,16},{16,8},{9,17},{17,9},{10,18},{18,10},{11,19},{19,11},{12,20... | collective-permute-start | bytes 2359304 | tf_op jit(solution)/shard_map/ppermute | solution.py:58
  76.2 53.7 %collective-permute-start.15 = (bf16[512,768]{1,0:T(8,128)(2,1)S(1)}, bf16[512,768]{1,0:T(8,128)(2,1)S(1)}, u32[]{:S(2)}, u32[]{:S(2)}) collective-permute-start(bf16[512,768]{1,0:T(8,128)(2,1)S(1)} %bitcast.166), channel_id=1, source_target_pairs={{0,16},{8,24},{16,0},{24,8},{1,17},{9,25},{17,1},{25,9},{2,18},{10... | collective-permute-start | bytes 2359304 | tf_op jit(solution)/shard_map/ppermute | solution.py:58
  77.0 53.1 %collective-permute-start.14 = (bf16[512,768]{1,0:T(8,128)(2,1)S(1)}, bf16[512,768]{1,0:T(8,128)(2,1)}, u32[]{:S(2)}, u32[]{:S(2)}) collective-permute-start(bf16[512,768]{1,0:T(8,128)(2,1)S(1)} %bitcast.167), channel_id=1, source_target_pairs={{0,8},{8,0},{16,24},{24,16},{1,9},{9,1},{17,25},{25,17},{2,10},{10... | collective-permute-start | bytes 2359304 | tf_op jit(solution)/shard_map/ppermute | solution.py:58
  78.8 52.2 %collective-permute-start.24 = (bf16[256,2048]{1,0:T(8,128)(2,1)S(1)}, bf16[256,2048]{1,0:T(8,128)(2,1)}, u32[]{:S(2)}, u32[]{:S(2)}) collective-permute-start(bf16[256,2048]{1,0:T(8,128)(2,1)S(1)} %copy-done), channel_id=1, source_target_pairs={{0,1},{1,0},{2,3},{3,2},{4,5},{5,4},{6,7},{7,6},{8,9},{9,8},{10,11... | collective-permute-start | bytes 3145736 | tf_op jit(solution)/shard_map/ppermute | solution.py:54
  213.7 60.0 %collective-permute-start.66 = (bf16[256,2048]{1,0:T(8,128)(2,1)}, bf16[256,2048]{1,0:T(8,128)(2,1)}, u32[]{:S(2)}, u32[]{:S(2)}) collective-permute-start(bf16[256,2048]{1,0:T(8,128)(2,1)} %fusion.12.refs_5_), channel_id=1, source_target_pairs={{0,1},{1,0},{2,3},{3,2},{4,5},{5,4},{6,7},{7,6},{8,9},{9,8},{10,11... | collective-permute-start | bytes 3145736 | tf_op jit(solution)/shard_map/ppermute | solution.py:54
  213.8 52.2 %collective-permute-start.39 = (bf16[256,2048]{1,0:T(8,128)(2,1)}, bf16[256,2048]{1,0:T(8,128)(2,1)}, u32[]{:S(2)}, u32[]{:S(2)}) collective-permute-start(bf16[256,2048]{1,0:T(8,128)(2,1)} %fusion.12.refs_5_), channel_id=1, source_target_pairs={{0,4},{4,0},{1,5},{5,1},{2,6},{6,2},{3,7},{7,3},{8,12},{12,8},{9,1... | collective-permute-start | bytes 3145736 | tf_op jit(solution)/shard_map/ppermute | solution.py:50
  235.2 46.6 %collective-permute-start.33 = (bf16[256,2048]{1,0:T(8,128)(2,1)}, bf16[256,2048]{1,0:T(8,128)(2,1)}, u32[]{:S(2)}, u32[]{:S(2)}) collective-permute-start(bf16[256,2048]{1,0:T(8,128)(2,1)} %pad_maximum_fusion.3), channel_id=1, source_target_pairs={{0,4},{4,0},{1,5},{5,1},{2,6},{6,2},{3,7},{7,3},{8,12},{12,8},{9,1... | collective-permute-start | bytes 3145736 | tf_op jit(solution)/shard_map/ppermute | solution.py:50
  260.6 44.8 %collective-permute-start.31 = (bf16[256,2048]{1,0:T(8,128)(2,1)}, bf16[256,2048]{1,0:T(8,128)(2,1)}, u32[]{:S(2)}, u32[]{:S(2)}) collective-permute-start(bf16[256,2048]{1,0:T(8,128)(2,1)} %pad_maximum_fusion.2), channel_id=1, source_target_pairs={{0,2},{2,0},{1,3},{3,1},{4,6},{6,4},{5,7},{7,5},{8,10},{10,8},{9,1... | collective-permute-start | bytes 3145736 | tf_op jit(solution)/shard_map/ppermute | solution.py:46
  271.4 60.7 %collective-permute-start.50 = (bf16[512,704]{0,1:T(8,128)(2,1)}, bf16[512,704]{0,1:T(8,128)(2,1)S(1)}, u32[]{:S(2)}, u32[]{:S(2)}) collective-permute-start(bf16[512,704]{0,1:T(8,128)(2,1)} %copy.223), channel_id=1, source_target_pairs={{0,16},{8,24},{16,0},{24,8},{1,17},{9,25},{17,1},{25,9},{2,18},{10... | collective-permute-start | bytes 2162696 | tf_op jit(solution)/shard_map/ppermute | solution.py:58
  273.7 59.2 %collective-permute-start.49 = (bf16[512,704]{0,1:T(8,128)(2,1)}, bf16[512,704]{0,1:T(8,128)(2,1)S(1)}, u32[]{:S(2)}, u32[]{:S(2)}) collective-permute-start(bf16[512,704]{0,1:T(8,128)(2,1)} %copy.223), channel_id=1, source_target_pairs={{0,8},{8,0},{16,24},{24,16},{1,9},{9,1},{17,25},{25,17},{2,10},{10... | collective-permute-start | bytes 2162696 | tf_op jit(solution)/shard_map/ppermute | solution.py:58
  275.3 59.6 %collective-permute-start.59 = (bf16[512,704]{0,1:T(8,128)(2,1)S(1)}, bf16[512,704]{0,1:T(8,128)(2,1)S(1)}, u32[]{:S(2)}, u32[]{:S(2)}) collective-permute-start(bf16[512,704]{0,1:T(8,128)(2,1)S(1)} %copy-done.44), channel_id=1, source_target_pairs={{8,16},{16,8},{9,17},{17,9},{10,18},{18,10},{11,19},{19,11},{12,20... | collective-permute-start | bytes 2162696 | tf_op jit(solution)/shard_map/ppermute | solution.py:58
  281.8 96.7 %collective-permute-start.58 = (bf16[512,704]{0,1:T(8,128)(2,1)S(1)}, bf16[512,704]{0,1:T(8,128)(2,1)S(1)}, u32[]{:S(2)}, u32[]{:S(2)}) collective-permute-start(bf16[512,704]{0,1:T(8,128)(2,1)S(1)} %copy-done.44), channel_id=1, source_target_pairs={{0,16},{8,24},{16,0},{24,8},{1,17},{9,25},{17,1},{25,9},{2,18},{10... | collective-permute-start | bytes 2162696 | tf_op jit(solution)/shard_map/ppermute | solution.py:58
  305.3 73.6 %collective-permute-start.57 = (bf16[512,704]{0,1:T(8,128)(2,1)S(1)}, bf16[512,704]{0,1:T(8,128)(2,1)S(1)}, u32[]{:S(2)}, u32[]{:S(2)}) collective-permute-start(bf16[512,704]{0,1:T(8,128)(2,1)S(1)} %copy-done.44), channel_id=1, source_target_pairs={{0,8},{8,0},{16,24},{24,16},{1,9},{9,1},{17,25},{25,17},{2,10},{10... | collective-permute-start | bytes 2162696 | tf_op jit(solution)/shard_map/ppermute | solution.py:58
  332.1 48.6 %collective-permute-start.55 = (bf16[512,704]{0,1:T(8,128)(2,1)S(1)}, bf16[512,704]{0,1:T(8,128)(2,1)S(1)}, u32[]{:S(2)}, u32[]{:S(2)}) collective-permute-start(bf16[512,704]{0,1:T(8,128)(2,1)S(1)} %copy-done.43), channel_id=1, source_target_pairs={{8,16},{16,8},{9,17},{17,9},{10,18},{18,10},{11,19},{19,11},{12,20... | collective-permute-start | bytes 2162696 | tf_op jit(solution)/shard_map/ppermute | solution.py:58
  332.8 75.9 %collective-permute-start.54 = (bf16[512,704]{0,1:T(8,128)(2,1)S(1)}, bf16[512,704]{0,1:T(8,128)(2,1)S(1)}, u32[]{:S(2)}, u32[]{:S(2)}) collective-permute-start(bf16[512,704]{0,1:T(8,128)(2,1)S(1)} %copy-done.43), channel_id=1, source_target_pairs={{0,16},{8,24},{16,0},{24,8},{1,17},{9,25},{17,1},{25,9},{2,18},{10... | collective-permute-start | bytes 2162696 | tf_op jit(solution)/shard_map/ppermute | solution.py:58
  334.9 74.7 %collective-permute-start.53 = (bf16[512,704]{0,1:T(8,128)(2,1)S(1)}, bf16[512,704]{0,1:T(8,128)(2,1)S(1)}, u32[]{:S(2)}, u32[]{:S(2)}) collective-permute-start(bf16[512,704]{0,1:T(8,128)(2,1)S(1)} %copy-done.43), channel_id=1, source_target_pairs={{0,8},{8,0},{16,24},{24,16},{1,9},{9,1},{17,25},{25,17},{2,10},{10... | collective-permute-start | bytes 2162696 | tf_op jit(solution)/shard_map/ppermute | solution.py:58
  379.0 45.1 %collective-permute-start.52 = (bf16[512,704]{0,1:T(8,128)(2,1)S(1)}, bf16[512,704]{0,1:T(8,128)(2,1)S(1)}, u32[]{:S(2)}, u32[]{:S(2)}) collective-permute-start(bf16[512,704]{0,1:T(8,128)(2,1)S(1)} %collective-permute-done.50), channel_id=1, source_target_pairs={{16,24},{8,0},{17,25},{9,1},{18,26},{10,2},{19,27},{11,3},{20,28},... | collective-permute-start | bytes 2162696 | tf_op jit(solution)/shard_map/ppermute | solution.py:58
  380.7 60.0 %collective-permute-start.35 = (bf16[256,2048]{1,0:T(8,128)(2,1)S(1)}, bf16[256,2048]{1,0:T(8,128)(2,1)}, u32[]{:S(2)}, u32[]{:S(2)}) collective-permute-start(bf16[256,2048]{1,0:T(8,128)(2,1)S(1)} %add_convert_fusion.refs_0_), channel_id=1, source_target_pairs={{0,4},{4,0},{1,5},{5,1},{2,6},{6,2},{3,7},{7,3},{8,12},{12,8},{9,1... | collective-permute-start | bytes 3145736 | tf_op jit(solution)/shard_map/ppermute | solution.py:50
  459.4 44.0 %collective-permute-start.61 = (bf16[256,2048]{1,0:T(8,128)(2,1)S(1)}, bf16[256,2048]{1,0:T(8,128)(2,1)}, u32[]{:S(2)}, u32[]{:S(2)}) collective-permute-start(bf16[256,2048]{1,0:T(8,128)(2,1)S(1)} %add_convert_fusion.refs_0_), channel_id=1, source_target_pairs={{0,1},{1,0},{2,3},{3,2},{4,5},{5,4},{6,7},{7,6},{8,9},{9,8},{10,11... | collective-permute-start | bytes 3145736 | tf_op jit(solution)/shard_map/ppermute | solution.py:54
  461.1 42.3 %collective-permute-start.63 = (bf16[256,2048]{1,0:T(8,128)(2,1)}, bf16[256,2048]{1,0:T(8,128)(2,1)}, u32[]{:S(2)}, u32[]{:S(2)}) collective-permute-start(bf16[256,2048]{1,0:T(8,128)(2,1)} %collective-permute-done.35.refs_2_), channel_id=1, source_target_pairs={{0,1},{1,0},{2,3},{3,2},{4,5},{5,4},{6,7},{7,6},{8,9},{9,8},{10,11... | collective-permute-start | bytes 3145736 | tf_op jit(solution)/shard_map/ppermute | solution.py:54
  583.2 129.9 %collective-permute-start.71 = (bf16[1024,2048]{1,0:T(8,128)(2,1)}, bf16[1024,2048]{1,0:T(8,128)(2,1)}, u32[]{:S(2)}, u32[]{:S(2)}) collective-permute-start(bf16[1024,2048]{1,0:T(8,128)(2,1)} %get-tuple-element.51), channel_id=1, source_target_pairs={{0,1},{1,0},{2,3},{3,2},{4,5},{5,4},{6,7},{7,6},{8,9},{9,8},{10,11... | collective-permute-start | bytes 12582920 | tf_op jit(solution)/shard_map/ppermute | solution.py:54
  583.7 125.2 %collective-permute-start.76 = (bf16[1024,2048]{1,0:T(8,128)(2,1)}, bf16[1024,2048]{1,0:T(8,128)(2,1)}, u32[]{:S(2)}, u32[]{:S(2)}) collective-permute-start(bf16[1024,2048]{1,0:T(8,128)(2,1)} %get-tuple-element.53), channel_id=1, source_target_pairs={{0,1},{1,0},{2,3},{3,2},{4,5},{5,4},{6,7},{7,6},{8,9},{9,8},{10,11... | collective-permute-start | bytes 12582920 | tf_op jit(solution)/shard_map/ppermute | solution.py:54
  676.1 65.5 %collective-permute-start.115 = (bf16[512,704]{0,1:T(8,128)(2,1)S(1)}, bf16[512,704]{0,1:T(8,128)(2,1)S(1)}, u32[]{:S(2)}, u32[]{:S(2)}) collective-permute-start(bf16[512,704]{0,1:T(8,128)(2,1)S(1)} %bitcast.201), channel_id=1, source_target_pairs={{8,16},{16,8},{9,17},{17,9},{10,18},{18,10},{11,19},{19,11},{12,20... | collective-permute-start | bytes 2162696 | tf_op jit(solution)/shard_map/ppermute | solution.py:58
  687.5 55.0 %collective-permute-start.116 = (bf16[512,704]{0,1:T(8,128)(2,1)S(1)}, bf16[512,704]{0,1:T(8,128)(2,1)S(1)}, u32[]{:S(2)}, u32[]{:S(2)}) collective-permute-start(bf16[512,704]{0,1:T(8,128)(2,1)S(1)} %bitcast.202), channel_id=1, source_target_pairs={{0,8},{8,0},{16,24},{24,16},{1,9},{9,1},{17,25},{25,17},{2,10},{10... | collective-permute-start | bytes 2162696 | tf_op jit(solution)/shard_map/ppermute | solution.py:58
  707.6 46.3 %collective-permute-start.118 = (bf16[512,704]{0,1:T(8,128)(2,1)S(1)}, bf16[512,704]{0,1:T(8,128)(2,1)S(1)}, u32[]{:S(2)}, u32[]{:S(2)}) collective-permute-start(bf16[512,704]{0,1:T(8,128)(2,1)S(1)} %fusion.25), channel_id=1, source_target_pairs={{0,16},{8,24},{16,0},{24,8},{1,17},{9,25},{17,1},{25,9},{2,18},{10... | collective-permute-start | bytes 2162696 | tf_op jit(solution)/shard_map/ppermute | solution.py:58
  741.6 47.1 %collective-permute-start.119 = (bf16[512,704]{0,1:T(8,128)(2,1)S(1)}, bf16[512,704]{0,1:T(8,128)(2,1)S(1)}, u32[]{:S(2)}, u32[]{:S(2)}) collective-permute-start(bf16[512,704]{0,1:T(8,128)(2,1)S(1)} %bitcast.198), channel_id=1, source_target_pairs={{8,16},{16,8},{9,17},{17,9},{10,18},{18,10},{11,19},{19,11},{12,20... | collective-permute-start | bytes 2162696 | tf_op jit(solution)/shard_map/ppermute | solution.py:58
  882.7 58.6 %collective-permute-start.90 = (bf16[1024,2048]{1,0:T(8,128)(2,1)}, bf16[1024,2048]{1,0:T(8,128)(2,1)}, u32[]{:S(2)}, u32[]{:S(2)}) collective-permute-start(bf16[1024,2048]{1,0:T(8,128)(2,1)} %get-tuple-element.58), channel_id=1, source_target_pairs={{0,1},{1,0},{2,3},{3,2},{4,5},{5,4},{6,7},{7,6},{8,9},{9,8},{10,11... | collective-permute-start | bytes 12582920 | tf_op jit(solution)/shard_map/ppermute | solution.py:54
  920.1 48.4 %collective-permute-start.95 = (bf16[512,768]{1,0:T(8,128)(2,1)S(1)}, bf16[512,768]{1,0:T(8,128)(2,1)S(1)}, u32[]{:S(2)}, u32[]{:S(2)}) collective-permute-start(bf16[512,768]{1,0:T(8,128)(2,1)S(1)} %get-tuple-element.107), channel_id=1, source_target_pairs={{8,16},{16,8},{9,17},{17,9},{10,18},{18,10},{11,19},{19,11},{12,20... | collective-permute-start | bytes 2359304 | tf_op jit(solution)/shard_map/ppermute | solution.py:58
  983.0 44.5 %collective-permute-start.94 = (bf16[256,2048]{1,0:T(8,128)(2,1)S(1)}, bf16[256,2048]{1,0:T(8,128)(2,1)S(1)}, u32[]{:S(2)}, u32[]{:S(2)}) collective-permute-start(bf16[256,2048]{1,0:T(8,128)(2,1)S(1)} %pad_maximum_fusion.9), channel_id=1, source_target_pairs={{0,4},{4,0},{1,5},{5,1},{2,6},{6,2},{3,7},{7,3},{8,12},{12,8},{9,1... | collective-permute-start | bytes 3145736 | tf_op jit(solution)/shard_map/ppermute | solution.py:50
  984.5 43.0 %collective-permute-start.92 = (bf16[256,2048]{1,0:T(8,128)(2,1)S(1)}, bf16[256,2048]{1,0:T(8,128)(2,1)S(1)}, u32[]{:S(2)}, u32[]{:S(2)}) collective-permute-start(bf16[256,2048]{1,0:T(8,128)(2,1)S(1)} %pad_maximum_fusion.8), channel_id=1, source_target_pairs={{0,2},{2,0},{1,3},{3,1},{4,6},{6,4},{5,7},{7,5},{8,10},{10,8},{9,1... | collective-permute-start | bytes 3145736 | tf_op jit(solution)/shard_map/ppermute | solution.py:46
  (174 other events, 3758.8 us)

commit v3 on v2

--- a/solution.py
+++ b/solution.py
@@ -19,9 +19,6 @@
 SWAP = ((0, 1), (1, 0))
 NEAR = ((0, 1), (1, 0), (2, 3), (3, 2))
 FAR = ((0, 2), (1, 3), (2, 0), (3, 1))
-INNER = ((1, 2), (2, 1))
-OUTWARD = ((2, 3), (1, 0))
-INWARD = ((3, 2), (0, 1))
 
 eps_norm = 1e-05
 f32 = jnp.float32
@@ -54,72 +51,93 @@
     return lax.ppermute(values, "c", SWAP)
 
 
-def along_z(values, perm):
-    return lax.ppermute(values, "z", perm)
+def gather_line(values):
+    return lax.all_gather(values, "z", axis=0, tiled=True)
+
+
+def scatter_line(values):
+    return lax.psum_scatter(values.astype(bf16), "z", scatter_dimension=0, tiled=True)
 
 
 def after(values, *earlier):
     return lax.optimization_barrier((values, *earlier))[0]
 
 
-def gather_plane(own):
+def gather_plane(own, *earlier):
     half = own.shape[0] // 2
     from_x = over_x(own)
     from_y = over_y(own)
-    line = [own, from_x, from_y, over_x(from_y[:half]), over_y(from_x[half:])]
+    low, high = from_y[:half], from_x[half:]
+    if earlier:
+        low, high, *_ = lax.optimization_barrier((low, high, *earlier))
+    line = [own, from_x, from_y, over_x(low), over_y(high)]
     return line, [over_c(part) for part in line]
 
 
-def scatter_plane(kept, sent, rows):
+def scatter_plane(kept, sent, rows, first=None, second=None):
     half = rows // 2
     came = over_c(sent)
 
     def joined(low, high):
         return kept[low:high].astype(f32) + came[low:high].astype(f32)
 
-    low = over_x(joined(3 * rows, 3 * rows + half).astype(bf16))
-    high = over_y(joined(3 * rows + half, 4 * rows).astype(bf16))
+    far_low = joined(3 * rows, 3 * rows + half).astype(bf16)
+    far_high = joined(3 * rows + half, 4 * rows).astype(bf16)
+    done = []
+    if first is not None:
+        done.append(first(far_low, far_high))
+    low, high = over_x(far_low), over_y(far_high)
+    if done:
+        low, high, _ = lax.optimization_barrier((low, high, done[0]))
     near_x = jnp.concatenate(
         [joined(rows, rows + half), joined(rows + half, 2 * rows) + high.astype(f32)], axis=0
-    )
+    ).astype(bf16)
     near_y = jnp.concatenate(
         [joined(2 * rows, 2 * rows + half) + low.astype(f32), joined(2 * rows + half, 3 * rows)],
         axis=0,
-    )
-    return (
-        joined(0, rows)
-        + over_x(near_x.astype(bf16)).astype(f32)
-        + over_y(near_y.astype(bf16)).astype(f32)
-    )
-
-
-def exchange(blocks, me):
-    result = blocks
-    for mask in range(1, PARTS):
-        there = me ^ mask
-        piece = lax.dynamic_index_in_dim(blocks, there, 0, keepdims=True)
-        came = lax.ppermute(piece, PLANE, [(i, i ^ mask) for i in range(PARTS)])
-        result = lax.dynamic_update_slice_in_dim(result, came, there, 0)
-    return result
-
-
-def gather_line(own):
-    far = along_z(own, FAR)
-    return (own, along_z(own, NEAR), far, along_z(own, INNER), along_z(far, OUTWARD))
-
-
-def scatter_line(full, iz):
-    blocks = full.reshape(LINE, -1, full.shape[1])
-
-    def block(mask):
-        return lax.dynamic_index_in_dim(blocks, iz ^ mask, 0, keepdims=False)
-
-    last = block(3)
-    inward = along_z(last, INWARD)
-    inner = along_z(last, INNER)
-    near = along_z(block(1), NEAR)
-    far = along_z((block(2).astype(f32) + inward.astype(f32)).astype(bf16), FAR)
-    return block(0).astype(f32) + inner.astype(f32) + near.astype(f32) + far.astype(f32)
+    ).astype(bf16)
+    if second is not None:
+        done.append(second(near_x, near_y))
+    last_x, last_y = over_x(near_x), over_y(near_y)
+    if second is not None:
+        last_x, last_y, _ = lax.optimization_barrier((last_x, last_y, done[-1]))
+    total = joined(0, rows) + last_x.astype(f32) + last_y.astype(f32)
+    return (total, *done) if done else total
+
+
+def place_pieces(stacks, me_ref, *refs):
+    result = refs[PARTS]
+    for mask, piece in enumerate(refs[:PARTS]):
+        there = jnp.bitwise_xor(me_ref[0], mask)
+        if stacks:
+            for index in range(result.shape[0]):
+                result[index, there] = piece[index]
+        else:
+            result[there] = piece[...]
+
+
+def pieces_for(blocks, me, axis=0):
+    return [
+        lax.dynamic_index_in_dim(blocks, me ^ mask, axis, keepdims=False) for mask in range(PARTS)
+    ]
+
+
+def exchange(pieces, me, shape):
+    stacks = len(shape) == 4
+    pieces = [
+        lax.ppermute(piece, PLANE, [(i, i ^ mask) for i in range(PARTS)]) if mask else piece
+        for mask, piece in enumerate(pieces)
+    ]
+    size = 2 * pieces[0].dtype.itemsize * PARTS * pieces[0].size
+    return pl.pallas_call(
+        functools.partial(place_pieces, stacks),
+        in_specs=[pl.BlockSpec(memory_space=pltpu.SMEM)]
+        + [pl.BlockSpec(memory_space=pltpu.VMEM)] * PARTS,
+        out_specs=pl.BlockSpec(memory_space=pltpu.VMEM),
+        compiler_params=pltpu.CompilerParams(vmem_limit_bytes=16 * 1024 * 1024),
+        out_shape=jax.ShapeDtypeStruct(shape, pieces[0].dtype),
+        cost_estimate=pl.CostEstimate(flops=0, bytes_accessed=size, transcendentals=0),
+    )(me.astype(jnp.int32).reshape(1), *pieces)
 
 
 def doubled(values, axis, perm, upper):
@@ -200,35 +218,6 @@
     return copies
 
 
-def block_target(target, z, mask, size):
-    return target.at[pl.ds(pl.multiple_of(jnp.bitwise_xor(z, mask) * size, size), size)]
-
-
-def start_blocks(pieces, target, sems, z):
-    size = pieces[0].shape[0]
-    for mask in range(3):
-        pltpu.make_async_copy(
-            pieces[mask], block_target(target, z, mask, size), sems.at[mask]
-        ).start()
-    inner = jnp.logical_or(z == 1, z == 2)
-
-    @pl.when(inner)
-    def _():
-        pltpu.make_async_copy(pieces[3], block_target(target, z, 3, size), sems.at[3]).start()
-
-    @pl.when(jnp.logical_not(inner))
-    def _():
-        pltpu.make_async_copy(pieces[4], block_target(target, z, 3, size), sems.at[3]).start()
-
-
-def wait_blocks(pieces, target, sems, z):
-    size = pieces[0].shape[0]
-    for mask in range(4):
-        pltpu.make_async_copy(
-            pieces[mask], block_target(target, z, mask, size), sems.at[mask]
-        ).wait()
-
-
 def begin_lines(step, lines):
     @pl.when(step == 0)
     def _():
@@ -237,14 +226,30 @@
                 copy.start()
 
 
-def await_lines(step, lines):
-    for index in range(GROUPS):
+def await_lines(step, lines, groups=1):
+    steps = GROUPS // groups
+    for index in range(steps):
 
         @pl.when(step == index)
         def _(index=index):
             for copies in lines:
-                for copy in copies[index:] if index == GROUPS - 1 else copies[index : index + 1]:
+                last = None if index == steps - 1 else (index + 1) * groups
+                for copy in copies[index * groups : last]:
                     copy.wait()
+
+
+def keep_rows(step, steps, pairs):
+    @pl.when(step == steps - 1)
+    def _():
+        for copy in pairs:
+            copy.start()
+
+
+def await_kept(step, steps, pairs):
+    @pl.when(step == steps - 1)
+    def _():
+        for copy in pairs:
+            copy.wait()
 
 
 def row_marks(marks, group, shape, axis):
@@ -302,35 +307,21 @@
     return expo / jnp.sum(expo, axis=1, keepdims=True)
 
 
-def attend_forward(first, heads, rows, half, z_ref, marks_ref, *refs):
-    tokens, qkv_pieces, out_pieces = refs[0:5], refs[5:10], refs[10:15]
-    gain, shift, bias, cos_ref, ahead_ref, behind_ref = refs[15:21]
-    refs = refs[21 if first else 24 :]
-    normed_ref, qkv_ref, mixed_ref, part_ref = refs[:4]
-    token_rows, qkv_weight, out_weight, line_sems, qkv_sems, out_sems = refs[4:]
+def attend_forward(first, heads, rows, half, marks_ref, *refs):
+    tokens = refs[0:5]
+    qkv_weight, out_weight, gain, shift, bias, cos_ref, ahead_ref, behind_ref = refs[5:13]
+    refs = refs[13 if first else 16 :]
+    normed_ref, qkv_ref, mixed_ref, part_ref, token_rows, line_sems = refs
     step = pl.program_id(0)
     group = half * GROUPS + step
-    z = z_ref[0]
     line = line_copies(tokens, token_rows, line_sems)
     begin_lines(step, [line])
-
-    @pl.when(step == 0)
-    def _():
-        start_blocks(qkv_pieces, qkv_weight, qkv_sems, z)
-        start_blocks(out_pieces, out_weight, out_sems, z)
-
     await_lines(step, [line])
     values = token_rows[pl.ds(pl.multiple_of(step * rows, rows), rows), :].astype(f32)
     centre = values - jnp.mean(values, axis=1, keepdims=True)
     inverse = lax.rsqrt(jnp.mean(centre * centre, axis=1, keepdims=True) + eps_norm)
     normed = (centre * inverse * gain[...] + shift[...]).astype(bf16)
     normed_ref[...] = normed
-
-    @pl.when(step == 0)
-    def _():
-        wait_blocks(qkv_pieces, qkv_weight, qkv_sems, z)
-        wait_blocks(out_pieces, out_weight, out_sems, z)
-
     width = heads * HEAD
     qkv = mat(normed, qkv_weight[...]) + bias[...]
     tables = [placed_table(ref, marks_ref, group, rows) for ref in (cos_ref, ahead_ref, behind_ref)]
@@ -350,15 +341,32 @@
     part_ref[...] = mat(mixed, out_weight[...]).astype(bf16)
 
 
-def feed_both(first, rows, z_ref, *refs):
-    normed, grads = refs[0:5], refs[5:10]
-    gate_pieces, up_pieces, down_pieces = refs[10:15], refs[15:20], refs[20:25]
-    refs = refs[25 if first else 30 :]
-    normed_ref, grad_ref, hidden_ref, gate_ref, up_ref, back_ref, down_ref = refs[:7]
-    normed_rows, grad_rows, gate_weight, up_weight, down_weight = refs[7:12]
-    normed_sems, grad_sems, gate_sems, up_sems, down_sems = refs[12:]
+def feed_both(first, rows, half, *refs):
+    normed, grads, weights = refs[0:5], refs[5:10], refs[10]
+    refs = refs[11 if first else 15 :]
+    normed_ref, grad_ref, hidden_ref, both_ref, back_ref, down_ref = refs[:6]
+    normed_rows, grad_rows, gate_weight, up_weight, down_weight = refs[6:11]
+    normed_sems, grad_sems, weight_sems, keep_sems = refs[11:]
     step = pl.program_id(0)
-    z = z_ref[0]
+    groups = rows * GROUPS // normed_rows.shape[0]
+    steps = GROUPS // groups
+    place = pl.ds(half * normed_rows.shape[0], normed_rows.shape[0])
+    kept = [
+        pltpu.make_async_copy(normed_rows, normed_ref.at[place], keep_sems.at[0]),
+        pltpu.make_async_copy(grad_rows, grad_ref.at[place], keep_sems.at[1]),
+    ]
+    size = gate_weight.shape[0] // LINE
+    loads = [
+        [
+            pltpu.make_async_copy(
+                weights.at[place, index],
+                target.at[pl.ds(place * size, size)],
+                weight_sems.at[LINE * index + place],
+            )
+            for place in range(LINE)
+        ]
+        for index, target in enumerate((gate_weight, up_weight, down_weight))
+    ]
     lines = [
         line_copies(normed, normed_rows, normed_sems),
         line_copies(grads, grad_rows, grad_sems),
@@ -366,26 +374,28 @@
 
     @pl.when(step == 0)
     def _():
-        start_blocks(gate_pieces, gate_weight, gate_sems, z)
+        for copy in loads[0]:
+            copy.start()
 
     begin_lines(step, lines)
 
     @pl.when(step == 0)
     def _():
-        start_blocks(up_pieces, up_weight, up_sems, z)
-        start_blocks(down_pieces, down_weight, down_sems, z)
-        wait_blocks(gate_pieces, gate_weight, gate_sems, z)
-
-    await_lines(step, lines)
+        for copy in loads[1] + loads[2]:
+            copy.start()
+        for copy in loads[0]:
+            copy.wait()
+
+    await_lines(step, lines, groups)
+    keep_rows(step, steps, kept)
     here = pl.ds(pl.multiple_of(step * rows, rows), rows)
     values = normed_rows[here, :]
-    normed_ref[...] = values
     gate = mat(values, gate_weight[...])
 
     @pl.when(step == 0)
     def _():
-        wait_blocks(up_pieces, up_weight, up_sems, z)
-        wait_blocks(down_pieces, down_weight, down_sems, z)
+        for copy in loads[1] + loads[2]:
+            copy.wait()
 
     upward = mat(values, up_weight[...])
     sigma = jax.nn.sigmoid(gate)
@@ -393,43 +403,33 @@
     hidden = (gated * upward).astype(bf16)
     hidden_ref[...] = hidden
     grad_low = grad_rows[here, :]
-    grad_ref[...] = grad_low
     grad_hidden = mat(grad_low, down_weight[...])
     grad_gate = (grad_hidden * upward * sigma * (1.0 + gate * (1.0 - sigma))).astype(bf16)
     grad_up = (grad_hidden * gated).astype(bf16)
-    gate_ref[...] = grad_gate
-    up_ref[...] = grad_up
+    columns = hidden.shape[1]
+    both_ref[:, :columns] = grad_gate
+    both_ref[:, columns:] = grad_up
     back_ref[...] = (
         mat_cols(grad_gate, gate_weight[...]) + mat_cols(grad_up, up_weight[...])
     ).astype(bf16)
     down_ref[...] = mat_cols(hidden, down_weight[...]).astype(bf16)
-
-
-def attend_backward(first, heads, rows, half, z_ref, marks_ref, *refs):
-    branch, qkv_pieces, out_pieces = refs[0:5], refs[5:10], refs[10:15]
-    saved, cos_ref, ahead_ref, behind_ref = refs[15:19]
-    refs = refs[19 if first else 21 :]
-    branch_ref, grad_ref, part_ref = refs[:3]
-    branch_rows, qkv_weight, out_weight, line_sems, qkv_sems, out_sems = refs[3:]
+    await_kept(step, steps, kept)
+
+
+def attend_backward(first, heads, rows, half, marks_ref, *refs):
+    branch = refs[0:5]
+    saved, qkv_weight, out_weight, cos_ref, ahead_ref, behind_ref = refs[5:11]
+    refs = refs[11 if first else 13 :]
+    branch_ref, grad_ref, part_ref, branch_rows, line_sems, keep_sems = refs
     step = pl.program_id(0)
     group = half * GROUPS + step
-    z = z_ref[0]
     line = line_copies(branch, branch_rows, line_sems)
-
-    @pl.when(step == 0)
-    def _():
-        start_blocks(out_pieces, out_weight, out_sems, z)
-
+    place = pl.ds(half * GROUPS * rows, GROUPS * rows)
+    kept = [pltpu.make_async_copy(branch_rows, branch_ref.at[place], keep_sems.at[0])]
     begin_lines(step, [line])
-
-    @pl.when(step == 0)
-    def _():
-        start_blocks(qkv_pieces, qkv_weight, qkv_sems, z)
-        wait_blocks(out_pieces, out_weight, out_sems, z)
-
     await_lines(step, [line])
+    keep_rows(step, GROUPS, kept)
     values = branch_rows[pl.ds(pl.multiple_of(step * rows, rows), rows), :]
-    branch_ref[...] = values
     width = heads * HEAD
     factor = HEAD ** (-0.5)
     grad_mixed = mat_cols(values, out_weight[...]).astype(bf16)
@@ -459,39 +459,34 @@
         axis=1,
     ).astype(bf16)
     grad_ref[...] = grads
-
-    @pl.when(step == 0)
-    def _():
-        wait_blocks(qkv_pieces, qkv_weight, qkv_sems, z)
-
     part_ref[...] = mat_cols(grads, qkv_weight[...]).astype(bf16)
-
-
-def run_half(body, scalars, loose, blocked, whole, outputs, scratch, half, rows, prior, flops):
+    await_kept(step, GROUPS, kept)
+
+
+def run_half(body, scalars, loose, blocked, whole, outputs, scratch, half, rows, prior, steps=GROUPS):
     loose, blocked, whole = list(loose), list(blocked), list(whole)
     kept = list(prior or [])
     out_shape, out_specs = [], []
-    for width, shared in outputs:
-        total = 2 * GROUPS if shared else GROUPS
-        offset = half * GROUPS if shared else 0
+    for width, shared, by_copy in outputs:
+        total = 2 * steps if shared else steps
+        offset = half * steps if shared else 0
         out_shape.append(jax.ShapeDtypeStruct((total * rows, width), bf16))
-        out_specs.append(pl.BlockSpec((rows, width), lambda i, *_, offset=offset: (i + offset, 0)))
+        block = pl.BlockSpec((rows, width), lambda i, *_, offset=offset: (i + offset, 0))
+        out_specs.append(ANYWHERE if by_copy else block)
     in_specs = [ANYWHERE] * len(loose)
     for values in blocked:
+        in_specs.append(pl.BlockSpec((rows, values.shape[1]), lambda i, *_: (i + half * steps, 0)))
+    for values in whole:
         in_specs.append(
-            pl.BlockSpec((rows, values.shape[1]), lambda i, *_: (i + half * GROUPS, 0))
+            pl.BlockSpec(values.shape, lambda i, *_: (0, 0), pipeline_mode=pl.Buffered(1))
         )
-    for values in whole:
-        in_specs.append(pl.BlockSpec(values.shape, lambda i, *_: (0, 0)))
     in_specs += [ANYWHERE] * len(kept)
     before = len(scalars) + len(loose) + len(blocked) + len(whole)
-    moved = sum(values.size * values.dtype.itemsize for values in loose + blocked + whole)
-    moved += sum(width * rows * GROUPS * 2 for width, _ in outputs)
     return pl.pallas_call(
         body,
         grid_spec=pltpu.PrefetchScalarGridSpec(
             num_scalar_prefetch=len(scalars),
-            grid=(GROUPS,),
+            grid=(steps,),
             in_specs=in_specs,
             out_specs=out_specs,
             scratch_shapes=scratch,
@@ -501,7 +496,7 @@
         compiler_params=pltpu.CompilerParams(
             dimension_semantics=("arbitrary",), vmem_limit_bytes=VMEM_BYTES
         ),
-        cost_estimate=pl.CostEstimate(flops=flops, bytes_accessed=moved, transcendentals=0),
+        cost_estimate=pl.CostEstimate(flops=1, bytes_accessed=1, transcendentals=0),
     )(*scalars, *loose, *blocked, *whole, *kept)
 
 
@@ -533,7 +528,6 @@
     ix = lax.axis_index("x")
     ic = lax.axis_index("c")
     me = iy * 4 + ix * 2 + ic
-    z_scalar = iz.astype(jnp.int32).reshape(1)
 
     def spread_gather(values, axis):
         return lax.all_gather(values, "s", axis=axis, tiled=True) if spread > 1 else values
@@ -542,8 +536,6 @@
         if spread == 1:
             return values
         return lax.psum_scatter(values, "s", scatter_dimension=axis, tiled=True)
-
-    out_blocks = gather_line(spread_gather(out_weight, 0))
 
     own_marks = block_marks(seq_lengths[0], block_counts[0])
     packed = jnp.concatenate(
@@ -564,10 +556,10 @@
         .transpose(2, 0, 1, 3)
         .reshape(PARTS, share, 3 * head_cols)
     )
-    qkv_rows = spread_gather(exchange(qkv_parts, me), 1).reshape(-1, 3 * head_cols)
-    qkv_blocks = gather_line(qkv_rows)
-
-    token_lines = gather_plane(tokens)
+    qkv_rows = exchange(pieces_for(qkv_parts, me), me, qkv_parts.shape)
+    qkv_rows = spread_gather(qkv_rows, 1).reshape(-1, 3 * head_cols)
+    qkv_full = gather_line(qkv_rows)
+    out_full = gather_line(spread_gather(out_weight, 0))
 
     plane_pack = doubled(packed, "c", SWAP, ic == 1)
     plane_pack = doubled(plane_pack, "x", SWAP, ix == 1)
@@ -599,13 +591,17 @@
         [
             weight.reshape(share, PARTS, hidden_share).transpose(1, 0, 2)
             for weight in (gate_weight, up_weight, down_weight)
-        ],
-        axis=1,
-    )
-    mlp_rows = spread_gather(exchange(mlp_parts, me), 2)
-    gate_blocks, up_blocks, down_blocks = (
-        gather_line(mlp_rows[:, index].reshape(-1, hidden_share)) for index in range(3)
-    )
+        ]
+    )
+    mlp_pieces = pieces_for(mlp_parts, me, 1)
+    token_lines = gather_plane(tokens, *mlp_pieces)
+    mlp_rows = spread_gather(exchange(mlp_pieces, me, mlp_parts.shape), 2)
+    mlp_full = gather_line(mlp_rows.reshape(-1, hidden_share))
+    mlp_full = mlp_full.reshape(LINE, 3, -1, hidden_share)
+
+    valid = valid_rows(own_marks, rows)[:, None]
+    grad_top = jnp.where(valid, out_grad.astype(f32), 0.0)
+    grad_lines = gather_plane(after(grad_top.astype(bf16), token_lines[0][3], token_lines[0][4]))
 
     dma = pltpu.SemaphoreType.DMA
     line_rows = GROUPS * rows
@@ -613,65 +609,64 @@
     def attention(half, prior):
         return run_half(
             functools.partial(attend_forward, prior is None, heads, rows, half),
-            (z_scalar, marks),
-            token_lines[half] + list(qkv_blocks) + list(out_blocks),
+            (after(marks, mlp_rows, *grad_lines[0][:3]) if prior is None else marks,),
+            token_lines[half],
             (),
-            (gain_one, shift_one, bias_mine) + tables,
-            ((width, True), (3 * head_cols, True), (head_cols, True), (width, False)),
+            (qkv_full, out_full, gain_one, shift_one, bias_mine) + tables,
+            (
+                (width, True, False),
+                (3 * head_cols, True, False),
+                (head_cols, True, False),
+                (width, False, False),
+            ),
             [
                 pltpu.VMEM((line_rows, width), bf16),
-                pltpu.VMEM((width, 3 * head_cols), bf16),
-                pltpu.VMEM((head_cols, width), bf16),
                 dma((5,)),
-                dma((4,)),
-                dma((4,)),
             ],
             half,
             rows,
             prior,
-            2 * line_rows * width * 4 * head_cols,
         )
 
     *shared, out_sent = attention(1, None)
     normed_one, saved, mixed, out_kept = attention(0, shared)
+    out_sent = after(out_sent, *grad_lines[0])
     inputs = tokens.astype(f32)
     middle = inputs + scatter_plane(out_kept, out_sent, rows)
 
     standard_two, inverse_two = standardize(middle)
     normed_lines = gather_plane((standard_two * gain_two + shift_two).astype(bf16))
 
-    valid = valid_rows(own_marks, rows)[:, None]
-    grad_top = jnp.where(valid, out_grad.astype(f32), 0.0)
-    grad_lines = gather_plane(grad_top.astype(bf16))
-
     def feed(half, prior):
         return run_half(
-            functools.partial(feed_both, prior is None, rows),
-            (z_scalar,),
-            normed_lines[half]
-            + grad_lines[half]
-            + list(gate_blocks)
-            + list(up_blocks)
-            + list(down_blocks),
+            functools.partial(feed_both, prior is None, 2 * rows, half),
+            (),
+            normed_lines[half] + grad_lines[half] + [mlp_full],
             (),
             (),
-            ((width, True),) * 2 + ((hidden_share, True),) * 3 + ((width, False),) * 2,
+            ((width, True, True),) * 2
+            + ((hidden_share, True, False), (2 * hidden_share, True, False))
+            + ((width, False, False),) * 2,
             [pltpu.VMEM((line_rows, width), bf16)] * 2
             + [pltpu.VMEM((width, hidden_share), bf16)] * 3
-            + [dma((5,))] * 2
-            + [dma((4,))] * 3,
+            + [dma((5,)), dma((5,)), dma((3 * LINE,)), dma((2,))],
             half,
-            rows,
+            2 * rows,
             prior,
-            12 * line_rows * width * hidden_share,
+            GROUPS // 2,
         )
 
     *shared, back_sent, down_sent = feed(1, None)
-    normed_two, grad_low, hidden, grad_gate, grad_up, back_kept, down_kept = feed(0, shared)
-    grad_normed_two = scatter_plane(back_kept, back_sent, rows)
-    down_grad = scatter_line(mat_rows(grad_low, hidden).astype(bf16), iz)
-    gate_grad = scatter_line(mat_rows(normed_two, grad_gate).astype(bf16), iz)
-    up_grad = scatter_line(mat_rows(normed_two, grad_up).astype(bf16), iz)
+    normed_two, grad_low, hidden, grad_both, back_kept, down_kept = feed(0, shared)
+    grad_normed_two, down_part, both_part = scatter_plane(
+        back_kept,
+        back_sent,
+        rows,
+        lambda *far: mat_rows(after(grad_low, *far), hidden).astype(bf16),
+        lambda *near: mat_rows(after(normed_two, *near), grad_both).astype(bf16),
+    )
+    down_grad = scatter_line(down_part)
+    both_grad = scatter_line(both_part)
 
     grad_middle_norm, gain_two_grad, shift_two_grad = norm_back(
         grad_normed_two, standard_two, inverse_two, gain_two
@@ -679,41 +674,53 @@
     grad_middle = grad_top + grad_middle_norm
     branch_lines = gather_plane(grad_middle.astype(bf16))
 
-    down = scatter_plane(down_kept, down_sent, rows)
-    layer_out = jnp.where(valid, middle + down, 0.0).astype(bf16)
-
-    def attention_back(half, prior):
+    def attention_back(half, prior, *earlier):
         return run_half(
             functools.partial(attend_backward, prior is None, heads, rows, half),
-            (z_scalar, marks),
-            branch_lines[half] + list(qkv_blocks) + list(out_blocks),
+            (after(marks, *earlier),),
+            branch_lines[half],
             (saved,),
-            tables,
-            ((width, True), (3 * head_cols, True), (width, False)),
+            (qkv_full, out_full) + tables,
+            ((width, True, True), (3 * head_cols, True, False), (width, False, False)),
             [
                 pltpu.VMEM((line_rows, width), bf16),
-                pltpu.VMEM((width, 3 * head_cols), bf16),
-                pltpu.VMEM((head_cols, width), bf16),
                 dma((5,)),
-                dma((4,)),
-                dma((4,)),
+                dma((1,)),
             ],
             half,
             rows,
             prior,
-            2 * line_rows * width * 4 * head_cols,
         )
 
-    *shared, input_sent = attention_back(1, None)
-    grad_branch, grad_qkv, input_kept = attention_back(0, shared)
-    qkv_grad = scatter_line(mat_rows(normed_one, grad_qkv).astype(bf16), iz)
-    out_grad_weight = scatter_line(mat_rows(mixed, grad_branch).astype(bf16), iz)
+    backs = []
+
+    def back_first(*far):
+        backs.append(attention_back(1, None, down_grad, *far))
+        return backs[0][2]
+
+    def back_second(*near):
+        backs.append(attention_back(0, backs[0][:2], *near))
+        return backs[1][2]
+
+    down, input_sent, input_kept = scatter_plane(
+        down_kept, after(down_sent, grad_middle), rows, back_first, back_second
+    )
+    layer_out = jnp.where(valid, middle + down, 0.0).astype(bf16)
+    grad_branch, grad_qkv, _ = backs[1]
+    grad_normed_one, qkv_part, out_part = scatter_plane(
+        input_kept,
+        input_sent,
+        rows,
+        lambda *far: mat_rows(after(normed_one, *far), grad_qkv).astype(bf16),
+        lambda *near: mat_rows(after(mixed, *near), grad_branch).astype(bf16),
+    )
+    qkv_grad = scatter_line(qkv_part)
+    grad_normed_one = after(grad_normed_one, both_grad)
     bias_part = jnp.sum(grad_qkv.astype(f32), axis=0).reshape(3 * heads, 1, HEAD)
     bias_grad = jnp.where(
         lax.broadcasted_iota(jnp.int32, (3 * heads, PARTS, HEAD), 1) == me, bias_part, 0.0
     )
 
-    grad_normed_one = scatter_plane(input_kept, input_sent, rows)
     standard_one, inverse_one = standardize(inputs)
     grad_input_norm, gain_one_grad, shift_one_grad = norm_back(
         grad_normed_one, standard_one, inverse_one, gain_one
@@ -735,22 +742,30 @@
     small = halved(small, "c", SWAP, ic == 1)
     small = spread_scatter(small, 0)[0]
 
-    mlp_back = jnp.stack(
-        [part.reshape(PARTS, -1, hidden_share) for part in (gate_grad, up_grad, down_grad)], axis=1
-    )
-    mlp_back = exchange(spread_scatter(mlp_back, 2).astype(bf16), me)
-    gate_share, up_share, down_share = (
-        mlp_back[:, index].transpose(1, 0, 2).reshape(share, -1).astype(f32) for index in range(3)
-    )
-    qkv_back = spread_scatter(qkv_grad.reshape(PARTS, -1, 3 * head_cols), 1)
-    qkv_back = exchange(qkv_back.astype(bf16), me)
+    def back_blocks(values):
+        return spread_scatter(values.reshape(PARTS, -1, values.shape[1]), 1)
+
+    def send_back(blocks):
+        return exchange(pieces_for(blocks, me), me, blocks.shape)
+
+    def in_rows(blocks):
+        return blocks.transpose(1, 0, 2).astype(f32)
+
+    down_back = send_back(back_blocks(after(down_grad, grad_normed_one)))
+    both_back = send_back(back_blocks(after(both_grad, grad_normed_one)))
+    qkv_blocks = back_blocks(after(qkv_grad, down_back, both_back))
+    qkv_pieces = pieces_for(qkv_blocks, me)
+    down_back, both_back, *_ = lax.optimization_barrier((down_back, both_back, *qkv_pieces))
+    down_share = in_rows(down_back).reshape(share, -1)
+    both_back = in_rows(both_back)
+    gate_share = both_back[:, :, :hidden_share].reshape(share, -1)
+    up_share = both_back[:, :, hidden_share:].reshape(share, -1)
+    qkv_back = in_rows(exchange(qkv_pieces, me, qkv_blocks.shape))
+    out_grad_weight = scatter_line(after(out_part, qkv_grad))
     qkv_share = (
-        qkv_back.reshape(PARTS, share, 3 * heads, HEAD)
-        .transpose(1, 2, 0, 3)
-        .reshape(share, 3 * width)
-        .astype(f32)
-    )
-    out_share = spread_scatter(out_grad_weight, 0)
+        qkv_back.reshape(share, PARTS, 3 * heads, HEAD).transpose(0, 2, 1, 3).reshape(share, 3 * width)
+    )
+    out_share = spread_scatter(out_grad_weight, 0).astype(f32)
     return (
         layer_out,
         tokens_grad,

time: 1070 us -> 671 us (0.63)
  waiting for transfers between devices: 444 us -> 242 us
  starting transfers between devices: 214 us -> 86.5 us
  local copies, waits for them, and re-layouts: 152 us -> 70.7 us
  between operations: 3.71 us -> 16.5 us
    ppermute x68 -> x35, waiting for transfers between devices: 344 us -> 24.3 us  [exchange(): lax.ppermute(piece, PLANE, [(i, i ^ mask) for i in range(PARTS)])]
    ppermute x68 -> x35, starting transfers between devices: 132 us -> 35.6 us  [exchange(): lax.ppermute(piece, PLANE, [(i, i ^ mask) for i in range(PARTS)])]
    ppermute x16, waiting for transfers between devices: 35.4 us -> 125 us  [over_y(): return lax.ppermute(values, 'y', SWAP)]
    ppermute x12 -> x0, local copies, waits for them, and re-layouts: 27.4 us -> none  [along_z(): return lax.ppermute(values, 'z', perm)]
    ppermute x16, starting transfers between devices: 45.3 us -> 18.3 us  [over_x(): return lax.ppermute(values, 'x', SWAP)]
    dynamic_slice x11 -> x0, local copies, waits for them, and re-layouts: 23.5 us -> none  [the longest x3 22.3 us: block(): return lax.dynamic_index_in_dim(blocks, iz ^ mask, 0, keepdims=False)]
    convert_element_type x9 -> x0, local copies, waits for them, and re-layouts: 19.6 us -> none  [the longest x3 11.8 us: per_device(): qkv_share = qkv_back.reshape(PARTS, share, 3 * heads, HEAD).transpose(1,...]
    ppermute x16, waiting for transfers between devices: 41.3 us -> 55.7 us  [over_x(): return lax.ppermute(values, 'x', SWAP)]
  transfers between devices with their start and end apart: 134 -> 108, of which waited for: 53 -> 48; matrix products, arithmetic and copies ran while one was open for 21% -> 23% of each run, Pallas kernels for 4% -> 18%
where the time goes in v3:
time: 671 us; the launch traced here: 664 us
  waiting for transfers between devices  242 us (36%)
  Pallas kernels  147 us (22%)
  starting transfers between devices  86.5 us (13%)
  local copies, waits for them, and re-layouts  70.7 us (11%)
  other arithmetic  60.4 us (9%)
  matrix products  41.1 us (6%)
  between operations  16.5 us (2%)
    pallas_call x6, Pallas kernels, run_half(): pl.pallas_call(body, grid_spec=pltpu.PrefetchScalarGridSpec(num_scalar_pr...  144 us
    ppermute x16, waiting for transfers between devices, over_y(): return lax.ppermute(values, 'y', SWAP)  125 us
    ppermute x16, waiting for transfers between devices, over_x(): return lax.ppermute(values, 'x', SWAP)  55.7 us
    dot_general x4, matrix products, mat_rows(): lax.dot_general(left, right, (((0,), (0,)), ((), ())), preferred_element_...  41.1 us
    ppermute x35, starting transfers between devices, exchange(): lax.ppermute(piece, PLANE, [(i, i ^ mask) for i in range(PARTS)])  35.6 us
    ppermute x35, waiting for transfers between devices, exchange(): lax.ppermute(piece, PLANE, [(i, i ^ mask) for i in range(PARTS)])  24.3 us
    ppermute x5, waiting for transfers between devices, doubled(): other = lax.ppermute(values, axis, perm)  21.5 us
    ppermute x16, starting transfers between devices, over_x(): return lax.ppermute(values, 'x', SWAP)  18.3 us
  transfers between devices with their start and end apart: 108, of which 48 were waited for; matrix products, arithmetic and copies ran while one was open for 23% of the time, Pallas kernels for 18%

profile of v3, /device:TPU:0, one launch (start us, length us, event | category | flops | bytes accessed | tf_op | source)
XLA Modules:
  0.0 663.5 jit_solution(15267564128049906527)
XLA Ops:
  8.0 3.4 reshape.330
  43.4 11.7 %collective-permute-done.4.refs_2_ = bf16[256,2048]{1,0:T(8,128)(2,1)} collective-permute-done((bf16[256,2048]{1,0:T(8,128)(2,1)S(1)}, bf16[256,2048]{1,0:T(8,128)(2,1)}, u32[]{:S(2)}, u32[]{:S(2)}) %collective-permute-start.4) | collective-permute-done | bytes 1048608 | tf_op jit(solution)/shard_map/ppermute | solution.py:47
  61.6 18.5 %collective-permute-done.1 = bf16[2,512]{1,0:T(2,128)(2,1)S(1)} collective-permute-done((bf16[2,512]{1,0:T(2,128)(2,1)S(1)}, bf16[2,512]{1,0:T(2,128)(2,1)S(1)}, u32[]{:S(2)}, u32[]{:S(2)}) %collective-permute-start.1) | collective-permute-done | bytes 2080 | tf_op jit(solution)/shard_map/ppermute | solution.py:144
  94.0 4.1 collective-permute-done.19.refs_4_
  105.8 14.8 %collective-permute-done.24.refs_7_ = bf16[256,2048]{1,0:T(8,128)(2,1)} collective-permute-done((bf16[256,2048]{1,0:T(8,128)(2,1)}, bf16[256,2048]{1,0:T(8,128)(2,1)}, u32[]{:S(2)}, u32[]{:S(2)}) %collective-permute-start.24) | collective-permute-done | bytes 1048608 | tf_op jit(solution)/shard_map/ppermute | solution.py:47
  135.5 20.0 %shard_map.231 = (bf16[2048,2048]{1,0:T(8,128)(2,1)}, bf16[2048,768]{1,0:T(8,128)(2,1)}, bf16[2048,256]{1,0:T(8,128)(2,1)}, bf16[1024,2048]{1,0:T(8,128)(2,1)}) custom-call(s32[8,6]{1,0:T(8,128)} %copy.120.marks_ref, bf16[256,2048]{1,0:T(8,128)(2,1)} %collective-permute-done.25.refs_0_, bf16[256,2048]{1,0:T(8,128)(2,1)} %copy-done.16, ...), custom_call_target="tpu_custom_call" | custom-call | flops 1 | bytes 1 | tf_op jit(solution)/shard_map/pallas_call | solution.py:485
  156.4 19.4 %shard_map.232 = (bf16[2048,2048]{1,0:T(8,128)(2,1)}, bf16[2048,768]{1,0:T(8,128)(2,1)}, bf16[2048,256]{1,0:T(8,128)(2,1)}, bf16[1024,2048]{1,0:T(8,128)(2,1)}) custom-call(s32[8,6]{1,0:T(8,128)} %copy.124.marks_ref, bf16[256,2048]{1,0:T(8,128)(2,1)} %refs_0_.1, ...), custom_call_target="tpu_custom_call", output_to_operand_aliasing={{0}: (14, {}), {1}: (15, {}), {2}: (16, {})} | custom-call | flops 1 | bytes 1 | tf_op jit(solution)/shard_map/pallas_call | solution.py:485
  179.9 13.1 %collective-permute-done.35 = bf16[128,2048]{1,0:T(8,128)(2,1)S(1)} collective-permute-done((bf16[128,2048]{1,0:T(8,128)(2,1)S(1)}, bf16[128,2048]{1,0:T(8,128)(2,1)S(1)}, u32[]{:S(2)}, u32[]{:S(2)}) %collective-permute-start.35) | collective-permute-done | bytes 524320 | tf_op jit(solution)/shard_map/ppermute | solution.py:43
  198.1 22.1 %collective-permute-done.36 = bf16[256,2048]{1,0:T(8,128)(2,1)} collective-permute-done((bf16[256,2048]{1,0:T(8,128)(2,1)S(1)}, bf16[256,2048]{1,0:T(8,128)(2,1)}, u32[]{:S(2)}, u32[]{:S(2)}) %collective-permute-start.36) | collective-permute-done | bytes 1048608 | tf_op jit(solution)/shard_map/ppermute | solution.py:47
  228.3 19.9 %collective-permute-done.38.refs_2_ = bf16[256,2048]{1,0:T(8,128)(2,1)S(1)} collective-permute-done((bf16[256,2048]{1,0:T(8,128)(2,1)S(1)}, bf16[256,2048]{1,0:T(8,128)(2,1)S(1)}, u32[]{:S(2)}, u32[]{:S(2)}) %collective-permute-start.38) | collective-permute-done | bytes 1048608 | tf_op jit(solution)/shard_map/ppermute | solution.py:47
  253.4 10.7 %collective-permute-done.39.refs_3_ = bf16[128,2048]{1,0:T(8,128)(2,1)S(1)} collective-permute-done((bf16[128,2048]{1,0:T(8,128)(2,1)S(1)}, bf16[128,2048]{1,0:T(8,128)(2,1)S(1)}, u32[]{:S(2)}, u32[]{:S(2)}) %collective-permute-start.39) | collective-permute-done | bytes 524320 | tf_op jit(solution)/shard_map/ppermute | solution.py:43
  268.5 4.8 all-gather.8.cloned.1.call-done
  273.2 29.9 %shard_map.233 = (bf16[2048,2048]{1,0:T(8,128)(2,1)}, bf16[2048,2048]{1,0:T(8,128)(2,1)}, bf16[2048,704]{1,0:T(8,128)(2,1)}, bf16[2048,1408]{1,0:T(8,128)(2,1)},...) custom-call(bf16[256,2048]{1,0:T(8,128)(2,1)} %copy-done.20, bf16[256,2048]{1,0:T(8,128)(2,1)} %copy-done.22, ...), custom_call_target="tpu_custom_call" | custom-call | flops 1 | bytes 1 | tf_op jit(solution)/shard_map/pallas_call | solution.py:485
  303.3 29.9 %shard_map.234 = (bf16[2048,2048]{1,0:T(8,128)(2,1)}, bf16[2048,2048]{1,0:T(8,128)(2,1)}, bf16[2048,704]{1,0:T(8,128)(2,1)}, bf16[2048,1408]{1,0:T(8,128)(2,1)},...) custom-call(bf16[256,2048]{1,0:T(8,128)(2,1)} %copy-done.11, ...), custom_call_target="tpu_custom_call", output_to_operand_aliasing={{0}: (11, {}), {1}: (12, {}), {2}: (13, {}), {3}: (14, {})} | custom-call | flops 1 | bytes 1 | tf_op jit(solution)/shard_map/pallas_call | solution.py:485
  338.2 10.0 %convolution_convert_fusion.2 = bf16[2048,704]{0,1:T(8,128)(2,1)} fusion(bf16[2048,2048]{1,0:T(8,128)(2,1)} %get-tuple-element.88, bf16[2048,704]{1,0:T(8,128)(2,1)S(1)} %copy-done.12), kind=kOutput, calls=%fused_computation.3 | convolution fusion | flops 5907021824 | bytes 14155776 | tf_op jit(solution)/shard_map/dot_general | solution.py:31
  351.6 11.6 %collective-permute-done.53 = bf16[128,2048]{1,0:T(8,128)(2,1)S(1)} collective-permute-done((bf16[128,2048]{1,0:T(8,128)(2,1)}, bf16[128,2048]{1,0:T(8,128)(2,1)S(1)}, u32[]{:S(2)}, u32[]{:S(2)}) %collective-permute-start.53) | collective-permute-done | bytes 524320 | tf_op jit(solution)/shard_map/ppermute | solution.py:47
  372.0 17.3 %convolution_convert_fusion = bf16[2048,1408]{1,0:T(8,128)(2,1)} fusion(bf16[2048,2048]{1,0:T(8,128)(2,1)S(1)} %copy-done.3, bf16[2048,1408]{1,0:T(8,128)(2,1)} %get-tuple-element.94), kind=kOutput, calls=%fused_computation | convolution fusion | flops 11814043648 | bytes 19922944 | tf_op jit(solution)/shard_map/dot_general | solution.py:31
  389.3 4.3 collective-permute-done.54
  395.9 3.5 multiply_reduce_fusion
  404.0 24.4 %collective-permute-done.62.refs_2_ = bf16[256,2048]{1,0:T(8,128)(2,1)} collective-permute-done((bf16[256,2048]{1,0:T(8,128)(2,1)}, bf16[256,2048]{1,0:T(8,128)(2,1)}, u32[]{:S(2)}, u32[]{:S(2)}) %collective-permute-start.62) | collective-permute-done | bytes 1048608 | tf_op jit(solution)/shard_map/ppermute | solution.py:47
  432.4 10.8 %collective-permute-done.64.refs_3_ = bf16[128,2048]{1,0:T(8,128)(2,1)} collective-permute-done((bf16[128,2048]{1,0:T(8,128)(2,1)S(1)}, bf16[128,2048]{1,0:T(8,128)(2,1)}, u32[]{:S(2)}, u32[]{:S(2)}) %collective-permute-start.64) | collective-permute-done | bytes 524320 | tf_op jit(solution)/shard_map/ppermute | solution.py:43
  451.0 23.3 %shard_map.235 = (bf16[2048,2048]{1,0:T(8,128)(2,1)}, bf16[2048,768]{1,0:T(8,128)(2,1)}, bf16[1024,2048]{1,0:T(8,128)(2,1)}) custom-call(s32[8,6]{1,0:T(8,128)} %copy.128.marks_ref, bf16[256,2048]{1,0:T(8,128)(2,1)} %collective-permute-done.59.refs_0_, bf16[256,2048]{1,0:T(8,128)(2,1)} %collective-permute-done.61.refs_1_, ...), custom_call_target="tpu_custom_call" | custom-call | flops 1 | bytes 1 | tf_op jit(solution)/shard_map/pallas_call | solution.py:485
  477.0 12.0 %collective-permute-done.58 = bf16[128,2048]{1,0:T(8,128)(2,1)S(1)} collective-permute-done((bf16[128,2048]{1,0:T(8,128)(2,1)}, bf16[128,2048]{1,0:T(8,128)(2,1)S(1)}, u32[]{:S(2)}, u32[]{:S(2)}) %collective-permute-start.58) | collective-permute-done | bytes 524320 | tf_op jit(solution)/shard_map/ppermute | solution.py:47
  497.5 21.6 %shard_map.236 = (bf16[2048,2048]{1,0:T(8,128)(2,1)}, bf16[2048,768]{1,0:T(8,128)(2,1)}, bf16[1024,2048]{1,0:T(8,128)(2,1)}) custom-call(s32[8,6]{1,0:T(8,128)} %copy.132.marks_ref, bf16[256,2048]{1,0:T(8,128)(2,1)} %get-tuple-element.134.refs_0_, bf16[256,2048]{1,0:T(8,128)(2,1)} %collective-permute-done.60.refs_1_, ...), custom_call_target="tpu_custom_call", output_to_operand_aliasing={{0}: (12, {}), {1}: (13, {})} | custom-call | flops 1 | bytes 1 | tf_op jit(solution)/shard_map/pallas_call | solution.py:485
  526.2 10.5 %convolution_convert_fusion.1 = bf16[2048,768]{1,0:T(8,128)(2,1)} fusion(bf16[2048,2048]{1,0:T(8,128)(2,1)} %get-tuple-element.110, bf16[2048,768]{1,0:T(8,128)(2,1)S(1)} %copy-done.2), kind=kOutput, calls=%fused_computation.2 | convolution fusion | flops 6444023808 | bytes 14680064 | tf_op jit(solution)/shard_map/dot_general | solution.py:31
  537.9 3.7 add_convert_fusion.2
  545.6 4.1 select_convert_fusion
  553.0 12.4 %collective-permute-done.73 = bf16[256,2048]{1,0:T(8,128)(2,1)} collective-permute-done((bf16[256,2048]{1,0:T(8,128)(2,1)}, bf16[256,2048]{1,0:T(8,128)(2,1)}, u32[]{:S(2)}, u32[]{:S(2)}) %collective-permute-start.73) | collective-permute-done | bytes 1048608 | tf_op jit(solution)/shard_map/ppermute | solution.py:43
  572.5 6.3 collective-permute-done.96
  616.2 3.8 collective-permute-done.85.refs_4_
  634.1 3.5 copy.139
  648.9 3.7 copy.138
  (455 shorter events, 238.1 us)
Async XLA Ops:
  7.2 127.0 %all-gather.6.cloned.1.call-start = ((), (), s32[]{:S(2)}) async-start(), calls=%async_computation.5 | async-start | bytes 1310720 | tf_op jit(solution)/shard_map/all_gather | solution.py:55
  7.9 126.3 %all-gather.4.cloned.1.call-start = ((), (), s32[]{:S(2)}) async-start(), calls=%async_computation.4 | async-start | bytes 3932160 | tf_op jit(solution)/shard_map/all_gather | solution.py:55
  29.6 243.7 %all-gather.8.cloned.1.call-start = ((), (), s32[]{:S(2)}) async-start(), calls=%async_computation.6 | async-start | bytes 11796480 | tf_op jit(solution)/shard_map/all_gather | solution.py:55
  29.6 25.4 %collective-permute-start.4 = (bf16[256,2048]{1,0:T(8,128)(2,1)S(1)}, bf16[256,2048]{1,0:T(8,128)(2,1)}, u32[]{:S(2)}, u32[]{:S(2)}) collective-permute-start(bf16[256,2048]{1,0:T(8,128)(2,1)S(1)} %copy-done), channel_id=1, source_target_pairs={{0,4},{4,0},{1,5},{5,1},{2,6},{6,2},{3,7},{7,3},{8,12},{12,8},{9,1... | collective-permute-start | bytes 3145736 | tf_op jit(solution)/shard_map/ppermute | solution.py:47
  31.1 26.1 %collective-permute-start.3 = (bf16[256,2048]{1,0:T(8,128)(2,1)S(1)}, bf16[256,2048]{1,0:T(8,128)(2,1)}, u32[]{:S(2)}, u32[]{:S(2)}) collective-permute-start(bf16[256,2048]{1,0:T(8,128)(2,1)S(1)} %copy-done), channel_id=1, source_target_pairs={{0,2},{2,0},{1,3},{3,1},{4,6},{6,4},{5,7},{7,5},{8,10},{10,8},{9,1... | collective-permute-start | bytes 3145736 | tf_op jit(solution)/shard_map/ppermute | solution.py:43
  33.5 27.5 %collective-permute-start = (bf16[1,512]{1,0:T(2,128)(2,1)S(1)}, bf16[1,512]{1,0:T(2,128)(2,1)S(1)}, u32[]{:S(2)}, u32[]{:S(2)}) collective-permute-start(bf16[1,512]{1,0:T(2,128)(2,1)S(1)} %broadcast_in_dim.120), channel_id=1, source_target_pairs={{0,1},{1,0},{2,3},{3,2},{4,5},{5,4},{6,7},{7,6},{8,9},{9,8},{10,11... | collective-permute-start | bytes 3080 | tf_op jit(solution)/shard_map/ppermute | solution.py:144
  38.8 45.0 %collective-permute-start.22 = (bf16[3,64,704]{2,1,0:T(8,128)(2,1)S(1)}, bf16[3,64,704]{2,1,0:T(8,128)(2,1)S(1)}, u32[]{:S(2)}, u32[]{:S(2)}) collective-permute-start(bf16[3,64,704]{2,1,0:T(8,128)(2,1)S(1)} %get-tuple-element.165), channel_id=1, source_target_pairs={{0,7},{1,6},{2,5},{3,4},{4,3},{5,2},{6,1},{7,0},{8,15},{9,14},{10,... | collective-permute-start | bytes 811016 | tf_op jit(solution)/shard_map/ppermute | solution.py:128
  39.4 52.0 %collective-permute-start.21 = (bf16[3,64,704]{2,1,0:T(8,128)(2,1)}, bf16[3,64,704]{2,1,0:T(8,128)(2,1)S(1)}, u32[]{:S(2)}, u32[]{:S(2)}) collective-permute-start(bf16[3,64,704]{2,1,0:T(8,128)(2,1)} %get-tuple-element.166), channel_id=1, source_target_pairs={{0,6},{1,7},{2,4},{3,5},{4,2},{5,3},{6,0},{7,1},{8,14},{9,15},{10,... | collective-permute-start | bytes 811016 | tf_op jit(solution)/shard_map/ppermute | solution.py:128
  58.3 26.1 %collective-permute-start.5 = (bf16[128,2048]{1,0:T(8,128)(2,1)}, bf16[128,2048]{1,0:T(8,128)(2,1)}, u32[]{:S(2)}, u32[]{:S(2)}) collective-permute-start(bf16[128,2048]{1,0:T(8,128)(2,1)} %slice.377), channel_id=1, source_target_pairs={{0,2},{2,0},{1,3},{3,1},{4,6},{6,4},{5,7},{7,5},{8,10},{10,8},{9,1... | collective-permute-start | bytes 1572872 | tf_op jit(solution)/shard_map/ppermute | solution.py:43
  59.9 26.9 %collective-permute-start.6 = (bf16[128,2048]{1,0:T(8,128)(2,1)S(1)}, bf16[128,2048]{1,0:T(8,128)(2,1)}, u32[]{:S(2)}, u32[]{:S(2)}) collective-permute-start(bf16[128,2048]{1,0:T(8,128)(2,1)S(1)} %slice.378), channel_id=1, source_target_pairs={{0,4},{4,0},{1,5},{5,1},{2,6},{6,2},{3,7},{7,3},{8,12},{12,8},{9,1... | collective-permute-start | bytes 1572872 | tf_op jit(solution)/shard_map/ppermute | solution.py:47
  93.3 27.3 %collective-permute-start.24 = (bf16[256,2048]{1,0:T(8,128)(2,1)}, bf16[256,2048]{1,0:T(8,128)(2,1)}, u32[]{:S(2)}, u32[]{:S(2)}) collective-permute-start(bf16[256,2048]{1,0:T(8,128)(2,1)} %fusion.12.refs_5_), channel_id=1, source_target_pairs={{0,4},{4,0},{1,5},{5,1},{2,6},{6,2},{3,7},{7,3},{8,12},{12,8},{9,1... | collective-permute-start | bytes 3145736 | tf_op jit(solution)/shard_map/ppermute | solution.py:47
  98.0 30.1 %collective-permute-start.25 = (bf16[256,2048]{1,0:T(8,128)(2,1)S(1)}, bf16[256,2048]{1,0:T(8,128)(2,1)}, u32[]{:S(2)}, u32[]{:S(2)}) collective-permute-start(bf16[256,2048]{1,0:T(8,128)(2,1)S(1)} %copy-done), channel_id=1, source_target_pairs={{0,1},{1,0},{2,3},{3,2},{4,5},{5,4},{6,7},{7,6},{8,9},{9,8},{10,11... | collective-permute-start | bytes 3145736 | tf_op jit(solution)/shard_map/ppermute | solution.py:51
  99.8 29.8 %collective-permute-start.27 = (bf16[256,2048]{1,0:T(8,128)(2,1)}, bf16[256,2048]{1,0:T(8,128)(2,1)}, u32[]{:S(2)}, u32[]{:S(2)}) collective-permute-start(bf16[256,2048]{1,0:T(8,128)(2,1)} %collective-permute-done.4.refs_2_), channel_id=1, source_target_pairs={{0,1},{1,0},{2,3},{3,2},{4,5},{5,4},{6,7},{7,6},{8,9},{9,8},{10,11... | collective-permute-start | bytes 3145736 | tf_op jit(solution)/shard_map/ppermute | solution.py:51
  100.9 24.9 %collective-permute-start.23 = (bf16[256,2048]{1,0:T(8,128)(2,1)}, bf16[256,2048]{1,0:T(8,128)(2,1)}, u32[]{:S(2)}, u32[]{:S(2)}) collective-permute-start(bf16[256,2048]{1,0:T(8,128)(2,1)} %fusion.12.refs_5_), channel_id=1, source_target_pairs={{0,2},{2,0},{1,3},{3,1},{4,6},{6,4},{5,7},{7,5},{8,10},{10,8},{9,1... | collective-permute-start | bytes 3145736 | tf_op jit(solution)/shard_map/ppermute | solution.py:43
  105.1 345.2 %reduce-scatter.5.cloned.1.call-start = ((), (), s32[]{:S(2)}) async-start(), calls=%async_computation.7 | async-start | bytes 3604480 | tf_op jit(solution)/shard_map/reduce_scatter | solution.py:59
  105.5 28.6 %collective-permute-start.26 = (bf16[256,2048]{1,0:T(8,128)(2,1)}, bf16[256,2048]{1,0:T(8,128)(2,1)S(1)}, u32[]{:S(2)}, u32[]{:S(2)}) collective-permute-start(bf16[256,2048]{1,0:T(8,128)(2,1)} %collective-permute-done.3.refs_1_), channel_id=1, source_target_pairs={{0,1},{1,0},{2,3},{3,2},{4,5},{5,4},{6,7},{7,6},{8,9},{9,8},{10,11... | collective-permute-start | bytes 3145736 | tf_op jit(solution)/shard_map/ppermute | solution.py:51
  128.1 27.3 %collective-permute-start.30 = (bf16[128,2048]{1,0:T(8,128)(2,1)}, bf16[128,2048]{1,0:T(8,128)(2,1)S(1)}, u32[]{:S(2)}, u32[]{:S(2)}) collective-permute-start(bf16[128,2048]{1,0:T(8,128)(2,1)} %slice.382), channel_id=1, source_target_pairs={{0,2},{2,0},{1,3},{3,1},{4,6},{6,4},{5,7},{7,5},{8,10},{10,8},{9,1... | collective-permute-start | bytes 1572872 | tf_op jit(solution)/shard_map/ppermute | solution.py:43
  129.6 25.8 %collective-permute-start.31 = (bf16[128,2048]{1,0:T(8,128)(2,1)}, bf16[128,2048]{1,0:T(8,128)(2,1)S(1)}, u32[]{:S(2)}, u32[]{:S(2)}) collective-permute-start(bf16[128,2048]{1,0:T(8,128)(2,1)} %slice.383), channel_id=1, source_target_pairs={{0,4},{4,0},{1,5},{5,1},{2,6},{6,2},{3,7},{7,3},{8,12},{12,8},{9,1... | collective-permute-start | bytes 1572872 | tf_op jit(solution)/shard_map/ppermute | solution.py:47
  195.4 24.8 %collective-permute-start.36 = (bf16[256,2048]{1,0:T(8,128)(2,1)S(1)}, bf16[256,2048]{1,0:T(8,128)(2,1)}, u32[]{:S(2)}, u32[]{:S(2)}) collective-permute-start(bf16[256,2048]{1,0:T(8,128)(2,1)S(1)} %pad_maximum_fusion.2), channel_id=1, source_target_pairs={{0,4},{4,0},{1,5},{5,1},{2,6},{6,2},{3,7},{7,3},{8,12},{12,8},{9,1... | collective-permute-start | bytes 3145736 | tf_op jit(solution)/shard_map/ppermute | solution.py:47
  196.2 24.3 %collective-permute-start.34 = (bf16[256,2048]{1,0:T(8,128)(2,1)S(1)}, bf16[256,2048]{1,0:T(8,128)(2,1)}, u32[]{:S(2)}, u32[]{:S(2)}) collective-permute-start(bf16[256,2048]{1,0:T(8,128)(2,1)S(1)} %pad_maximum_fusion.1), channel_id=1, source_target_pairs={{0,2},{2,0},{1,3},{3,1},{4,6},{6,4},{5,7},{7,5},{8,10},{10,8},{9,1... | collective-permute-start | bytes 3145736 | tf_op jit(solution)/shard_map/ppermute | solution.py:43
  303.2 30.0 %collective-permute-start.51 = (bf16[1024,2048]{1,0:T(8,128)(2,1)}, bf16[1024,2048]{1,0:T(8,128)(2,1)S(1)}, u32[]{:S(2)}, u32[]{:S(2)}) collective-permute-start(bf16[1024,2048]{1,0:T(8,128)(2,1)} %get-tuple-element.86), channel_id=1, source_target_pairs={{0,1},{1,0},{2,3},{3,2},{4,5},{5,4},{6,7},{7,6},{8,9},{9,8},{10,11... | collective-permute-start | bytes 12582920 | tf_op jit(solution)/shard_map/ppermute | solution.py:51
  348.2 221.9 %reduce-scatter.7.cloned.1.call-start = ((), (), s32[]{:S(2)}) async-start(), calls=%async_computation.8 | async-start | bytes 7208960 | tf_op jit(solution)/shard_map/reduce_scatter | solution.py:59
  368.8 24.8 %collective-permute-start.54 = (bf16[256,2048]{1,0:T(8,128)(2,1)}, bf16[256,2048]{1,0:T(8,128)(2,1)}, u32[]{:S(2)}, u32[]{:S(2)}) collective-permute-start(bf16[256,2048]{1,0:T(8,128)(2,1)} %pad_maximum_fusion.3), channel_id=1, source_target_pairs={{0,2},{2,0},{1,3},{3,1},{4,6},{6,4},{5,7},{7,5},{8,10},{10,8},{9,1... | collective-permute-start | bytes 3145736 | tf_op jit(solution)/shard_map/ppermute | solution.py:43
  371.3 24.6 %collective-permute-start.55 = (bf16[256,2048]{1,0:T(8,128)(2,1)}, bf16[256,2048]{1,0:T(8,128)(2,1)}, u32[]{:S(2)}, u32[]{:S(2)}) collective-permute-start(bf16[256,2048]{1,0:T(8,128)(2,1)} %pad_maximum_fusion.4), channel_id=1, source_target_pairs={{0,4},{4,0},{1,5},{5,1},{2,6},{6,2},{3,7},{7,3},{8,12},{12,8},{9,1... | collective-permute-start | bytes 3145736 | tf_op jit(solution)/shard_map/ppermute | solution.py:47
  389.3 207.2 %reduce-scatter.9.cloned.1.call-start = ((), (), s32[]{:S(2)}) async-start(), calls=%async_computation.9 | async-start | bytes 3932160 | tf_op jit(solution)/shard_map/reduce_scatter | solution.py:59
  402.5 43.2 %collective-permute-start.56 = (bf16[1024,2048]{1,0:T(8,128)(2,1)S(1)}, bf16[1024,2048]{1,0:T(8,128)(2,1)S(1)}, u32[]{:S(2)}, u32[]{:S(2)}) collective-permute-start(bf16[1024,2048]{1,0:T(8,128)(2,1)S(1)} %copy-done.44), channel_id=1, source_target_pairs={{0,1},{1,0},{2,3},{3,2},{4,5},{5,4},{6,7},{7,6},{8,9},{9,8},{10,11... | collective-permute-start | bytes 12582920 | tf_op jit(solution)/shard_map/ppermute | solution.py:51
  402.5 25.9 %collective-permute-start.62 = (bf16[256,2048]{1,0:T(8,128)(2,1)}, bf16[256,2048]{1,0:T(8,128)(2,1)}, u32[]{:S(2)}, u32[]{:S(2)}) collective-permute-start(bf16[256,2048]{1,0:T(8,128)(2,1)} %get-tuple-element.134.refs_0_), channel_id=1, source_target_pairs={{0,4},{4,0},{1,5},{5,1},{2,6},{6,2},{3,7},{7,3},{8,12},{12,8},{9,1... | collective-permute-start | bytes 3145736 | tf_op jit(solution)/shard_map/ppermute | solution.py:47
  403.2 27.0 %collective-permute-start.60 = (bf16[256,2048]{1,0:T(8,128)(2,1)}, bf16[256,2048]{1,0:T(8,128)(2,1)}, u32[]{:S(2)}, u32[]{:S(2)}) collective-permute-start(bf16[256,2048]{1,0:T(8,128)(2,1)} %get-tuple-element.134.refs_0_), channel_id=1, source_target_pairs={{0,2},{2,0},{1,3},{3,1},{4,6},{6,4},{5,7},{7,5},{8,10},{10,8},{9,1... | collective-permute-start | bytes 3145736 | tf_op jit(solution)/shard_map/ppermute | solution.py:43
  474.3 47.5 %collective-permute-start.70 = (bf16[1024,2048]{1,0:T(8,128)(2,1)}, bf16[1024,2048]{1,0:T(8,128)(2,1)}, u32[]{:S(2)}, u32[]{:S(2)}) collective-permute-start(bf16[1024,2048]{1,0:T(8,128)(2,1)} %get-tuple-element.100), channel_id=1, source_target_pairs={{0,1},{1,0},{2,3},{3,2},{4,5},{5,4},{6,7},{7,6},{8,9},{9,8},{10,11... | collective-permute-start | bytes 12582920 | tf_op jit(solution)/shard_map/ppermute | solution.py:51
  493.0 28.8 %collective-permute-start.68 = (bf16[256,2048]{1,0:T(8,128)(2,1)}, bf16[256,2048]{1,0:T(8,128)(2,1)}, u32[]{:S(2)}, u32[]{:S(2)}) collective-permute-start(bf16[256,2048]{1,0:T(8,128)(2,1)} %pad_maximum_fusion.5), channel_id=1, source_target_pairs={{0,2},{2,0},{1,3},{3,1},{4,6},{6,4},{5,7},{7,5},{8,10},{10,8},{9,1... | collective-permute-start | bytes 3145736 | tf_op jit(solution)/shard_map/ppermute | solution.py:43
  495.3 26.5 %collective-permute-start.69 = (bf16[256,2048]{1,0:T(8,128)(2,1)}, bf16[256,2048]{1,0:T(8,128)(2,1)}, u32[]{:S(2)}, u32[]{:S(2)}) collective-permute-start(bf16[256,2048]{1,0:T(8,128)(2,1)} %pad_maximum_fusion.6), channel_id=1, source_target_pairs={{0,4},{4,0},{1,5},{5,1},{2,6},{6,2},{3,7},{7,3},{8,12},{12,8},{9,1... | collective-permute-start | bytes 3145736 | tf_op jit(solution)/shard_map/ppermute | solution.py:47
  536.7 117.7 %reduce-scatter.11.cloned.1.call-start = ((), (), s32[]{:S(2)}) async-start(), calls=%async_computation.10 | async-start | bytes 1310720 | tf_op jit(solution)/shard_map/reduce_scatter | solution.py:59
  (124 other events, 1429.3 us)
Sparse Core Ops, SparseCore 0:
  9.6 30.6 all-gather.5
  42.4 63.0 all-gather.3
  107.1 166.1 all-gather.7
  348.3 54.3 reduce-scatter.4
  404.9 102.0 reduce-scatter.6
  536.8 59.5 reduce-scatter.8
  598.7 27.1 reduce-scatter.10

commit v4 on v3

--- a/solution.py
+++ b/solution.py
@@ -105,39 +105,71 @@
     return (total, *done) if done else total
 
 
-def place_pieces(stacks, me_ref, *refs):
+def place_pieces(me_ref, *refs):
     result = refs[PARTS]
     for mask, piece in enumerate(refs[:PARTS]):
         there = jnp.bitwise_xor(me_ref[0], mask)
-        if stacks:
+        if len(result.shape) == 4:
             for index in range(result.shape[0]):
                 result[index, there] = piece[index]
         else:
             result[there] = piece[...]
 
 
+def place_columns(chunks, me_ref, *refs):
+    results, held = refs[PARTS:-1], refs[-1]
+    for mask, piece in enumerate(refs[:PARTS]):
+        held[jnp.bitwise_xor(me_ref[0], mask)] = piece[...]
+    offset = 0
+    for result in results:
+        size = result.shape[1] // (PARTS * chunks)
+        for chunk in range(chunks):
+            parts = [held[member, :, offset : offset + size] for member in range(PARTS)]
+            joined = jnp.concatenate(parts, axis=1).astype(f32)
+            result[:, chunk * PARTS * size : (chunk + 1) * PARTS * size] = joined
+            offset += size
+
+
 def pieces_for(blocks, me, axis=0):
     return [
         lax.dynamic_index_in_dim(blocks, me ^ mask, axis, keepdims=False) for mask in range(PARTS)
     ]
 
 
-def exchange(pieces, me, shape):
-    stacks = len(shape) == 4
-    pieces = [
+def send_pieces(pieces):
+    return [
         lax.ppermute(piece, PLANE, [(i, i ^ mask) for i in range(PARTS)]) if mask else piece
         for mask, piece in enumerate(pieces)
     ]
-    size = 2 * pieces[0].dtype.itemsize * PARTS * pieces[0].size
+
+
+def collect(body, pieces, me, shapes, scratch=()):
+    pieces = send_pieces(pieces)
+    whole = pl.BlockSpec(memory_space=pltpu.VMEM)
+    size = 3 * pieces[0].dtype.itemsize * PARTS * pieces[0].size
     return pl.pallas_call(
-        functools.partial(place_pieces, stacks),
-        in_specs=[pl.BlockSpec(memory_space=pltpu.SMEM)]
-        + [pl.BlockSpec(memory_space=pltpu.VMEM)] * PARTS,
-        out_specs=pl.BlockSpec(memory_space=pltpu.VMEM),
-        compiler_params=pltpu.CompilerParams(vmem_limit_bytes=16 * 1024 * 1024),
-        out_shape=jax.ShapeDtypeStruct(shape, pieces[0].dtype),
+        body,
+        in_specs=[pl.BlockSpec(memory_space=pltpu.SMEM)] + [whole] * PARTS,
+        out_specs=[whole] * len(shapes),
+        scratch_shapes=scratch,
+        compiler_params=pltpu.CompilerParams(vmem_limit_bytes=24 * 1024 * 1024),
+        out_shape=shapes,
         cost_estimate=pl.CostEstimate(flops=0, bytes_accessed=size, transcendentals=0),
     )(me.astype(jnp.int32).reshape(1), *pieces)
+
+
+def exchange(pieces, me, shape):
+    return collect(place_pieces, pieces, me, [jax.ShapeDtypeStruct(shape, pieces[0].dtype)])[0]
+
+
+def exchange_columns(pieces, me, shapes, chunks=1):
+    return collect(
+        functools.partial(place_columns, chunks),
+        pieces,
+        me,
+        [jax.ShapeDtypeStruct(shape, f32) for shape in shapes],
+        [pltpu.VMEM((PARTS,) + pieces[0].shape, pieces[0].dtype)],
+    )
 
 
 def doubled(values, axis, perm, upper):
@@ -692,21 +724,8 @@
             prior,
         )
 
-    backs = []
-
-    def back_first(*far):
-        backs.append(attention_back(1, None, down_grad, *far))
-        return backs[0][2]
-
-    def back_second(*near):
-        backs.append(attention_back(0, backs[0][:2], *near))
-        return backs[1][2]
-
-    down, input_sent, input_kept = scatter_plane(
-        down_kept, after(down_sent, grad_middle), rows, back_first, back_second
-    )
-    layer_out = jnp.where(valid, middle + down, 0.0).astype(bf16)
-    grad_branch, grad_qkv, _ = backs[1]
+    *shared, input_sent = attention_back(1, None, down_grad)
+    grad_branch, grad_qkv, input_kept = attention_back(0, shared)
     grad_normed_one, qkv_part, out_part = scatter_plane(
         input_kept,
         input_sent,
@@ -716,6 +735,8 @@
     )
     qkv_grad = scatter_line(qkv_part)
     grad_normed_one = after(grad_normed_one, both_grad)
+    down = scatter_plane(down_kept, after(down_sent, input_sent), rows)
+    layer_out = jnp.where(valid, middle + down, 0.0).astype(bf16)
     bias_part = jnp.sum(grad_qkv.astype(f32), axis=0).reshape(3 * heads, 1, HEAD)
     bias_grad = jnp.where(
         lax.broadcasted_iota(jnp.int32, (3 * heads, PARTS, HEAD), 1) == me, bias_part, 0.0
@@ -745,26 +766,15 @@
     def back_blocks(values):
         return spread_scatter(values.reshape(PARTS, -1, values.shape[1]), 1)
 
-    def send_back(blocks):
-        return exchange(pieces_for(blocks, me), me, blocks.shape)
-
-    def in_rows(blocks):
-        return blocks.transpose(1, 0, 2).astype(f32)
-
-    down_back = send_back(back_blocks(after(down_grad, grad_normed_one)))
-    both_back = send_back(back_blocks(after(both_grad, grad_normed_one)))
-    qkv_blocks = back_blocks(after(qkv_grad, down_back, both_back))
-    qkv_pieces = pieces_for(qkv_blocks, me)
-    down_back, both_back, *_ = lax.optimization_barrier((down_back, both_back, *qkv_pieces))
-    down_share = in_rows(down_back).reshape(share, -1)
-    both_back = in_rows(both_back)
-    gate_share = both_back[:, :, :hidden_share].reshape(share, -1)
-    up_share = both_back[:, :, hidden_share:].reshape(share, -1)
-    qkv_back = in_rows(exchange(qkv_pieces, me, qkv_blocks.shape))
+    columns = PARTS * hidden_share
+    mlp_blocks = (back_blocks(after(down_grad, grad_normed_one)), back_blocks(both_grad))
+    mlp_pieces = [
+        jnp.concatenate(parts, axis=1) for parts in zip(*(pieces_for(b, me) for b in mlp_blocks))
+    ]
+    down_share, gate_share, up_share = exchange_columns(mlp_pieces, me, [(share, columns)] * 3)
+    qkv_pieces = pieces_for(back_blocks(after(qkv_grad, *mlp_pieces)), me)
+    (qkv_share,) = exchange_columns(qkv_pieces, me, [(share, 3 * width)], 3 * heads)
     out_grad_weight = scatter_line(after(out_part, qkv_grad))
-    qkv_share = (
-        qkv_back.reshape(share, PARTS, 3 * heads, HEAD).transpose(0, 2, 1, 3).reshape(share, 3 * width)
-    )
     out_share = spread_scatter(out_grad_weight, 0).astype(f32)
     return (
         layer_out,

time: 671 us -> 657 us (0.979)
  local copies, waits for them, and re-layouts: 70.7 us -> 40.3 us
  waiting for transfers between devices: 242 us -> 256 us
  starting transfers between devices: 86.5 us -> 78.9 us
    reshape x8 -> x0, local copies, waits for them, and re-layouts: 19.7 us -> none  [the longest x4 9.01 us: per_device(): qkv_back.reshape(share, PARTS, 3 * heads, HEAD).transpose(0, 2, 1, 3)]
    ppermute x16, waiting for transfers between devices: 125 us -> 135 us  [over_y(): return lax.ppermute(values, 'y', SWAP)]
    ppermute x35 -> x28, waiting for transfers between devices: 24.3 us -> 31.6 us  [send_pieces(): lax.ppermute(piece, PLANE, [(i, i ^ mask) for i in range(PARTS)])]
    slice x3 -> x0, local copies, waits for them, and re-layouts: 7.22 us -> none  [the longest x2 3.74 us: per_device(): up_share = both_back[:, :, hidden_share:].reshape(share, -1)]
    ppermute x35 -> x28, starting transfers between devices: 35.6 us -> 28.7 us  [send_pieces(): lax.ppermute(piece, PLANE, [(i, i ^ mask) for i in range(PARTS)])]
    another operation x5 -> x6, other arithmetic: 14.5 us -> 19 us
  transfers between devices with their start and end apart: 108 -> 101, of which waited for: 48 -> 42; matrix products, arithmetic and copies ran while one was open for 23% -> 20% of each run, Pallas kernels for 18% -> 18%
where the time goes in v4:
time: 657 us; the launch traced here: 649 us
  waiting for transfers between devices  256 us (39%)
  Pallas kernels  150 us (23%)
  starting transfers between devices  78.9 us (12%)
  other arithmetic  66.2 us (10%)
  matrix products  41.3 us (6%)
  local copies, waits for them, and re-layouts  40.3 us (6%)
  between operations  16.1 us (2%)
    pallas_call x6, Pallas kernels, run_half(): pl.pallas_call(body, grid_spec=pltpu.PrefetchScalarGridSpec(num_scalar_pr...  143 us
    ppermute x16, waiting for transfers between devices, over_y(): return lax.ppermute(values, 'y', SWAP)  135 us
    ppermute x16, waiting for transfers between devices, over_x(): return lax.ppermute(values, 'x', SWAP)  53.4 us
    dot_general x4, matrix products, mat_rows(): lax.dot_general(left, right, (((0,), (0,)), ((), ())), preferred_element_...  41.3 us
    ppermute x28, waiting for transfers between devices, send_pieces(): lax.ppermute(piece, PLANE, [(i, i ^ mask) for i in range(PARTS)])  31.6 us
    ppermute x28, starting transfers between devices, send_pieces(): lax.ppermute(piece, PLANE, [(i, i ^ mask) for i in range(PARTS)])  28.7 us
    ppermute x5, waiting for transfers between devices, doubled(): other = lax.ppermute(values, axis, perm)  21.5 us
    another operation x6, other arithmetic  19 us
  transfers between devices with their start and end apart: 101, of which 42 were waited for; matrix products, arithmetic and copies ran while one was open for 20% of the time, Pallas kernels for 18%

profile of v4, /device:TPU:0, one launch (start us, length us, event | category | flops | bytes accessed | tf_op | source)
XLA Modules:
  0.0 648.9 jit_solution(13166726998502670532)
XLA Ops:
  8.0 3.4 reshape.307
  43.4 11.6 %collective-permute-done.4.refs_2_ = bf16[256,2048]{1,0:T(8,128)(2,1)} collective-permute-done((bf16[256,2048]{1,0:T(8,128)(2,1)S(1)}, bf16[256,2048]{1,0:T(8,128)(2,1)}, u32[]{:S(2)}, u32[]{:S(2)}) %collective-permute-start.4) | collective-permute-done | bytes 1048608 | tf_op jit(solution)/shard_map/ppermute | solution.py:47
  61.6 18.5 %collective-permute-done.1 = bf16[2,512]{1,0:T(2,128)(2,1)S(1)} collective-permute-done((bf16[2,512]{1,0:T(2,128)(2,1)S(1)}, bf16[2,512]{1,0:T(2,128)(2,1)S(1)}, u32[]{:S(2)}, u32[]{:S(2)}) %collective-permute-start.1) | collective-permute-done | bytes 2080 | tf_op jit(solution)/shard_map/ppermute | solution.py:176
  94.0 4.1 collective-permute-done.19.refs_4_
  105.8 14.8 %collective-permute-done.24.refs_7_ = bf16[256,2048]{1,0:T(8,128)(2,1)} collective-permute-done((bf16[256,2048]{1,0:T(8,128)(2,1)}, bf16[256,2048]{1,0:T(8,128)(2,1)}, u32[]{:S(2)}, u32[]{:S(2)}) %collective-permute-start.24) | collective-permute-done | bytes 1048608 | tf_op jit(solution)/shard_map/ppermute | solution.py:47
  135.5 19.7 %shard_map.231 = (bf16[2048,2048]{1,0:T(8,128)(2,1)}, bf16[2048,768]{1,0:T(8,128)(2,1)}, bf16[2048,256]{1,0:T(8,128)(2,1)}, bf16[1024,2048]{1,0:T(8,128)(2,1)}) custom-call(s32[8,6]{1,0:T(8,128)} %copy.110.marks_ref, bf16[256,2048]{1,0:T(8,128)(2,1)} %collective-permute-done.25.refs_0_, bf16[256,2048]{1,0:T(8,128)(2,1)} %copy-done.18, ...), custom_call_target="tpu_custom_call" | custom-call | flops 1 | bytes 1 | tf_op jit(solution)/shard_map/pallas_call | solution.py:517
  156.1 19.5 %shard_map.232 = (bf16[2048,2048]{1,0:T(8,128)(2,1)}, bf16[2048,768]{1,0:T(8,128)(2,1)}, bf16[2048,256]{1,0:T(8,128)(2,1)}, bf16[1024,2048]{1,0:T(8,128)(2,1)}) custom-call(s32[8,6]{1,0:T(8,128)} %copy.114.marks_ref, bf16[256,2048]{1,0:T(8,128)(2,1)} %refs_0_.1, ...), custom_call_target="tpu_custom_call", output_to_operand_aliasing={{0}: (14, {}), {1}: (15, {}), {2}: (16, {})} | custom-call | flops 1 | bytes 1 | tf_op jit(solution)/shard_map/pallas_call | solution.py:517
  179.7 13.1 %collective-permute-done.35 = bf16[128,2048]{1,0:T(8,128)(2,1)S(1)} collective-permute-done((bf16[128,2048]{1,0:T(8,128)(2,1)S(1)}, bf16[128,2048]{1,0:T(8,128)(2,1)S(1)}, u32[]{:S(2)}, u32[]{:S(2)}) %collective-permute-start.35) | collective-permute-done | bytes 524320 | tf_op jit(solution)/shard_map/ppermute | solution.py:43
  197.8 22.0 %collective-permute-done.36 = bf16[256,2048]{1,0:T(8,128)(2,1)} collective-permute-done((bf16[256,2048]{1,0:T(8,128)(2,1)S(1)}, bf16[256,2048]{1,0:T(8,128)(2,1)}, u32[]{:S(2)}, u32[]{:S(2)}) %collective-permute-start.36) | collective-permute-done | bytes 1048608 | tf_op jit(solution)/shard_map/ppermute | solution.py:47
  228.0 19.8 %collective-permute-done.38.refs_2_ = bf16[256,2048]{1,0:T(8,128)(2,1)S(1)} collective-permute-done((bf16[256,2048]{1,0:T(8,128)(2,1)S(1)}, bf16[256,2048]{1,0:T(8,128)(2,1)S(1)}, u32[]{:S(2)}, u32[]{:S(2)}) %collective-permute-start.38) | collective-permute-done | bytes 1048608 | tf_op jit(solution)/shard_map/ppermute | solution.py:47
  253.1 10.6 %collective-permute-done.39.refs_3_ = bf16[128,2048]{1,0:T(8,128)(2,1)S(1)} collective-permute-done((bf16[128,2048]{1,0:T(8,128)(2,1)S(1)}, bf16[128,2048]{1,0:T(8,128)(2,1)S(1)}, u32[]{:S(2)}, u32[]{:S(2)}) %collective-permute-start.39) | collective-permute-done | bytes 524320 | tf_op jit(solution)/shard_map/ppermute | solution.py:43
  268.2 5.1 all-gather.8.cloned.1.call-done
  273.2 30.1 %shard_map.233 = (bf16[2048,2048]{1,0:T(8,128)(2,1)}, bf16[2048,2048]{1,0:T(8,128)(2,1)}, bf16[2048,704]{1,0:T(8,128)(2,1)}, bf16[2048,1408]{1,0:T(8,128)(2,1)},...) custom-call(bf16[256,2048]{1,0:T(8,128)(2,1)} %copy-done.22, bf16[256,2048]{1,0:T(8,128)(2,1)} %copy-done.24, ...), custom_call_target="tpu_custom_call" | custom-call | flops 1 | bytes 1 | tf_op jit(solution)/shard_map/pallas_call | solution.py:517
  303.5 29.9 %shard_map.234 = (bf16[2048,2048]{1,0:T(8,128)(2,1)}, bf16[2048,2048]{1,0:T(8,128)(2,1)}, bf16[2048,704]{1,0:T(8,128)(2,1)}, bf16[2048,1408]{1,0:T(8,128)(2,1)},...) custom-call(bf16[256,2048]{1,0:T(8,128)(2,1)} %copy-done.11, ...), custom_call_target="tpu_custom_call", output_to_operand_aliasing={{0}: (11, {}), {1}: (12, {}), {2}: (13, {}), {3}: (14, {})} | custom-call | flops 1 | bytes 1 | tf_op jit(solution)/shard_map/pallas_call | solution.py:517
  338.4 10.0 %convolution_convert_fusion.2 = bf16[2048,704]{0,1:T(8,128)(2,1)} fusion(bf16[2048,2048]{1,0:T(8,128)(2,1)} %get-tuple-element.83, bf16[2048,704]{1,0:T(8,128)(2,1)S(1)} %copy-done.12), kind=kOutput, calls=%fused_computation.3 | convolution fusion | flops 5907021824 | bytes 14155776 | tf_op jit(solution)/shard_map/dot_general | solution.py:31
  351.9 11.6 %collective-permute-done.53 = bf16[128,2048]{1,0:T(8,128)(2,1)S(1)} collective-permute-done((bf16[128,2048]{1,0:T(8,128)(2,1)}, bf16[128,2048]{1,0:T(8,128)(2,1)S(1)}, u32[]{:S(2)}, u32[]{:S(2)}) %collective-permute-start.53) | collective-permute-done | bytes 524320 | tf_op jit(solution)/shard_map/ppermute | solution.py:47
  372.2 17.3 %convolution_convert_fusion = bf16[2048,1408]{1,0:T(8,128)(2,1)} fusion(bf16[2048,2048]{1,0:T(8,128)(2,1)S(1)} %copy-done.5, bf16[2048,1408]{1,0:T(8,128)(2,1)} %get-tuple-element.90), kind=kOutput, calls=%fused_computation | convolution fusion | flops 11814043648 | bytes 19922944 | tf_op jit(solution)/shard_map/dot_general | solution.py:31
  389.6 4.3 collective-permute-done.54
  396.1 3.5 multiply_reduce_fusion
  403.4 22.4 %collective-permute-done.59.refs_2_ = bf16[256,2048]{1,0:T(8,128)(2,1)} collective-permute-done((bf16[256,2048]{1,0:T(8,128)(2,1)}, bf16[256,2048]{1,0:T(8,128)(2,1)}, u32[]{:S(2)}, u32[]{:S(2)}) %collective-permute-start.59) | collective-permute-done | bytes 1048608 | tf_op jit(solution)/shard_map/ppermute | solution.py:47
  429.8 8.5 %collective-permute-done.61.refs_3_ = bf16[128,2048]{1,0:T(8,128)(2,1)} collective-permute-done((bf16[128,2048]{1,0:T(8,128)(2,1)S(1)}, bf16[128,2048]{1,0:T(8,128)(2,1)}, u32[]{:S(2)}, u32[]{:S(2)}) %collective-permute-start.61) | collective-permute-done | bytes 524320 | tf_op jit(solution)/shard_map/ppermute | solution.py:43
  442.0 22.7 %shard_map.235 = (bf16[2048,2048]{1,0:T(8,128)(2,1)}, bf16[2048,768]{1,0:T(8,128)(2,1)}, bf16[1024,2048]{1,0:T(8,128)(2,1)}) custom-call(s32[8,6]{1,0:T(8,128)} %copy.118.marks_ref, bf16[256,2048]{1,0:T(8,128)(2,1)} %collective-permute-done.56.refs_0_, bf16[256,2048]{1,0:T(8,128)(2,1)} %collective-permute-done.58.refs_1_, ...), custom_call_target="tpu_custom_call" | custom-call | flops 1 | bytes 1 | tf_op jit(solution)/shard_map/pallas_call | solution.py:517
  466.2 21.5 %shard_map.236 = (bf16[2048,2048]{1,0:T(8,128)(2,1)}, bf16[2048,768]{1,0:T(8,128)(2,1)}, bf16[1024,2048]{1,0:T(8,128)(2,1)}) custom-call(s32[8,6]{1,0:T(8,128)} %copy.122.marks_ref, bf16[256,2048]{1,0:T(8,128)(2,1)} %get-tuple-element.124.refs_0_, bf16[256,2048]{1,0:T(8,128)(2,1)} %collective-permute-done.57.refs_1_, ...), custom_call_target="tpu_custom_call", output_to_operand_aliasing={{0}: (12, {}), {1}: (13, {})} | custom-call | flops 1 | bytes 1 | tf_op jit(solution)/shard_map/pallas_call | solution.py:517
  490.3 4.2 add_convert_fusion.12
  501.4 10.7 %convolution_convert_fusion.1 = bf16[2048,768]{1,0:T(8,128)(2,1)} fusion(bf16[2048,2048]{1,0:T(8,128)(2,1)} %get-tuple-element.100, bf16[2048,768]{1,0:T(8,128)(2,1)S(1)} %copy-done.3), kind=kOutput, calls=%fused_computation.2 | convolution fusion | flops 6444023808 | bytes 14680064 | tf_op jit(solution)/shard_map/dot_general | solution.py:31
  512.2 9.0 %collective-permute-done.72 = bf16[128,2048]{1,0:T(8,128)(2,1)} collective-permute-done((bf16[128,2048]{1,0:T(8,128)(2,1)}, bf16[128,2048]{1,0:T(8,128)(2,1)}, u32[]{:S(2)}, u32[]{:S(2)}) %collective-permute-start.72) | collective-permute-done | bytes 524320 | tf_op jit(solution)/shard_map/ppermute | solution.py:47
  521.2 3.7 add_convert_fusion.2
  538.9 13.4 %collective-permute-done.73 = bf16[256,2048]{1,0:T(8,128)(2,1)} collective-permute-done((bf16[256,2048]{1,0:T(8,128)(2,1)}, bf16[256,2048]{1,0:T(8,128)(2,1)}, u32[]{:S(2)}, u32[]{:S(2)}) %collective-permute-start.73) | collective-permute-done | bytes 1048608 | tf_op jit(solution)/shard_map/ppermute | solution.py:43
  554.1 4.2 convert_add_fusion.1
  558.3 16.0 %collective-permute-done.69 = bf16[256,2048]{1,0:T(8,128)(2,1)} collective-permute-done((bf16[256,2048]{1,0:T(8,128)(2,1)}, bf16[256,2048]{1,0:T(8,128)(2,1)}, u32[]{:S(2)}, u32[]{:S(2)}) %collective-permute-start.69) | collective-permute-done | bytes 1048608 | tf_op jit(solution)/shard_map/ppermute | solution.py:47
  574.3 4.1 select_convert_fusion
  611.4 18.2 %collective-permute-done.91.refs_5_ = bf16[64,2112]{1,0:T(8,128)(2,1)S(1)} collective-permute-done((bf16[64,2112]{1,0:T(8,128)(2,1)S(1)}, bf16[64,2112]{1,0:T(8,128)(2,1)S(1)}, u32[]{:S(2)}, u32[]{:S(2)}) %collective-permute-start.91) | collective-permute-done | bytes 270368 | tf_op jit(solution)/shard_map/ppermute | solution.py:141
  (438 shorter events, 205.4 us)
Async XLA Ops:
  7.2 127.0 %all-gather.6.cloned.1.call-start = ((), (), s32[]{:S(2)}) async-start(), calls=%async_computation.5 | async-start | bytes 1310720 | tf_op jit(solution)/shard_map/all_gather | solution.py:55
  7.9 126.3 %all-gather.4.cloned.1.call-start = ((), (), s32[]{:S(2)}) async-start(), calls=%async_computation.4 | async-start | bytes 3932160 | tf_op jit(solution)/shard_map/all_gather | solution.py:55
  29.6 243.7 %all-gather.8.cloned.1.call-start = ((), (), s32[]{:S(2)}) async-start(), calls=%async_computation.6 | async-start | bytes 11796480 | tf_op jit(solution)/shard_map/all_gather | solution.py:55
  29.6 25.4 %collective-permute-start.4 = (bf16[256,2048]{1,0:T(8,128)(2,1)S(1)}, bf16[256,2048]{1,0:T(8,128)(2,1)}, u32[]{:S(2)}, u32[]{:S(2)}) collective-permute-start(bf16[256,2048]{1,0:T(8,128)(2,1)S(1)} %copy-done), channel_id=1, source_target_pairs={{0,4},{4,0},{1,5},{5,1},{2,6},{6,2},{3,7},{7,3},{8,12},{12,8},{9,1... | collective-permute-start | bytes 3145736 | tf_op jit(solution)/shard_map/ppermute | solution.py:47
  31.1 26.1 %collective-permute-start.3 = (bf16[256,2048]{1,0:T(8,128)(2,1)S(1)}, bf16[256,2048]{1,0:T(8,128)(2,1)}, u32[]{:S(2)}, u32[]{:S(2)}) collective-permute-start(bf16[256,2048]{1,0:T(8,128)(2,1)S(1)} %copy-done), channel_id=1, source_target_pairs={{0,2},{2,0},{1,3},{3,1},{4,6},{6,4},{5,7},{7,5},{8,10},{10,8},{9,1... | collective-permute-start | bytes 3145736 | tf_op jit(solution)/shard_map/ppermute | solution.py:43
  33.5 27.5 %collective-permute-start = (bf16[1,512]{1,0:T(2,128)(2,1)S(1)}, bf16[1,512]{1,0:T(2,128)(2,1)S(1)}, u32[]{:S(2)}, u32[]{:S(2)}) collective-permute-start(bf16[1,512]{1,0:T(2,128)(2,1)S(1)} %broadcast_in_dim.120), channel_id=1, source_target_pairs={{0,1},{1,0},{2,3},{3,2},{4,5},{5,4},{6,7},{7,6},{8,9},{9,8},{10,11... | collective-permute-start | bytes 3080 | tf_op jit(solution)/shard_map/ppermute | solution.py:176
  38.8 45.0 %collective-permute-start.22 = (bf16[3,64,704]{2,1,0:T(8,128)(2,1)S(1)}, bf16[3,64,704]{2,1,0:T(8,128)(2,1)S(1)}, u32[]{:S(2)}, u32[]{:S(2)}) collective-permute-start(bf16[3,64,704]{2,1,0:T(8,128)(2,1)S(1)} %get-tuple-element.153), channel_id=1, source_target_pairs={{0,7},{1,6},{2,5},{3,4},{4,3},{5,2},{6,1},{7,0},{8,15},{9,14},{10,... | collective-permute-start | bytes 811016 | tf_op jit(solution)/shard_map/ppermute | solution.py:141
  39.4 52.0 %collective-permute-start.21 = (bf16[3,64,704]{2,1,0:T(8,128)(2,1)}, bf16[3,64,704]{2,1,0:T(8,128)(2,1)S(1)}, u32[]{:S(2)}, u32[]{:S(2)}) collective-permute-start(bf16[3,64,704]{2,1,0:T(8,128)(2,1)} %get-tuple-element.154), channel_id=1, source_target_pairs={{0,6},{1,7},{2,4},{3,5},{4,2},{5,3},{6,0},{7,1},{8,14},{9,15},{10,... | collective-permute-start | bytes 811016 | tf_op jit(solution)/shard_map/ppermute | solution.py:141
  58.3 26.1 %collective-permute-start.5 = (bf16[128,2048]{1,0:T(8,128)(2,1)}, bf16[128,2048]{1,0:T(8,128)(2,1)}, u32[]{:S(2)}, u32[]{:S(2)}) collective-permute-start(bf16[128,2048]{1,0:T(8,128)(2,1)} %slice.369), channel_id=1, source_target_pairs={{0,2},{2,0},{1,3},{3,1},{4,6},{6,4},{5,7},{7,5},{8,10},{10,8},{9,1... | collective-permute-start | bytes 1572872 | tf_op jit(solution)/shard_map/ppermute | solution.py:43
  59.9 26.9 %collective-permute-start.6 = (bf16[128,2048]{1,0:T(8,128)(2,1)S(1)}, bf16[128,2048]{1,0:T(8,128)(2,1)}, u32[]{:S(2)}, u32[]{:S(2)}) collective-permute-start(bf16[128,2048]{1,0:T(8,128)(2,1)S(1)} %slice.370), channel_id=1, source_target_pairs={{0,4},{4,0},{1,5},{5,1},{2,6},{6,2},{3,7},{7,3},{8,12},{12,8},{9,1... | collective-permute-start | bytes 1572872 | tf_op jit(solution)/shard_map/ppermute | solution.py:47
  93.3 27.3 %collective-permute-start.24 = (bf16[256,2048]{1,0:T(8,128)(2,1)}, bf16[256,2048]{1,0:T(8,128)(2,1)}, u32[]{:S(2)}, u32[]{:S(2)}) collective-permute-start(bf16[256,2048]{1,0:T(8,128)(2,1)} %fusion.12.refs_5_), channel_id=1, source_target_pairs={{0,4},{4,0},{1,5},{5,1},{2,6},{6,2},{3,7},{7,3},{8,12},{12,8},{9,1... | collective-permute-start | bytes 3145736 | tf_op jit(solution)/shard_map/ppermute | solution.py:47
  98.0 30.1 %collective-permute-start.25 = (bf16[256,2048]{1,0:T(8,128)(2,1)S(1)}, bf16[256,2048]{1,0:T(8,128)(2,1)}, u32[]{:S(2)}, u32[]{:S(2)}) collective-permute-start(bf16[256,2048]{1,0:T(8,128)(2,1)S(1)} %copy-done), channel_id=1, source_target_pairs={{0,1},{1,0},{2,3},{3,2},{4,5},{5,4},{6,7},{7,6},{8,9},{9,8},{10,11... | collective-permute-start | bytes 3145736 | tf_op jit(solution)/shard_map/ppermute | solution.py:51
  99.8 29.8 %collective-permute-start.27 = (bf16[256,2048]{1,0:T(8,128)(2,1)}, bf16[256,2048]{1,0:T(8,128)(2,1)}, u32[]{:S(2)}, u32[]{:S(2)}) collective-permute-start(bf16[256,2048]{1,0:T(8,128)(2,1)} %collective-permute-done.4.refs_2_), channel_id=1, source_target_pairs={{0,1},{1,0},{2,3},{3,2},{4,5},{5,4},{6,7},{7,6},{8,9},{9,8},{10,11... | collective-permute-start | bytes 3145736 | tf_op jit(solution)/shard_map/ppermute | solution.py:51
  100.9 24.9 %collective-permute-start.23 = (bf16[256,2048]{1,0:T(8,128)(2,1)}, bf16[256,2048]{1,0:T(8,128)(2,1)}, u32[]{:S(2)}, u32[]{:S(2)}) collective-permute-start(bf16[256,2048]{1,0:T(8,128)(2,1)} %fusion.12.refs_5_), channel_id=1, source_target_pairs={{0,2},{2,0},{1,3},{3,1},{4,6},{6,4},{5,7},{7,5},{8,10},{10,8},{9,1... | collective-permute-start | bytes 3145736 | tf_op jit(solution)/shard_map/ppermute | solution.py:43
  105.1 334.7 %reduce-scatter.5.cloned.1.call-start = ((), (), s32[]{:S(2)}) async-start(), calls=%async_computation.7 | async-start | bytes 3604480 | tf_op jit(solution)/shard_map/reduce_scatter | solution.py:59
  105.5 28.6 %collective-permute-start.26 = (bf16[256,2048]{1,0:T(8,128)(2,1)}, bf16[256,2048]{1,0:T(8,128)(2,1)S(1)}, u32[]{:S(2)}, u32[]{:S(2)}) collective-permute-start(bf16[256,2048]{1,0:T(8,128)(2,1)} %collective-permute-done.3.refs_1_), channel_id=1, source_target_pairs={{0,1},{1,0},{2,3},{3,2},{4,5},{5,4},{6,7},{7,6},{8,9},{9,8},{10,11... | collective-permute-start | bytes 3145736 | tf_op jit(solution)/shard_map/ppermute | solution.py:51
  128.1 27.0 %collective-permute-start.30 = (bf16[128,2048]{1,0:T(8,128)(2,1)}, bf16[128,2048]{1,0:T(8,128)(2,1)S(1)}, u32[]{:S(2)}, u32[]{:S(2)}) collective-permute-start(bf16[128,2048]{1,0:T(8,128)(2,1)} %slice.374), channel_id=1, source_target_pairs={{0,2},{2,0},{1,3},{3,1},{4,6},{6,4},{5,7},{7,5},{8,10},{10,8},{9,1... | collective-permute-start | bytes 1572872 | tf_op jit(solution)/shard_map/ppermute | solution.py:43
  129.6 25.6 %collective-permute-start.31 = (bf16[128,2048]{1,0:T(8,128)(2,1)}, bf16[128,2048]{1,0:T(8,128)(2,1)S(1)}, u32[]{:S(2)}, u32[]{:S(2)}) collective-permute-start(bf16[128,2048]{1,0:T(8,128)(2,1)} %slice.375), channel_id=1, source_target_pairs={{0,4},{4,0},{1,5},{5,1},{2,6},{6,2},{3,7},{7,3},{8,12},{12,8},{9,1... | collective-permute-start | bytes 1572872 | tf_op jit(solution)/shard_map/ppermute | solution.py:47
  303.4 30.1 %collective-permute-start.51 = (bf16[1024,2048]{1,0:T(8,128)(2,1)}, bf16[1024,2048]{1,0:T(8,128)(2,1)S(1)}, u32[]{:S(2)}, u32[]{:S(2)}) collective-permute-start(bf16[1024,2048]{1,0:T(8,128)(2,1)} %get-tuple-element.82), channel_id=1, source_target_pairs={{0,1},{1,0},{2,3},{3,2},{4,5},{5,4},{6,7},{7,6},{8,9},{9,8},{10,11... | collective-permute-start | bytes 12582920 | tf_op jit(solution)/shard_map/ppermute | solution.py:51
  348.4 229.9 %reduce-scatter.7.cloned.1.call-start = ((), (), s32[]{:S(2)}) async-start(), calls=%async_computation.8 | async-start | bytes 7208960 | tf_op jit(solution)/shard_map/reduce_scatter | solution.py:59
  389.5 208.6 %reduce-scatter.9.cloned.1.call-start = ((), (), s32[]{:S(2)}) async-start(), calls=%async_computation.9 | async-start | bytes 3932160 | tf_op jit(solution)/shard_map/reduce_scatter | solution.py:59
  403.4 37.0 %collective-permute-start.56 = (bf16[256,2048]{1,0:T(8,128)(2,1)}, bf16[256,2048]{1,0:T(8,128)(2,1)}, u32[]{:S(2)}, u32[]{:S(2)}) collective-permute-start(bf16[256,2048]{1,0:T(8,128)(2,1)} %get-tuple-element.124.refs_0_), channel_id=1, source_target_pairs={{0,1},{1,0},{2,3},{3,2},{4,5},{5,4},{6,7},{7,6},{8,9},{9,8},{10,11... | collective-permute-start | bytes 3145736 | tf_op jit(solution)/shard_map/ppermute | solution.py:51
  464.7 25.6 %collective-permute-start.65 = (bf16[1024,2048]{1,0:T(8,128)(2,1)}, bf16[1024,2048]{1,0:T(8,128)(2,1)}, u32[]{:S(2)}, u32[]{:S(2)}) collective-permute-start(bf16[1024,2048]{1,0:T(8,128)(2,1)} %get-tuple-element.95), channel_id=1, source_target_pairs={{0,1},{1,0},{2,3},{3,2},{4,5},{5,4},{6,7},{7,6},{8,9},{9,8},{10,11... | collective-permute-start | bytes 12582920 | tf_op jit(solution)/shard_map/ppermute | solution.py:51
  464.9 31.7 %collective-permute-start.70 = (bf16[1024,2048]{1,0:T(8,128)(2,1)}, bf16[1024,2048]{1,0:T(8,128)(2,1)}, u32[]{:S(2)}, u32[]{:S(2)}) collective-permute-start(bf16[1024,2048]{1,0:T(8,128)(2,1)} %get-tuple-element.94), channel_id=1, source_target_pairs={{0,1},{1,0},{2,3},{3,2},{4,5},{5,4},{6,7},{7,6},{8,9},{9,8},{10,11... | collective-permute-start | bytes 12582920 | tf_op jit(solution)/shard_map/ppermute | solution.py:51
  494.5 33.6 %collective-permute-start.68 = (bf16[128,2048]{1,0:T(8,128)(2,1)}, bf16[128,2048]{1,0:T(8,128)(2,1)}, u32[]{:S(2)}, u32[]{:S(2)}) collective-permute-start(bf16[128,2048]{1,0:T(8,128)(2,1)} %get-tuple-element.137), channel_id=1, source_target_pairs={{0,2},{2,0},{1,3},{3,1},{4,6},{6,4},{5,7},{7,5},{8,10},{10,8},{9,1... | collective-permute-start | bytes 1572872 | tf_op jit(solution)/shard_map/ppermute | solution.py:43
  495.9 32.2 %collective-permute-start.66 = (bf16[128,2048]{1,0:T(8,128)(2,1)}, bf16[128,2048]{1,0:T(8,128)(2,1)}, u32[]{:S(2)}, u32[]{:S(2)}) collective-permute-start(bf16[128,2048]{1,0:T(8,128)(2,1)} %get-tuple-element.138), channel_id=1, source_target_pairs={{0,4},{4,0},{1,5},{5,1},{2,6},{6,2},{3,7},{7,3},{8,12},{12,8},{9,1... | collective-permute-start | bytes 1572872 | tf_op jit(solution)/shard_map/ppermute | solution.py:47
  512.1 127.9 %reduce-scatter.11.cloned.1.call-start = ((), (), s32[]{:S(2)}) async-start(), calls=%async_computation.10 | async-start | bytes 1310720 | tf_op jit(solution)/shard_map/reduce_scatter | solution.py:59
  526.0 26.4 %collective-permute-start.73 = (bf16[256,2048]{1,0:T(8,128)(2,1)}, bf16[256,2048]{1,0:T(8,128)(2,1)}, u32[]{:S(2)}, u32[]{:S(2)}) collective-permute-start(bf16[256,2048]{1,0:T(8,128)(2,1)} %pad_maximum_fusion.7), channel_id=1, source_target_pairs={{0,2},{2,0},{1,3},{3,1},{4,6},{6,4},{5,7},{7,5},{8,10},{10,8},{9,1... | collective-permute-start | bytes 3145736 | tf_op jit(solution)/shard_map/ppermute | solution.py:43
  527.7 26.4 %collective-permute-start.74 = (bf16[256,2048]{1,0:T(8,128)(2,1)}, bf16[256,2048]{1,0:T(8,128)(2,1)}, u32[]{:S(2)}, u32[]{:S(2)}) collective-permute-start(bf16[256,2048]{1,0:T(8,128)(2,1)} %pad_maximum_fusion.8), channel_id=1, source_target_pairs={{0,4},{4,0},{1,5},{5,1},{2,6},{6,2},{3,7},{7,3},{8,12},{12,8},{9,1... | collective-permute-start | bytes 3145736 | tf_op jit(solution)/shard_map/ppermute | solution.py:47
  531.9 42.4 %collective-permute-start.69 = (bf16[256,2048]{1,0:T(8,128)(2,1)}, bf16[256,2048]{1,0:T(8,128)(2,1)}, u32[]{:S(2)}, u32[]{:S(2)}) collective-permute-start(bf16[256,2048]{1,0:T(8,128)(2,1)} %pad_maximum_fusion.6), channel_id=1, source_target_pairs={{0,4},{4,0},{1,5},{5,1},{2,6},{6,2},{3,7},{7,3},{8,12},{12,8},{9,1... | collective-permute-start | bytes 3145736 | tf_op jit(solution)/shard_map/ppermute | solution.py:47
  534.2 40.1 %collective-permute-start.67 = (bf16[256,2048]{1,0:T(8,128)(2,1)}, bf16[256,2048]{1,0:T(8,128)(2,1)}, u32[]{:S(2)}, u32[]{:S(2)}) collective-permute-start(bf16[256,2048]{1,0:T(8,128)(2,1)} %pad_maximum_fusion.5), channel_id=1, source_target_pairs={{0,2},{2,0},{1,3},{3,1},{4,6},{6,4},{5,7},{7,5},{8,10},{10,8},{9,1... | collective-permute-start | bytes 3145736 | tf_op jit(solution)/shard_map/ppermute | solution.py:43
  604.8 24.8 %collective-permute-start.91 = (bf16[64,2112]{1,0:T(8,128)(2,1)S(1)}, bf16[64,2112]{1,0:T(8,128)(2,1)S(1)}, u32[]{:S(2)}, u32[]{:S(2)}) collective-permute-start(bf16[64,2112]{1,0:T(8,128)(2,1)S(1)} %pad_maximum_fusion.14), channel_id=1, source_target_pairs={{0,5},{1,4},{2,7},{3,6},{4,1},{5,0},{6,3},{7,2},{8,13},{9,12},{10,... | collective-permute-start | bytes 811016 | tf_op jit(solution)/shard_map/ppermute | solution.py:141
  (119 other events, 1424.6 us)
Sparse Core Ops, SparseCore 0:
  9.6 30.6 all-gather.5
  42.4 63.0 all-gather.3
  107.1 166.1 all-gather.7
  348.6 54.3 reduce-scatter.4
  405.1 102.0 reduce-scatter.6
  512.3 57.9 reduce-scatter.8
  598.3 26.6 reduce-scatter.10

commit v5 on v4

--- a/solution.py
+++ b/solution.py
@@ -76,10 +76,15 @@
 
 def scatter_plane(kept, sent, rows, first=None, second=None):
     half = rows // 2
-    came = over_c(sent)
+    kept, sent = (parts if isinstance(parts, list) else [parts] for parts in (kept, sent))
+    came = [over_c(part) for part in sent]
+
+    def rows_of(parts, low, high):
+        size = parts[0].shape[0]
+        return parts[low // size][low % size : low % size + high - low].astype(f32)
 
     def joined(low, high):
-        return kept[low:high].astype(f32) + came[low:high].astype(f32)
+        return rows_of(kept, low, high) + rows_of(came, low, high)
 
     far_low = joined(3 * rows, 3 * rows + half).astype(bf16)
     far_high = joined(3 * rows + half, 4 * rows).astype(bf16)
@@ -452,7 +457,7 @@
     branch = refs[0:5]
     saved, qkv_weight, out_weight, cos_ref, ahead_ref, behind_ref = refs[5:11]
     refs = refs[11 if first else 13 :]
-    branch_ref, grad_ref, part_ref, branch_rows, line_sems, keep_sems = refs
+    branch_ref, grad_ref, early_ref, late_ref, branch_rows, line_sems, keep_sems = refs
     step = pl.program_id(0)
     group = half * GROUPS + step
     line = line_copies(branch, branch_rows, line_sems)
@@ -491,11 +496,20 @@
         axis=1,
     ).astype(bf16)
     grad_ref[...] = grads
-    part_ref[...] = mat_cols(grads, qkv_weight[...]).astype(bf16)
+    part = mat_cols(grads, qkv_weight[...]).astype(bf16)
+
+    @pl.when(step < GROUPS // 2)
+    def _():
+        early_ref[...] = part
+
+    @pl.when(step >= GROUPS // 2)
+    def _():
+        late_ref[...] = part
+
     await_kept(step, GROUPS, kept)
 
 
-def run_half(body, scalars, loose, blocked, whole, outputs, scratch, half, rows, prior, steps=GROUPS):
+def run_half(body, scalars, loose, blocked, whole, outputs, scratch, half, rows, prior, flops=1, steps=GROUPS, parted=0):
     loose, blocked, whole = list(loose), list(blocked), list(whole)
     kept = list(prior or [])
     out_shape, out_specs = [], []
@@ -505,6 +519,12 @@
         out_shape.append(jax.ShapeDtypeStruct((total * rows, width), bf16))
         block = pl.BlockSpec((rows, width), lambda i, *_, offset=offset: (i + offset, 0))
         out_specs.append(ANYWHERE if by_copy else block)
+    if parted:
+        out_shape += [jax.ShapeDtypeStruct((steps // 2 * rows, parted), bf16)] * 2
+        out_specs += [
+            pl.BlockSpec((rows, parted), lambda i, *_: (jnp.minimum(i, steps // 2 - 1), 0)),
+            pl.BlockSpec((rows, parted), lambda i, *_: (jnp.maximum(i - steps // 2, 0), 0)),
+        ]
     in_specs = [ANYWHERE] * len(loose)
     for values in blocked:
         in_specs.append(pl.BlockSpec((rows, values.shape[1]), lambda i, *_: (i + half * steps, 0)))
@@ -528,7 +548,7 @@
         compiler_params=pltpu.CompilerParams(
             dimension_semantics=("arbitrary",), vmem_limit_bytes=VMEM_BYTES
         ),
-        cost_estimate=pl.CostEstimate(flops=1, bytes_accessed=1, transcendentals=0),
+        cost_estimate=pl.CostEstimate(flops=flops, bytes_accessed=1, transcendentals=0),
     )(*scalars, *loose, *blocked, *whole, *kept)
 
 
@@ -685,6 +705,7 @@
             half,
             2 * rows,
             prior,
+            1,
             GROUPS // 2,
         )
 
@@ -713,7 +734,7 @@
             branch_lines[half],
             (saved,),
             (qkv_full, out_full) + tables,
-            ((width, True, True), (3 * head_cols, True, False), (width, False, False)),
+            ((width, True, True), (3 * head_cols, True, False)),
             [
                 pltpu.VMEM((line_rows, width), bf16),
                 dma((5,)),
@@ -722,21 +743,35 @@
             half,
             rows,
             prior,
+            13 * line_rows * width * 4 * head_cols,
+            GROUPS,
+            width,
         )
 
-    *shared, input_sent = attention_back(1, None, down_grad)
-    grad_branch, grad_qkv, input_kept = attention_back(0, shared)
+    backs = []
+
+    def back_first(*far):
+        backs.append(attention_back(1, None, down_grad, *far))
+        return backs[0][3]
+
+    def back_second(*near):
+        backs.append(attention_back(0, backs[0][:2], *near))
+        return backs[1][3]
+
+    down, _, _ = scatter_plane(
+        down_kept, after(down_sent, grad_middle), rows, back_first, back_second
+    )
+    layer_out = jnp.where(valid, middle + down, 0.0).astype(bf16)
+    grad_branch, grad_qkv, *input_kept = backs[1]
+    input_sent = backs[0][2:]
     grad_normed_one, qkv_part, out_part = scatter_plane(
-        input_kept,
-        input_sent,
+        list(input_kept),
+        list(input_sent),
         rows,
-        lambda *far: mat_rows(after(normed_one, *far), grad_qkv).astype(bf16),
-        lambda *near: mat_rows(after(mixed, *near), grad_branch).astype(bf16),
+        lambda *far: mat_rows(after(normed_one, *far, down), grad_qkv).astype(bf16),
+        lambda *near: mat_rows(after(mixed, *near, both_grad), grad_branch).astype(bf16),
     )
     qkv_grad = scatter_line(qkv_part)
-    grad_normed_one = after(grad_normed_one, both_grad)
-    down = scatter_plane(down_kept, after(down_sent, input_sent), rows)
-    layer_out = jnp.where(valid, middle + down, 0.0).astype(bf16)
     bias_part = jnp.sum(grad_qkv.astype(f32), axis=0).reshape(3 * heads, 1, HEAD)
     bias_grad = jnp.where(
         lax.broadcasted_iota(jnp.int32, (3 * heads, PARTS, HEAD), 1) == me, bias_part, 0.0

time: 657 us -> 634 us (0.965)
  waiting for transfers between devices: 256 us -> 228 us
    ppermute x16, waiting for transfers between devices: 135 us -> 105 us  [over_y(): return lax.ppermute(values, 'y', SWAP)]
  transfers between devices with their start and end apart: 101 -> 102, of which waited for: 42 -> 40; matrix products, arithmetic and copies ran while one was open for 20% -> 22% of each run, Pallas kernels for 18% -> 19%
where the time goes in v5:
time: 634 us; the launch traced here: 626 us
  waiting for transfers between devices  228 us (36%)
  Pallas kernels  152 us (24%)
  starting transfers between devices  80 us (13%)
  other arithmetic  61.4 us (10%)
  matrix products  44.8 us (7%)
  local copies, waits for them, and re-layouts  43.7 us (7%)
  between operations  16.4 us (3%)
    pallas_call x6, Pallas kernels, run_half(): pl.pallas_call(body, grid_spec=pltpu.PrefetchScalarGridSpec(num_scalar_pr...  145 us
    ppermute x16, waiting for transfers between devices, over_y(): return lax.ppermute(values, 'y', SWAP)  105 us
    ppermute x16, waiting for transfers between devices, over_x(): return lax.ppermute(values, 'x', SWAP)  52.9 us
    dot_general x4, matrix products, mat_rows(): lax.dot_general(left, right, (((0,), (0,)), ((), ())), preferred_element_...  44.8 us
    ppermute x28, waiting for transfers between devices, send_pieces(): lax.ppermute(piece, PLANE, [(i, i ^ mask) for i in range(PARTS)])  31.3 us
    ppermute x28, starting transfers between devices, send_pieces(): lax.ppermute(piece, PLANE, [(i, i ^ mask) for i in range(PARTS)])  28.4 us
    ppermute x5, waiting for transfers between devices, doubled(): other = lax.ppermute(values, axis, perm)  21.5 us
    ppermute x16, starting transfers between devices, over_x(): return lax.ppermute(values, 'x', SWAP)  18.3 us
  transfers between devices with their start and end apart: 102, of which 40 were waited for; matrix products, arithmetic and copies ran while one was open for 22% of the time, Pallas kernels for 19%

profile of v5, /device:TPU:0, one launch (start us, length us, event | category | flops | bytes accessed | tf_op | source)
XLA Modules:
  0.0 626.1 jit_solution(11281630520249459625)
XLA Ops:
  8.0 3.4 reshape.307
  14.7 3.4 collective-permute-start.13
  43.4 11.6 %collective-permute-done.4.refs_2_ = bf16[256,2048]{1,0:T(8,128)(2,1)} collective-permute-done((bf16[256,2048]{1,0:T(8,128)(2,1)S(1)}, bf16[256,2048]{1,0:T(8,128)(2,1)}, u32[]{:S(2)}, u32[]{:S(2)}) %collective-permute-start.4) | collective-permute-done | bytes 1048608 | tf_op jit(solution)/shard_map/ppermute | solution.py:47
  61.6 18.5 %collective-permute-done.1 = bf16[2,512]{1,0:T(2,128)(2,1)S(1)} collective-permute-done((bf16[2,512]{1,0:T(2,128)(2,1)S(1)}, bf16[2,512]{1,0:T(2,128)(2,1)S(1)}, u32[]{:S(2)}, u32[]{:S(2)}) %collective-permute-start.1) | collective-permute-done | bytes 2080 | tf_op jit(solution)/shard_map/ppermute | solution.py:181
  94.0 4.1 collective-permute-done.19.refs_4_
  105.8 14.8 %collective-permute-done.24.refs_7_ = bf16[256,2048]{1,0:T(8,128)(2,1)} collective-permute-done((bf16[256,2048]{1,0:T(8,128)(2,1)}, bf16[256,2048]{1,0:T(8,128)(2,1)}, u32[]{:S(2)}, u32[]{:S(2)}) %collective-permute-start.24) | collective-permute-done | bytes 1048608 | tf_op jit(solution)/shard_map/ppermute | solution.py:47
  135.5 19.7 %shard_map.231 = (bf16[2048,2048]{1,0:T(8,128)(2,1)}, bf16[2048,768]{1,0:T(8,128)(2,1)}, bf16[2048,256]{1,0:T(8,128)(2,1)}, bf16[1024,2048]{1,0:T(8,128)(2,1)}) custom-call(s32[8,6]{1,0:T(8,128)} %copy.110.marks_ref, bf16[256,2048]{1,0:T(8,128)(2,1)} %collective-permute-done.25.refs_0_, bf16[256,2048]{1,0:T(8,128)(2,1)} %copy-done.21, ...), custom_call_target="tpu_custom_call" | custom-call | flops 1 | bytes 1 | tf_op jit(solution)/shard_map/pallas_call | solution.py:537
  156.1 19.4 %shard_map.232 = (bf16[2048,2048]{1,0:T(8,128)(2,1)}, bf16[2048,768]{1,0:T(8,128)(2,1)}, bf16[2048,256]{1,0:T(8,128)(2,1)}, bf16[1024,2048]{1,0:T(8,128)(2,1)}) custom-call(s32[8,6]{1,0:T(8,128)} %copy.114.marks_ref, bf16[256,2048]{1,0:T(8,128)(2,1)} %refs_0_.1, ...), custom_call_target="tpu_custom_call", output_to_operand_aliasing={{0}: (14, {}), {1}: (15, {}), {2}: (16, {})} | custom-call | flops 1 | bytes 1 | tf_op jit(solution)/shard_map/pallas_call | solution.py:537
  179.7 13.1 %collective-permute-done.35 = bf16[128,2048]{1,0:T(8,128)(2,1)S(1)} collective-permute-done((bf16[128,2048]{1,0:T(8,128)(2,1)S(1)}, bf16[128,2048]{1,0:T(8,128)(2,1)S(1)}, u32[]{:S(2)}, u32[]{:S(2)}) %collective-permute-start.35) | collective-permute-done | bytes 524320 | tf_op jit(solution)/shard_map/ppermute | solution.py:43
  197.8 22.1 %collective-permute-done.36 = bf16[256,2048]{1,0:T(8,128)(2,1)} collective-permute-done((bf16[256,2048]{1,0:T(8,128)(2,1)S(1)}, bf16[256,2048]{1,0:T(8,128)(2,1)}, u32[]{:S(2)}, u32[]{:S(2)}) %collective-permute-start.36) | collective-permute-done | bytes 1048608 | tf_op jit(solution)/shard_map/ppermute | solution.py:47
  228.0 19.9 %collective-permute-done.38.refs_2_ = bf16[256,2048]{1,0:T(8,128)(2,1)S(1)} collective-permute-done((bf16[256,2048]{1,0:T(8,128)(2,1)S(1)}, bf16[256,2048]{1,0:T(8,128)(2,1)S(1)}, u32[]{:S(2)}, u32[]{:S(2)}) %collective-permute-start.38) | collective-permute-done | bytes 1048608 | tf_op jit(solution)/shard_map/ppermute | solution.py:47
  253.1 10.6 %collective-permute-done.39.refs_3_ = bf16[128,2048]{1,0:T(8,128)(2,1)S(1)} collective-permute-done((bf16[128,2048]{1,0:T(8,128)(2,1)S(1)}, bf16[128,2048]{1,0:T(8,128)(2,1)S(1)}, u32[]{:S(2)}, u32[]{:S(2)}) %collective-permute-start.39) | collective-permute-done | bytes 524320 | tf_op jit(solution)/shard_map/ppermute | solution.py:43
  268.2 5.1 all-gather.8.cloned.1.call-done
  273.2 30.0 %shard_map.233 = (bf16[2048,2048]{1,0:T(8,128)(2,1)}, bf16[2048,2048]{1,0:T(8,128)(2,1)}, bf16[2048,704]{1,0:T(8,128)(2,1)}, bf16[2048,1408]{1,0:T(8,128)(2,1)},...) custom-call(bf16[256,2048]{1,0:T(8,128)(2,1)} %copy-done.25, bf16[256,2048]{1,0:T(8,128)(2,1)} %copy-done.27, ...), custom_call_target="tpu_custom_call" | custom-call | flops 1 | bytes 1 | tf_op jit(solution)/shard_map/pallas_call | solution.py:537
  303.3 30.1 %shard_map.234 = (bf16[2048,2048]{1,0:T(8,128)(2,1)}, bf16[2048,2048]{1,0:T(8,128)(2,1)}, bf16[2048,704]{1,0:T(8,128)(2,1)}, bf16[2048,1408]{1,0:T(8,128)(2,1)},...) custom-call(bf16[256,2048]{1,0:T(8,128)(2,1)} %copy-done.11, ...), custom_call_target="tpu_custom_call", output_to_operand_aliasing={{0}: (11, {}), {1}: (12, {}), {2}: (13, {}), {3}: (14, {})} | custom-call | flops 1 | bytes 1 | tf_op jit(solution)/shard_map/pallas_call | solution.py:537
  341.4 10.0 %convolution_convert_fusion.2 = bf16[2048,704]{0,1:T(8,128)(2,1)} fusion(bf16[2048,2048]{1,0:T(8,128)(2,1)} %get-tuple-element.89, bf16[2048,704]{1,0:T(8,128)(2,1)S(1)} %copy-done.14), kind=kOutput, calls=%fused_computation.3 | convolution fusion | flops 5907021824 | bytes 14155776 | tf_op jit(solution)/shard_map/dot_general | solution.py:31
  354.2 3.7 add_convert_fusion.14
  362.6 17.2 %convolution_convert_fusion = bf16[2048,1408]{1,0:T(8,128)(2,1)} fusion(bf16[2048,2048]{1,0:T(8,128)(2,1)S(1)} %copy-done.4, bf16[2048,1408]{1,0:T(8,128)(2,1)} %get-tuple-element.95), kind=kOutput, calls=%fused_computation | convolution fusion | flops 11814043648 | bytes 19922944 | tf_op jit(solution)/shard_map/dot_general | solution.py:31
  379.8 4.3 collective-permute-done.54
  386.5 3.5 multiply_reduce_fusion
  394.1 24.3 %collective-permute-done.62.refs_2_ = bf16[256,2048]{1,0:T(8,128)(2,1)} collective-permute-done((bf16[256,2048]{1,0:T(8,128)(2,1)}, bf16[256,2048]{1,0:T(8,128)(2,1)}, u32[]{:S(2)}, u32[]{:S(2)}) %collective-permute-start.62) | collective-permute-done | bytes 1048608 | tf_op jit(solution)/shard_map/ppermute | solution.py:47
  423.3 9.8 %collective-permute-done.64.refs_3_ = bf16[128,2048]{1,0:T(8,128)(2,1)S(1)} collective-permute-done((bf16[128,2048]{1,0:T(8,128)(2,1)S(1)}, bf16[128,2048]{1,0:T(8,128)(2,1)S(1)}, u32[]{:S(2)}, u32[]{:S(2)}) %collective-permute-start.64) | collective-permute-done | bytes 524320 | tf_op jit(solution)/shard_map/ppermute | solution.py:43
  442.1 23.9 %shard_map.235 = (bf16[2048,2048]{1,0:T(8,128)(2,1)}, bf16[2048,768]{1,0:T(8,128)(2,1)}, bf16[512,2048]{1,0:T(8,128)(2,1)}, bf16[512,2048]{1,0:T(8,128)(2,1)}) custom-call(s32[8,6]{1,0:T(8,128)} %copy.118.marks_ref, bf16[256,2048]{1,0:T(8,128)(2,1)} %collective-permute-done.59.refs_0_, bf16[256,2048]{1,0:T(8,128)(2,1)} %collective-permute-done.61.refs_1_, ...), custom_call_target="tpu_custom_call" | custom-call | flops 27917287424 | bytes 1 | tf_op jit(solution)/shard_map/pallas_call | solution.py:537
  474.9 22.3 %shard_map.236 = (bf16[2048,2048]{1,0:T(8,128)(2,1)}, bf16[2048,768]{1,0:T(8,128)(2,1)}, bf16[512,2048]{1,0:T(8,128)(2,1)}, bf16[512,2048]{1,0:T(8,128)(2,1)}) custom-call(s32[8,6]{1,0:T(8,128)} %copy.122.marks_ref, bf16[256,2048]{1,0:T(8,128)(2,1)} %get-tuple-element.139.refs_0_, ...), custom_call_target="tpu_custom_call", output_to_operand_aliasing={{0}: (12, {}), {1}: (13, {})} | custom-call | flops 27917287424 | bytes 1 | tf_op jit(solution)/shard_map/pallas_call | solution.py:537
  498.2 4.2 select_convert_fusion
  507.8 10.8 %convolution_convert_fusion.1 = bf16[2048,768]{1,0:T(8,128)(2,1)} fusion(bf16[2048,2048]{1,0:T(8,128)(2,1)} %get-tuple-element.113, bf16[2048,768]{1,0:T(8,128)(2,1)S(1)} %copy-done.12), kind=kOutput, calls=%fused_computation.2 | convolution fusion | flops 6444023808 | bytes 14680064 | tf_op jit(solution)/shard_map/dot_general | solution.py:31
  527.9 6.9 %convolution_convert_fusion.3 = bf16[256,2048]{1,0:T(8,128)(2,1)} fusion(bf16[2048,256]{1,0:T(8,128)(2,1)S(1)} %copy-done.5, bf16[2048,2048]{1,0:T(8,128)(2,1)} %get-tuple-element.119), kind=kOutput, calls=%fused_computation.7 | convolution fusion | flops 2148007936 | bytes 10485760 | tf_op jit(solution)/shard_map/dot_general | solution.py:31
  534.7 11.1 %collective-permute-done.74 = bf16[256,2048]{1,0:T(8,128)(2,1)} collective-permute-done((bf16[256,2048]{1,0:T(8,128)(2,1)S(1)}, bf16[256,2048]{1,0:T(8,128)(2,1)}, u32[]{:S(2)}, u32[]{:S(2)}) %collective-permute-start.74) | collective-permute-done | bytes 1048608 | tf_op jit(solution)/shard_map/ppermute | solution.py:43
  545.9 4.2 collective-permute-done.75
  550.0 4.9 fusion.10
  566.4 5.0 collective-permute-done.84
  588.7 17.9 %collective-permute-done.92.refs_5_ = bf16[64,2112]{1,0:T(8,128)(2,1)S(1)} collective-permute-done((bf16[64,2112]{1,0:T(8,128)(2,1)S(1)}, bf16[64,2112]{1,0:T(8,128)(2,1)S(1)}, u32[]{:S(2)}, u32[]{:S(2)}) %collective-permute-start.92) | collective-permute-done | bytes 270368 | tf_op jit(solution)/shard_map/ppermute | solution.py:146
  (445 shorter events, 200.1 us)
Async XLA Ops:
  7.2 127.0 %all-gather.6.cloned.1.call-start = ((), (), s32[]{:S(2)}) async-start(), calls=%async_computation.5 | async-start | bytes 1310720 | tf_op jit(solution)/shard_map/all_gather | solution.py:55
  7.9 126.3 %all-gather.4.cloned.1.call-start = ((), (), s32[]{:S(2)}) async-start(), calls=%async_computation.4 | async-start | bytes 3932160 | tf_op jit(solution)/shard_map/all_gather | solution.py:55
  29.6 243.7 %all-gather.8.cloned.1.call-start = ((), (), s32[]{:S(2)}) async-start(), calls=%async_computation.6 | async-start | bytes 11796480 | tf_op jit(solution)/shard_map/all_gather | solution.py:55
  29.6 25.4 %collective-permute-start.4 = (bf16[256,2048]{1,0:T(8,128)(2,1)S(1)}, bf16[256,2048]{1,0:T(8,128)(2,1)}, u32[]{:S(2)}, u32[]{:S(2)}) collective-permute-start(bf16[256,2048]{1,0:T(8,128)(2,1)S(1)} %copy-done), channel_id=1, source_target_pairs={{0,4},{4,0},{1,5},{5,1},{2,6},{6,2},{3,7},{7,3},{8,12},{12,8},{9,1... | collective-permute-start | bytes 3145736 | tf_op jit(solution)/shard_map/ppermute | solution.py:47
  31.1 26.1 %collective-permute-start.3 = (bf16[256,2048]{1,0:T(8,128)(2,1)S(1)}, bf16[256,2048]{1,0:T(8,128)(2,1)}, u32[]{:S(2)}, u32[]{:S(2)}) collective-permute-start(bf16[256,2048]{1,0:T(8,128)(2,1)S(1)} %copy-done), channel_id=1, source_target_pairs={{0,2},{2,0},{1,3},{3,1},{4,6},{6,4},{5,7},{7,5},{8,10},{10,8},{9,1... | collective-permute-start | bytes 3145736 | tf_op jit(solution)/shard_map/ppermute | solution.py:43
  33.5 27.5 %collective-permute-start = (bf16[1,512]{1,0:T(2,128)(2,1)S(1)}, bf16[1,512]{1,0:T(2,128)(2,1)S(1)}, u32[]{:S(2)}, u32[]{:S(2)}) collective-permute-start(bf16[1,512]{1,0:T(2,128)(2,1)S(1)} %broadcast_in_dim.120), channel_id=1, source_target_pairs={{0,1},{1,0},{2,3},{3,2},{4,5},{5,4},{6,7},{7,6},{8,9},{9,8},{10,11... | collective-permute-start | bytes 3080 | tf_op jit(solution)/shard_map/ppermute | solution.py:181
  38.8 45.0 %collective-permute-start.22 = (bf16[3,64,704]{2,1,0:T(8,128)(2,1)S(1)}, bf16[3,64,704]{2,1,0:T(8,128)(2,1)S(1)}, u32[]{:S(2)}, u32[]{:S(2)}) collective-permute-start(bf16[3,64,704]{2,1,0:T(8,128)(2,1)S(1)} %get-tuple-element.168), channel_id=1, source_target_pairs={{0,7},{1,6},{2,5},{3,4},{4,3},{5,2},{6,1},{7,0},{8,15},{9,14},{10,... | collective-permute-start | bytes 811016 | tf_op jit(solution)/shard_map/ppermute | solution.py:146
  39.4 52.0 %collective-permute-start.21 = (bf16[3,64,704]{2,1,0:T(8,128)(2,1)}, bf16[3,64,704]{2,1,0:T(8,128)(2,1)S(1)}, u32[]{:S(2)}, u32[]{:S(2)}) collective-permute-start(bf16[3,64,704]{2,1,0:T(8,128)(2,1)} %get-tuple-element.169), channel_id=1, source_target_pairs={{0,6},{1,7},{2,4},{3,5},{4,2},{5,3},{6,0},{7,1},{8,14},{9,15},{10,... | collective-permute-start | bytes 811016 | tf_op jit(solution)/shard_map/ppermute | solution.py:146
  58.3 26.1 %collective-permute-start.5 = (bf16[128,2048]{1,0:T(8,128)(2,1)}, bf16[128,2048]{1,0:T(8,128)(2,1)}, u32[]{:S(2)}, u32[]{:S(2)}) collective-permute-start(bf16[128,2048]{1,0:T(8,128)(2,1)} %slice.369), channel_id=1, source_target_pairs={{0,2},{2,0},{1,3},{3,1},{4,6},{6,4},{5,7},{7,5},{8,10},{10,8},{9,1... | collective-permute-start | bytes 1572872 | tf_op jit(solution)/shard_map/ppermute | solution.py:43
  59.9 26.9 %collective-permute-start.6 = (bf16[128,2048]{1,0:T(8,128)(2,1)S(1)}, bf16[128,2048]{1,0:T(8,128)(2,1)}, u32[]{:S(2)}, u32[]{:S(2)}) collective-permute-start(bf16[128,2048]{1,0:T(8,128)(2,1)S(1)} %slice.370), channel_id=1, source_target_pairs={{0,4},{4,0},{1,5},{5,1},{2,6},{6,2},{3,7},{7,3},{8,12},{12,8},{9,1... | collective-permute-start | bytes 1572872 | tf_op jit(solution)/shard_map/ppermute | solution.py:47
  93.3 27.3 %collective-permute-start.24 = (bf16[256,2048]{1,0:T(8,128)(2,1)}, bf16[256,2048]{1,0:T(8,128)(2,1)}, u32[]{:S(2)}, u32[]{:S(2)}) collective-permute-start(bf16[256,2048]{1,0:T(8,128)(2,1)} %fusion.12.refs_5_), channel_id=1, source_target_pairs={{0,4},{4,0},{1,5},{5,1},{2,6},{6,2},{3,7},{7,3},{8,12},{12,8},{9,1... | collective-permute-start | bytes 3145736 | tf_op jit(solution)/shard_map/ppermute | solution.py:47
  98.0 30.1 %collective-permute-start.25 = (bf16[256,2048]{1,0:T(8,128)(2,1)S(1)}, bf16[256,2048]{1,0:T(8,128)(2,1)}, u32[]{:S(2)}, u32[]{:S(2)}) collective-permute-start(bf16[256,2048]{1,0:T(8,128)(2,1)S(1)} %copy-done), channel_id=1, source_target_pairs={{0,1},{1,0},{2,3},{3,2},{4,5},{5,4},{6,7},{7,6},{8,9},{9,8},{10,11... | collective-permute-start | bytes 3145736 | tf_op jit(solution)/shard_map/ppermute | solution.py:51
  99.8 29.8 %collective-permute-start.27 = (bf16[256,2048]{1,0:T(8,128)(2,1)}, bf16[256,2048]{1,0:T(8,128)(2,1)}, u32[]{:S(2)}, u32[]{:S(2)}) collective-permute-start(bf16[256,2048]{1,0:T(8,128)(2,1)} %collective-permute-done.4.refs_2_), channel_id=1, source_target_pairs={{0,1},{1,0},{2,3},{3,2},{4,5},{5,4},{6,7},{7,6},{8,9},{9,8},{10,11... | collective-permute-start | bytes 3145736 | tf_op jit(solution)/shard_map/ppermute | solution.py:51
  100.9 24.9 %collective-permute-start.23 = (bf16[256,2048]{1,0:T(8,128)(2,1)}, bf16[256,2048]{1,0:T(8,128)(2,1)}, u32[]{:S(2)}, u32[]{:S(2)}) collective-permute-start(bf16[256,2048]{1,0:T(8,128)(2,1)} %fusion.12.refs_5_), channel_id=1, source_target_pairs={{0,2},{2,0},{1,3},{3,1},{4,6},{6,4},{5,7},{7,5},{8,10},{10,8},{9,1... | collective-permute-start | bytes 3145736 | tf_op jit(solution)/shard_map/ppermute | solution.py:43
  105.1 334.0 %reduce-scatter.5.cloned.1.call-start = ((), (), s32[]{:S(2)}) async-start(), calls=%async_computation.7 | async-start | bytes 3604480 | tf_op jit(solution)/shard_map/reduce_scatter | solution.py:59
  105.5 28.6 %collective-permute-start.26 = (bf16[256,2048]{1,0:T(8,128)(2,1)}, bf16[256,2048]{1,0:T(8,128)(2,1)S(1)}, u32[]{:S(2)}, u32[]{:S(2)}) collective-permute-start(bf16[256,2048]{1,0:T(8,128)(2,1)} %collective-permute-done.3.refs_1_), channel_id=1, source_target_pairs={{0,1},{1,0},{2,3},{3,2},{4,5},{5,4},{6,7},{7,6},{8,9},{9,8},{10,11... | collective-permute-start | bytes 3145736 | tf_op jit(solution)/shard_map/ppermute | solution.py:51
  128.1 27.0 %collective-permute-start.30 = (bf16[128,2048]{1,0:T(8,128)(2,1)}, bf16[128,2048]{1,0:T(8,128)(2,1)S(1)}, u32[]{:S(2)}, u32[]{:S(2)}) collective-permute-start(bf16[128,2048]{1,0:T(8,128)(2,1)} %slice.374), channel_id=1, source_target_pairs={{0,2},{2,0},{1,3},{3,1},{4,6},{6,4},{5,7},{7,5},{8,10},{10,8},{9,1... | collective-permute-start | bytes 1572872 | tf_op jit(solution)/shard_map/ppermute | solution.py:43
  129.6 25.5 %collective-permute-start.31 = (bf16[128,2048]{1,0:T(8,128)(2,1)}, bf16[128,2048]{1,0:T(8,128)(2,1)S(1)}, u32[]{:S(2)}, u32[]{:S(2)}) collective-permute-start(bf16[128,2048]{1,0:T(8,128)(2,1)} %slice.375), channel_id=1, source_target_pairs={{0,4},{4,0},{1,5},{5,1},{2,6},{6,2},{3,7},{7,3},{8,12},{12,8},{9,1... | collective-permute-start | bytes 1572872 | tf_op jit(solution)/shard_map/ppermute | solution.py:47
  303.2 30.2 %collective-permute-start.51 = (bf16[1024,2048]{1,0:T(8,128)(2,1)}, bf16[1024,2048]{1,0:T(8,128)(2,1)S(1)}, u32[]{:S(2)}, u32[]{:S(2)}) collective-permute-start(bf16[1024,2048]{1,0:T(8,128)(2,1)} %get-tuple-element.87), channel_id=1, source_target_pairs={{0,1},{1,0},{2,3},{3,2},{4,5},{5,4},{6,7},{7,6},{8,9},{9,8},{10,11... | collective-permute-start | bytes 12582920 | tf_op jit(solution)/shard_map/ppermute | solution.py:51
  351.4 176.5 %reduce-scatter.7.cloned.1.call-start = ((), (), s32[]{:S(2)}) async-start(), calls=%async_computation.8 | async-start | bytes 7208960 | tf_op jit(solution)/shard_map/reduce_scatter | solution.py:59
  359.0 25.0 %collective-permute-start.54 = (bf16[256,2048]{1,0:T(8,128)(2,1)}, bf16[256,2048]{1,0:T(8,128)(2,1)}, u32[]{:S(2)}, u32[]{:S(2)}) collective-permute-start(bf16[256,2048]{1,0:T(8,128)(2,1)} %pad_maximum_fusion.3), channel_id=1, source_target_pairs={{0,2},{2,0},{1,3},{3,1},{4,6},{6,4},{5,7},{7,5},{8,10},{10,8},{9,1... | collective-permute-start | bytes 3145736 | tf_op jit(solution)/shard_map/ppermute | solution.py:43
  392.5 43.0 %collective-permute-start.56 = (bf16[1024,2048]{1,0:T(8,128)(2,1)}, bf16[1024,2048]{1,0:T(8,128)(2,1)}, u32[]{:S(2)}, u32[]{:S(2)}) collective-permute-start(bf16[1024,2048]{1,0:T(8,128)(2,1)} %get-tuple-element.98), channel_id=1, source_target_pairs={{0,1},{1,0},{2,3},{3,2},{4,5},{5,4},{6,7},{7,6},{8,9},{9,8},{10,11... | collective-permute-start | bytes 12582920 | tf_op jit(solution)/shard_map/ppermute | solution.py:51
  392.5 25.9 %collective-permute-start.62 = (bf16[256,2048]{1,0:T(8,128)(2,1)}, bf16[256,2048]{1,0:T(8,128)(2,1)}, u32[]{:S(2)}, u32[]{:S(2)}) collective-permute-start(bf16[256,2048]{1,0:T(8,128)(2,1)} %get-tuple-element.139.refs_0_), channel_id=1, source_target_pairs={{0,4},{4,0},{1,5},{5,1},{2,6},{6,2},{3,7},{7,3},{8,12},{12,8},{9,1... | collective-permute-start | bytes 3145736 | tf_op jit(solution)/shard_map/ppermute | solution.py:47
  393.3 26.8 %collective-permute-start.60 = (bf16[256,2048]{1,0:T(8,128)(2,1)}, bf16[256,2048]{1,0:T(8,128)(2,1)}, u32[]{:S(2)}, u32[]{:S(2)}) collective-permute-start(bf16[256,2048]{1,0:T(8,128)(2,1)} %get-tuple-element.139.refs_0_), channel_id=1, source_target_pairs={{0,2},{2,0},{1,3},{3,1},{4,6},{6,4},{5,7},{7,5},{8,10},{10,8},{9,1... | collective-permute-start | bytes 3145736 | tf_op jit(solution)/shard_map/ppermute | solution.py:43
  393.9 182.9 %reduce-scatter.9.cloned.1.call-start = ((), (), s32[]{:S(2)}) async-start(), calls=%async_computation.9 | async-start | bytes 3932160 | tf_op jit(solution)/shard_map/reduce_scatter | solution.py:59
  439.7 26.8 %collective-permute-start.58 = (bf16[128,2048]{1,0:T(8,128)(2,1)}, bf16[128,2048]{1,0:T(8,128)(2,1)S(1)}, u32[]{:S(2)}, u32[]{:S(2)}) collective-permute-start(bf16[128,2048]{1,0:T(8,128)(2,1)} %get-tuple-element.148), channel_id=1, source_target_pairs={{0,4},{4,0},{1,5},{5,1},{2,6},{6,2},{3,7},{7,3},{8,12},{12,8},{9,1... | collective-permute-start | bytes 1572872 | tf_op jit(solution)/shard_map/ppermute | solution.py:47
  440.6 26.7 %collective-permute-start.57 = (bf16[128,2048]{1,0:T(8,128)(2,1)}, bf16[128,2048]{1,0:T(8,128)(2,1)}, u32[]{:S(2)}, u32[]{:S(2)}) collective-permute-start(bf16[128,2048]{1,0:T(8,128)(2,1)} %get-tuple-element.149), channel_id=1, source_target_pairs={{0,2},{2,0},{1,3},{3,1},{4,6},{6,4},{5,7},{7,5},{8,10},{10,8},{9,1... | collective-permute-start | bytes 1572872 | tf_op jit(solution)/shard_map/ppermute | solution.py:43
  465.9 53.2 %collective-permute-start.70 = (bf16[512,2048]{1,0:T(8,128)(2,1)}, bf16[512,2048]{1,0:T(8,128)(2,1)}, u32[]{:S(2)}, u32[]{:S(2)}) collective-permute-start(bf16[512,2048]{1,0:T(8,128)(2,1)} %get-tuple-element.111), channel_id=1, source_target_pairs={{0,1},{1,0},{2,3},{3,2},{4,5},{5,4},{6,7},{7,6},{8,9},{9,8},{10,11... | collective-permute-start | bytes 6291464 | tf_op jit(solution)/shard_map/ppermute | solution.py:51
  466.0 36.4 %collective-permute-start.71 = (bf16[512,2048]{1,0:T(8,128)(2,1)}, bf16[512,2048]{1,0:T(8,128)(2,1)}, u32[]{:S(2)}, u32[]{:S(2)}) collective-permute-start(bf16[512,2048]{1,0:T(8,128)(2,1)} %get-tuple-element.101), channel_id=1, source_target_pairs={{0,1},{1,0},{2,3},{3,2},{4,5},{5,4},{6,7},{7,6},{8,9},{9,8},{10,11... | collective-permute-start | bytes 6291464 | tf_op jit(solution)/shard_map/ppermute | solution.py:51
  471.3 25.9 %collective-permute-start.68 = (bf16[256,2048]{1,0:T(8,128)(2,1)}, bf16[256,2048]{1,0:T(8,128)(2,1)}, u32[]{:S(2)}, u32[]{:S(2)}) collective-permute-start(bf16[256,2048]{1,0:T(8,128)(2,1)} %pad_maximum_fusion.5), channel_id=1, source_target_pairs={{0,2},{2,0},{1,3},{3,1},{4,6},{6,4},{5,7},{7,5},{8,10},{10,8},{9,1... | collective-permute-start | bytes 3145736 | tf_op jit(solution)/shard_map/ppermute | solution.py:43
  473.0 25.2 %collective-permute-start.69 = (bf16[256,2048]{1,0:T(8,128)(2,1)}, bf16[256,2048]{1,0:T(8,128)(2,1)}, u32[]{:S(2)}, u32[]{:S(2)}) collective-permute-start(bf16[256,2048]{1,0:T(8,128)(2,1)} %pad_maximum_fusion.6), channel_id=1, source_target_pairs={{0,4},{4,0},{1,5},{5,1},{2,6},{6,2},{3,7},{7,3},{8,12},{12,8},{9,1... | collective-permute-start | bytes 3145736 | tf_op jit(solution)/shard_map/ppermute | solution.py:47
  518.6 98.4 %reduce-scatter.11.cloned.1.call-start = ((), (), s32[]{:S(2)}) async-start(), calls=%async_computation.10 | async-start | bytes 1310720 | tf_op jit(solution)/shard_map/reduce_scatter | solution.py:59
  (123 other events, 1476.3 us)
Sparse Core Ops, SparseCore 0:
  9.6 30.6 all-gather.5
  42.4 63.0 all-gather.3
  107.1 166.1 all-gather.7
  351.5 52.5 reduce-scatter.4
  406.2 102.0 reduce-scatter.6
  518.7 58.0 reduce-scatter.8
  579.1 27.1 reduce-scatter.10

commit v6 on v5

--- a/solution.py
+++ b/solution.py
@@ -11,6 +11,7 @@
 ROT = 16
 BLOCK = 128
 PARTS = 8
+CHIPS = 4
 LINE = 4
 GROUPS = 4
 
@@ -63,18 +64,29 @@
     return lax.optimization_barrier((values, *earlier))[0]
 
 
-def gather_plane(own, *earlier):
-    half = own.shape[0] // 2
-    from_x = over_x(own)
-    from_y = over_y(own)
-    low, high = from_y[:half], from_x[half:]
+def gather_plane(values, *earlier):
+    half = values.shape[0] // 2
+    low, high = values[:half], values[half:]
+    y_low, x_high = over_y(low), over_x(high)
+    x_low, y_high = over_x(low), over_y(high)
+    to_x, to_y = y_low, x_high
     if earlier:
-        low, high, *_ = lax.optimization_barrier((low, high, *earlier))
-    line = [own, from_x, from_y, over_x(low), over_y(high)]
+        to_x, to_y, *_ = lax.optimization_barrier((to_x, to_y, *earlier))
+    line = [low, high, x_low, x_high, y_low, y_high, over_x(to_x), over_y(to_y)]
     return line, [over_c(part) for part in line]
 
 
-def scatter_plane(kept, sent, rows, first=None, second=None):
+def gather_whole(values, *earlier):
+    half = values.shape[0] // 2
+    from_x, from_y = over_x(values), over_y(values)
+    to_x, to_y = from_y[:half], from_x[half:]
+    if earlier:
+        to_x, to_y, *_ = lax.optimization_barrier((to_x, to_y, *earlier))
+    line = [values, from_x, from_y, over_x(to_x), over_y(to_y)]
+    return line, [over_c(part) for part in line]
+
+
+def scatter_plane(kept, sent, rows, first=None, second=None, also=()):
     half = rows // 2
     kept, sent = (parts if isinstance(parts, list) else [parts] for parts in (kept, sent))
     came = [over_c(part) for part in sent]
@@ -93,7 +105,7 @@
         done.append(first(far_low, far_high))
     low, high = over_x(far_low), over_y(far_high)
     if done:
-        low, high, _ = lax.optimization_barrier((low, high, done[0]))
+        low, high, *_ = lax.optimization_barrier((low, high, done[0], *also))
     near_x = jnp.concatenate(
         [joined(rows, rows + half), joined(rows + half, 2 * rows) + high.astype(f32)], axis=0
     ).astype(bf16)
@@ -110,9 +122,13 @@
     return (total, *done) if done else total
 
 
+def members(refs):
+    return [(2 * chip + core, refs[chip].at[core]) for chip in range(CHIPS) for core in (0, 1)]
+
+
 def place_pieces(me_ref, *refs):
-    result = refs[PARTS]
-    for mask, piece in enumerate(refs[:PARTS]):
+    result = refs[CHIPS]
+    for mask, piece in members(refs):
         there = jnp.bitwise_xor(me_ref[0], mask)
         if len(result.shape) == 4:
             for index in range(result.shape[0]):
@@ -122,8 +138,8 @@
 
 
 def place_columns(chunks, me_ref, *refs):
-    results, held = refs[PARTS:-1], refs[-1]
-    for mask, piece in enumerate(refs[:PARTS]):
+    results, held = refs[CHIPS:-1], refs[-1]
+    for mask, piece in members(refs):
         held[jnp.bitwise_xor(me_ref[0], mask)] = piece[...]
     offset = 0
     for result in results:
@@ -135,45 +151,52 @@
             offset += size
 
 
-def pieces_for(blocks, me, axis=0):
-    return [
-        lax.dynamic_index_in_dim(blocks, me ^ mask, axis, keepdims=False) for mask in range(PARTS)
-    ]
-
-
-def send_pieces(pieces):
-    return [
-        lax.ppermute(piece, PLANE, [(i, i ^ mask) for i in range(PARTS)]) if mask else piece
-        for mask, piece in enumerate(pieces)
-    ]
-
-
-def collect(body, pieces, me, shapes, scratch=()):
-    pieces = send_pieces(pieces)
+def send_pieces(block, me):
+    chip, core = me // 2, me % 2
+    to_other = jnp.stack([block((chip ^ away) * 2 + 1 - core) for away in range(CHIPS)])
+    came = over_c(to_other)
+    pairs = []
+    for away in range(CHIPS):
+        pair = jnp.stack([block((chip ^ away) * 2 + core), came[away]])
+        if away:
+            pair = lax.ppermute(pair, ("y", "x"), [(i, i ^ away) for i in range(CHIPS)])
+        pairs.append(pair)
+    return pairs
+
+
+def block_of(*arrays, axis=0):
+    def block(index):
+        parts = [lax.dynamic_index_in_dim(a, index, axis, keepdims=False) for a in arrays]
+        return parts[0] if len(parts) == 1 else jnp.concatenate(parts, axis=-1)
+
+    return block
+
+
+def collect(body, pairs, me, shapes, scratch=()):
     whole = pl.BlockSpec(memory_space=pltpu.VMEM)
-    size = 3 * pieces[0].dtype.itemsize * PARTS * pieces[0].size
+    size = 3 * pairs[0].dtype.itemsize * CHIPS * pairs[0].size
     return pl.pallas_call(
         body,
-        in_specs=[pl.BlockSpec(memory_space=pltpu.SMEM)] + [whole] * PARTS,
+        in_specs=[pl.BlockSpec(memory_space=pltpu.SMEM)] + [whole] * CHIPS,
         out_specs=[whole] * len(shapes),
         scratch_shapes=scratch,
         compiler_params=pltpu.CompilerParams(vmem_limit_bytes=24 * 1024 * 1024),
         out_shape=shapes,
         cost_estimate=pl.CostEstimate(flops=0, bytes_accessed=size, transcendentals=0),
-    )(me.astype(jnp.int32).reshape(1), *pieces)
-
-
-def exchange(pieces, me, shape):
-    return collect(place_pieces, pieces, me, [jax.ShapeDtypeStruct(shape, pieces[0].dtype)])[0]
-
-
-def exchange_columns(pieces, me, shapes, chunks=1):
+    )(me.astype(jnp.int32).reshape(1), *pairs)
+
+
+def exchange(pairs, me, shape):
+    return collect(place_pieces, pairs, me, [jax.ShapeDtypeStruct(shape, pairs[0].dtype)])[0]
+
+
+def exchange_columns(pairs, me, shapes, chunks=1):
     return collect(
         functools.partial(place_columns, chunks),
-        pieces,
+        pairs,
         me,
         [jax.ShapeDtypeStruct(shape, f32) for shape in shapes],
-        [pltpu.VMEM((PARTS,) + pieces[0].shape, pieces[0].dtype)],
+        [pltpu.VMEM((PARTS,) + pairs[0].shape[1:], pairs[0].dtype)],
     )
 
 
@@ -248,9 +271,8 @@
     copies, offset = [], 0
     for index, piece in enumerate(pieces):
         size = piece.shape[0]
-        copies.append(
-            pltpu.make_async_copy(piece, target.at[pl.ds(offset, size)], sems.at[index])
-        )
+        copy = pltpu.make_async_copy(piece, target.at[pl.ds(offset, size)], sems.at[index])
+        copies.append((copy, offset))
         offset += size
     return copies
 
@@ -259,20 +281,19 @@
     @pl.when(step == 0)
     def _():
         for copies in lines:
-            for copy in copies:
+            for copy, _ in copies:
                 copy.start()
 
 
-def await_lines(step, lines, groups=1):
-    steps = GROUPS // groups
+def await_lines(step, steps, rows, lines):
     for index in range(steps):
 
         @pl.when(step == index)
         def _(index=index):
             for copies in lines:
-                last = None if index == steps - 1 else (index + 1) * groups
-                for copy in copies[index * groups : last]:
-                    copy.wait()
+                for copy, offset in copies:
+                    if offset // rows == index:
+                        copy.wait()
 
 
 def keep_rows(step, steps, pairs):
@@ -337,23 +358,36 @@
     ]
 
 
-def softmax_of(query, key_rows, allowed):
-    scores = mat_cols(query, key_rows) * HEAD ** (-0.5)
-    scores = jnp.where(allowed, scores, -1e30)
-    expo = jnp.exp(scores - jnp.max(scores, axis=1, keepdims=True))
-    return expo / jnp.sum(expo, axis=1, keepdims=True)
-
-
-def attend_forward(first, heads, rows, half, marks_ref, *refs):
-    tokens = refs[0:5]
-    qkv_weight, out_weight, gain, shift, bias, cos_ref, ahead_ref, behind_ref = refs[5:13]
-    refs = refs[13 if first else 16 :]
+def stacked(values, masks):
+    return jnp.concatenate([jnp.where(mask, values, 0) for mask in masks], axis=0)
+
+
+def of_heads(values, masks):
+    rows = values.shape[0] // len(masks)
+    result = jnp.zeros((rows, values.shape[1]), values.dtype)
+    for index, mask in enumerate(masks):
+        result = jnp.where(mask, values[index * rows : (index + 1) * rows], result)
+    return result
+
+
+def softmax_of(query_stack, key_rows, allowed):
+    rows = key_rows.shape[0]
+    scores = mat_cols(query_stack, key_rows).reshape(-1, rows, rows)
+    scores = jnp.where(allowed[None], scores, -1e30)
+    expo = jnp.exp(scores - jnp.max(scores, axis=2, keepdims=True))
+    return (expo * (1.0 / jnp.sum(expo, axis=2, keepdims=True))).reshape(-1, rows)
+
+
+def attend_forward(count, first, heads, rows, half, marks_ref, *refs):
+    tokens, refs = refs[:count], refs[count:]
+    qkv_weight, out_weight, gain, shift, bias, cos_ref, ahead_ref, behind_ref = refs[:8]
+    refs = refs[8 if first else 11 :]
     normed_ref, qkv_ref, mixed_ref, part_ref, token_rows, line_sems = refs
     step = pl.program_id(0)
     group = half * GROUPS + step
     line = line_copies(tokens, token_rows, line_sems)
     begin_lines(step, [line])
-    await_lines(step, [line])
+    await_lines(step, GROUPS, rows, [line])
     values = token_rows[pl.ds(pl.multiple_of(step * rows, rows), rows), :].astype(f32)
     centre = values - jnp.mean(values, axis=1, keepdims=True)
     inverse = lax.rsqrt(jnp.mean(centre * centre, axis=1, keepdims=True) + eps_norm)
@@ -369,18 +403,19 @@
     qkv_ref[:, width : 2 * width] = key_rows
     qkv_ref[:, 2 * width :] = value
     allowed = allowed_pairs(marks_ref, group, rows)
-    mixed = jnp.zeros((rows, width), f32)
-    for mask in head_masks((rows, width), heads):
-        probs = softmax_of(jnp.where(mask, query, 0), key_rows, allowed).astype(bf16)
-        mixed = jnp.where(mask, mat(probs, value), mixed)
-    mixed = mixed.astype(bf16)
+    masks = head_masks((rows, width), heads)
+    factor = jnp.asarray(HEAD ** (-0.5), bf16)
+    probs = softmax_of(stacked(query * factor, masks), key_rows, allowed).astype(bf16)
+    mixed = of_heads(mat(probs, value), masks).astype(bf16)
     mixed_ref[...] = mixed
     part_ref[...] = mat(mixed, out_weight[...]).astype(bf16)
 
 
-def feed_both(first, rows, half, *refs):
-    normed, grads, weights = refs[0:5], refs[5:10], refs[10]
-    refs = refs[11 if first else 15 :]
+def feed_both(count, first, rows, half, *refs):
+    normed, refs = refs[:count], refs[count:]
+    grads, refs = refs[:5], refs[5:]
+    weights = refs[0]
+    refs = refs[1 if first else 5 :]
     normed_ref, grad_ref, hidden_ref, both_ref, back_ref, down_ref = refs[:6]
     normed_rows, grad_rows, gate_weight, up_weight, down_weight = refs[6:11]
     normed_sems, grad_sems, weight_sems, keep_sems = refs[11:]
@@ -423,7 +458,7 @@
         for copy in loads[0]:
             copy.wait()
 
-    await_lines(step, lines, groups)
+    await_lines(step, steps, rows, lines)
     keep_rows(step, steps, kept)
     here = pl.ds(pl.multiple_of(step * rows, rows), rows)
     values = normed_rows[here, :]
@@ -435,13 +470,13 @@
             copy.wait()
 
     upward = mat(values, up_weight[...])
-    sigma = jax.nn.sigmoid(gate)
+    sigma = 0.5 + 0.5 * jnp.tanh(0.5 * gate)
     gated = gate * sigma
     hidden = (gated * upward).astype(bf16)
     hidden_ref[...] = hidden
     grad_low = grad_rows[here, :]
     grad_hidden = mat(grad_low, down_weight[...])
-    grad_gate = (grad_hidden * upward * sigma * (1.0 + gate * (1.0 - sigma))).astype(bf16)
+    grad_gate = (grad_hidden * upward * (sigma + gated * (1.0 - sigma))).astype(bf16)
     grad_up = (grad_hidden * gated).astype(bf16)
     columns = hidden.shape[1]
     both_ref[:, :columns] = grad_gate
@@ -454,9 +489,9 @@
 
 
 def attend_backward(first, heads, rows, half, marks_ref, *refs):
-    branch = refs[0:5]
-    saved, qkv_weight, out_weight, cos_ref, ahead_ref, behind_ref = refs[5:11]
-    refs = refs[11 if first else 13 :]
+    branch = refs[0:8]
+    saved, qkv_weight, out_weight, cos_ref, ahead_ref, behind_ref = refs[8:14]
+    refs = refs[14 if first else 16 :]
     branch_ref, grad_ref, early_ref, late_ref, branch_rows, line_sems, keep_sems = refs
     step = pl.program_id(0)
     group = half * GROUPS + step
@@ -464,33 +499,33 @@
     place = pl.ds(half * GROUPS * rows, GROUPS * rows)
     kept = [pltpu.make_async_copy(branch_rows, branch_ref.at[place], keep_sems.at[0])]
     begin_lines(step, [line])
-    await_lines(step, [line])
+    await_lines(step, GROUPS, rows, [line])
     keep_rows(step, GROUPS, kept)
     values = branch_rows[pl.ds(pl.multiple_of(step * rows, rows), rows), :]
     width = heads * HEAD
-    factor = HEAD ** (-0.5)
+    factor = jnp.asarray(HEAD ** (-0.5), bf16)
     grad_mixed = mat_cols(values, out_weight[...]).astype(bf16)
     query = saved[:, :width]
     key_rows = saved[:, width : 2 * width]
     value = saved[:, 2 * width :]
     allowed = allowed_pairs(marks_ref, group, rows)
-    zero = jnp.zeros((rows, width), f32)
-    grad_query, grad_key, grad_value = zero, zero, zero
-    for mask in head_masks((rows, width), heads):
-        probs = softmax_of(jnp.where(mask, query, 0), key_rows, allowed)
-        grad_probs = mat_cols(jnp.where(mask, grad_mixed, 0), value)
-        inner = jnp.sum(grad_probs * probs, axis=1, keepdims=True)
-        grad_scores = (probs * (grad_probs - inner)).astype(bf16)
-        grad_query = jnp.where(mask, mat(grad_scores, key_rows), grad_query)
-        grad_key = jnp.where(mask, mat_rows(grad_scores, query), grad_key)
-        grad_value = jnp.where(mask, mat_rows(probs.astype(bf16), grad_mixed), grad_value)
+    masks = head_masks((rows, width), heads)
+    query_stack = stacked(query * factor, masks)
+    mixed_stack = stacked(grad_mixed, masks)
+    probs = softmax_of(query_stack, key_rows, allowed)
+    grad_probs = mat_cols(mixed_stack, value)
+    inner = jnp.sum(grad_probs * probs, axis=1, keepdims=True)
+    grad_scores = (probs * (grad_probs - inner)).astype(bf16)
+    grad_query = of_heads(mat(grad_scores, key_rows * factor), masks)
+    grad_key = mat_rows(grad_scores, query_stack)
+    grad_value = mat_rows(probs.astype(bf16), mixed_stack)
     cosine, ahead, behind = (
         placed_table(ref, marks_ref, group, rows) for ref in (cos_ref, ahead_ref, behind_ref)
     )
     grads = jnp.concatenate(
         [
-            rotate(grad_query * factor, cosine, -ahead, -behind),
-            rotate(grad_key * factor, cosine, -ahead, -behind),
+            rotate(grad_query, cosine, -ahead, -behind),
+            rotate(grad_key, cosine, -ahead, -behind),
             grad_value,
         ],
         axis=1,
@@ -608,7 +643,7 @@
         .transpose(2, 0, 1, 3)
         .reshape(PARTS, share, 3 * head_cols)
     )
-    qkv_rows = exchange(pieces_for(qkv_parts, me), me, qkv_parts.shape)
+    qkv_rows = exchange(send_pieces(block_of(qkv_parts), me), me, qkv_parts.shape)
     qkv_rows = spread_gather(qkv_rows, 1).reshape(-1, 3 * head_cols)
     qkv_full = gather_line(qkv_rows)
     out_full = gather_line(spread_gather(out_weight, 0))
@@ -645,22 +680,22 @@
             for weight in (gate_weight, up_weight, down_weight)
         ]
     )
-    mlp_pieces = pieces_for(mlp_parts, me, 1)
-    token_lines = gather_plane(tokens, *mlp_pieces)
-    mlp_rows = spread_gather(exchange(mlp_pieces, me, mlp_parts.shape), 2)
+    mlp_pairs = send_pieces(block_of(mlp_parts, axis=1), me)
+    token_lines = gather_whole(tokens, mlp_pairs[0])
+    mlp_rows = spread_gather(exchange(mlp_pairs, me, mlp_parts.shape), 2)
     mlp_full = gather_line(mlp_rows.reshape(-1, hidden_share))
     mlp_full = mlp_full.reshape(LINE, 3, -1, hidden_share)
 
     valid = valid_rows(own_marks, rows)[:, None]
     grad_top = jnp.where(valid, out_grad.astype(f32), 0.0)
-    grad_lines = gather_plane(after(grad_top.astype(bf16), token_lines[0][3], token_lines[0][4]))
+    grad_lines = gather_whole(after(grad_top.astype(bf16), *token_lines[0][3:]))
 
     dma = pltpu.SemaphoreType.DMA
     line_rows = GROUPS * rows
 
     def attention(half, prior):
         return run_half(
-            functools.partial(attend_forward, prior is None, heads, rows, half),
+            functools.partial(attend_forward, len(token_lines[half]), prior is None, heads, rows, half),
             (after(marks, mlp_rows, *grad_lines[0][:3]) if prior is None else marks,),
             token_lines[half],
             (),
@@ -673,7 +708,7 @@
             ),
             [
                 pltpu.VMEM((line_rows, width), bf16),
-                dma((5,)),
+                dma((8,)),
             ],
             half,
             rows,
@@ -691,7 +726,7 @@
 
     def feed(half, prior):
         return run_half(
-            functools.partial(feed_both, prior is None, 2 * rows, half),
+            functools.partial(feed_both, len(normed_lines[half]), prior is None, 2 * rows, half),
             (),
             normed_lines[half] + grad_lines[half] + [mlp_full],
             (),
@@ -701,7 +736,7 @@
             + ((width, False, False),) * 2,
             [pltpu.VMEM((line_rows, width), bf16)] * 2
             + [pltpu.VMEM((width, hidden_share), bf16)] * 3
-            + [dma((5,)), dma((5,)), dma((3 * LINE,)), dma((2,))],
+            + [dma((8,)), dma((8,)), dma((3 * LINE,)), dma((2,))],
             half,
             2 * rows,
             prior,
@@ -737,13 +772,13 @@
             ((width, True, True), (3 * head_cols, True, False)),
             [
                 pltpu.VMEM((line_rows, width), bf16),
-                dma((5,)),
+                dma((8,)),
                 dma((1,)),
             ],
             half,
             rows,
             prior,
-            13 * line_rows * width * 4 * head_cols,
+            11 * line_rows * width * 4 * head_cols,
             GROUPS,
             width,
         )
@@ -764,25 +799,47 @@
     layer_out = jnp.where(valid, middle + down, 0.0).astype(bf16)
     grad_branch, grad_qkv, *input_kept = backs[1]
     input_sent = backs[0][2:]
+    def back_blocks(values):
+        return spread_scatter(values.reshape(PARTS, -1, values.shape[1]), 1)
+
+    columns = PARTS * hidden_share
+    mlp_pairs = send_pieces(
+        block_of(back_blocks(down_grad), back_blocks(both_grad)), me
+    )
+    down_share, gate_share, up_share = exchange_columns(mlp_pairs, me, [(share, columns)] * 3)
+    column_sums = jnp.sum(grad_qkv.astype(f32), axis=0)
+    norm_one_grads = []
+
+    def qkv_work(*far):
+        part = mat_rows(after(normed_one, *far), grad_qkv).astype(bf16)
+        weight = qkv_full.astype(f32)
+        shift_grad = jnp.sum(weight * column_sums[None, :], axis=1)
+        along = jnp.sum(weight * part.astype(f32), axis=1)
+        norm_one_grads.append((along - shift_one[0] * shift_grad) / gain_one[0])
+        norm_one_grads.append(shift_grad)
+        return part
+
+    near_rows = []
+
+    def out_work(*near):
+        near_rows.extend(near)
+        return mat_rows(after(mixed, *near), grad_branch).astype(bf16)
+
     grad_normed_one, qkv_part, out_part = scatter_plane(
         list(input_kept),
         list(input_sent),
         rows,
-        lambda *far: mat_rows(after(normed_one, *far, down), grad_qkv).astype(bf16),
-        lambda *near: mat_rows(after(mixed, *near, both_grad), grad_branch).astype(bf16),
+        qkv_work,
+        out_work,
+        (both_grad, down),
     )
     qkv_grad = scatter_line(qkv_part)
-    bias_part = jnp.sum(grad_qkv.astype(f32), axis=0).reshape(3 * heads, 1, HEAD)
+    bias_part = column_sums.reshape(3 * heads, 1, HEAD)
     bias_grad = jnp.where(
         lax.broadcasted_iota(jnp.int32, (3 * heads, PARTS, HEAD), 1) == me, bias_part, 0.0
     )
 
-    standard_one, inverse_one = standardize(inputs)
-    grad_input_norm, gain_one_grad, shift_one_grad = norm_back(
-        grad_normed_one, standard_one, inverse_one, gain_one
-    )
-    tokens_grad = (grad_middle + grad_input_norm).astype(bf16)
-
+    gain_one_grad, shift_one_grad = norm_one_grads
     devices = LINE * PARTS * spread
     small = jnp.concatenate(
         [
@@ -791,23 +848,20 @@
         ],
         axis=1,
     )
-    small = halved(small, "z", FAR, iz >= 2)
+    small = halved(after(small, *near_rows), "z", FAR, iz >= 2)
     small = halved(small, "z", NEAR, iz % 2 == 1)
     small = halved(small, "y", SWAP, iy == 1)
     small = halved(small, "x", SWAP, ix == 1)
     small = halved(small, "c", SWAP, ic == 1)
     small = spread_scatter(small, 0)[0]
 
-    def back_blocks(values):
-        return spread_scatter(values.reshape(PARTS, -1, values.shape[1]), 1)
-
-    columns = PARTS * hidden_share
-    mlp_blocks = (back_blocks(after(down_grad, grad_normed_one)), back_blocks(both_grad))
-    mlp_pieces = [
-        jnp.concatenate(parts, axis=1) for parts in zip(*(pieces_for(b, me) for b in mlp_blocks))
-    ]
-    down_share, gate_share, up_share = exchange_columns(mlp_pieces, me, [(share, columns)] * 3)
-    qkv_pieces = pieces_for(back_blocks(after(qkv_grad, *mlp_pieces)), me)
+    standard_one, inverse_one = standardize(inputs)
+    grad_input_norm, _, _ = norm_back(
+        grad_normed_one, standard_one, inverse_one, gain_one
+    )
+    tokens_grad = (grad_middle + grad_input_norm).astype(bf16)
+
+    qkv_pieces = send_pieces(block_of(back_blocks(after(qkv_grad, *mlp_pairs[1:]))), me)
     (qkv_share,) = exchange_columns(qkv_pieces, me, [(share, 3 * width)], 3 * heads)
     out_grad_weight = scatter_line(after(out_part, qkv_grad))
     out_share = spread_scatter(out_grad_weight, 0).astype(f32)

time: 634 us -> 625 us (0.986)
  Pallas kernels: 152 us -> 136 us
  starting transfers between devices: 80 us -> 66.2 us
  local copies, waits for them, and re-layouts: 43.7 us -> 56.6 us
  other arithmetic: 61.4 us -> 72.4 us
    ppermute x16 -> x18, waiting for transfers between devices: 52.9 us -> 32.7 us  [over_x(): return lax.ppermute(values, 'x', SWAP)]
    pallas_call x6, Pallas kernels: 145 us -> 130 us  [run_half(): pl.pallas_call(body, grid_spec=pltpu.PrefetchScalarGridSpec(num_scalar_pr...]
    all_gather x3, waiting for transfers between devices: 5.07 us -> 19.2 us  [gather_line(): return lax.all_gather(values, 'z', axis=0, tiled=True)]
    ppermute x28 -> x12, starting transfers between devices: 28.4 us -> 14.5 us  [send_pieces(): pair = lax.ppermute(pair, ('y', 'x'), [(i, i ^ away) for i in range(CHIPS)])]
    ppermute x5, waiting for transfers between devices: 8.06 us -> 20.8 us  [halved(): came = lax.ppermute(jnp.where(upper, low, high), axis, perm)]
    ppermute x5, waiting for transfers between devices: 21.5 us -> 9.81 us  [doubled(): other = lax.ppermute(values, axis, perm)]
    another operation x6 -> x34, other arithmetic: 15.9 us -> 26.5 us
    ppermute x28 -> x12, waiting for transfers between devices: 31.3 us -> 35.6 us  [send_pieces(): pair = lax.ppermute(pair, ('y', 'x'), [(i, i ^ away) for i in range(CHIPS)])]
  transfers between devices with their start and end apart: 102 -> 100, of which waited for: 40 -> 39; matrix products, arithmetic and copies ran while one was open for 22% -> 26% of each run, Pallas kernels for 19% -> 17%
where the time goes in v6:
time: 625 us; the launch traced here: 617 us
  waiting for transfers between devices  227 us (36%)
  Pallas kernels  136 us (22%)
  other arithmetic  72.4 us (12%)
  starting transfers between devices  66.2 us (11%)
  local copies, waits for them, and re-layouts  56.6 us (9%)
  matrix products  42 us (7%)
  between operations  16.8 us (3%)
    pallas_call x6, Pallas kernels, run_half(): pl.pallas_call(body, grid_spec=pltpu.PrefetchScalarGridSpec(num_scalar_pr...  130 us
    ppermute x18, waiting for transfers between devices, over_y(): return lax.ppermute(values, 'y', SWAP)  102 us
    dot_general x4, matrix products, mat_rows(): lax.dot_general(left, right, (((0,), (0,)), ((), ())), preferred_element_...  42 us
    ppermute x12, waiting for transfers between devices, send_pieces(): pair = lax.ppermute(pair, ('y', 'x'), [(i, i ^ away) for i in range(CHIPS)])  35.6 us
    ppermute x18, waiting for transfers between devices, over_x(): return lax.ppermute(values, 'x', SWAP)  32.7 us
    ppermute x5, waiting for transfers between devices, halved(): came = lax.ppermute(jnp.where(upper, low, high), axis, perm)  20.8 us
    all_gather x3, waiting for transfers between devices, gather_line(): return lax.all_gather(values, 'z', axis=0, tiled=True)  19.2 us
    ppermute x18, starting transfers between devices, over_x(): return lax.ppermute(values, 'x', SWAP)  18.4 us
  transfers between devices with their start and end apart: 100, of which 39 were waited for; matrix products, arithmetic and copies ran while one was open for 26% of the time, Pallas kernels for 17%

profile of v6, /device:TPU:0, one launch (start us, length us, event | category | flops | bytes accessed | tf_op | source)
XLA Modules:
  0.0 617.3 jit_solution(3046715547762318746)
XLA Ops:
  21.4 3.9 collective-permute-done.9.refs_1_
  25.3 5.3 collective-permute-done.10.refs_2_
  52.1 7.3 %collective-permute-done.1 = bf16[2,512]{1,0:T(2,128)(2,1)S(1)} collective-permute-done((bf16[2,512]{1,0:T(2,128)(2,1)S(1)}, bf16[2,512]{1,0:T(2,128)(2,1)S(1)}, u32[]{:S(2)}, u32[]{:S(2)}) %collective-permute-start.1) | collective-permute-done | bytes 2080 | tf_op jit(solution)/shard_map/ppermute | solution.py:204
  78.3 6.3 %collective-permute-done.16.refs_3_ = bf16[2,3,64,704]{3,2,1,0:T(8,128)(2,1)S(1)} collective-permute-done((bf16[2,3,64,704]{3,2,1,0:T(8,128)(2,1)}, bf16[2,3,64,704]{3,2,1,0:T(8,128)(2,1)S(1)}, u32[]{:S(2)}, u32[]{:S(2)}) %collective-permute-start.16) | collective-permute-done | bytes 540704 | tf_op jit(solution)/shard_map/ppermute | solution.py:162
  86.4 7.2 %collective-permute-done.6.refs_3_ = bf16[128,2048]{1,0:T(8,128)(2,1)S(1)} collective-permute-done((bf16[128,2048]{1,0:T(8,128)(2,1)}, bf16[128,2048]{1,0:T(8,128)(2,1)S(1)}, u32[]{:S(2)}, u32[]{:S(2)}) %collective-permute-start.6) | collective-permute-done | bytes 524320 | tf_op jit(solution)/shard_map/ppermute | solution.py:44
  101.5 17.7 %collective-permute-done.18.refs_10_ = bf16[256,2048]{1,0:T(8,128)(2,1)} collective-permute-done((bf16[256,2048]{1,0:T(8,128)(2,1)}, bf16[256,2048]{1,0:T(8,128)(2,1)}, u32[]{:S(2)}, u32[]{:S(2)}) %collective-permute-start.18) | collective-permute-done | bytes 1048608 | tf_op jit(solution)/shard_map/ppermute | solution.py:48
  129.3 16.4 %shard_map.231 = (bf16[2048,2048]{1,0:T(8,128)(2,1)}, bf16[2048,768]{1,0:T(8,128)(2,1)}, bf16[2048,256]{1,0:T(8,128)(2,1)}, bf16[1024,2048]{1,0:T(8,128)(2,1)}) custom-call(s32[8,6]{1,0:T(8,128)} %copy.88.marks_ref, bf16[256,2048]{1,0:T(8,128)(2,1)} %collective-permute-done.19.refs_0_, bf16[256,2048]{1,0:T(8,128)(2,1)} %copy-done.23, ...), custom_call_target="tpu_custom_call" | custom-call | flops 1 | bytes 1 | tf_op jit(solution)/shard_map/pallas_call | solution.py:572
  146.6 16.2 %shard_map.232 = (bf16[2048,2048]{1,0:T(8,128)(2,1)}, bf16[2048,768]{1,0:T(8,128)(2,1)}, bf16[2048,256]{1,0:T(8,128)(2,1)}, bf16[1024,2048]{1,0:T(8,128)(2,1)}) custom-call(s32[8,6]{1,0:T(8,128)} %copy.92.marks_ref, bf16[256,2048]{1,0:T(8,128)(2,1)} %refs_0_.1, ...), custom_call_target="tpu_custom_call", output_to_operand_aliasing={{0}: (14, {}), {1}: (15, {}), {2}: (16, {})} | custom-call | flops 1 | bytes 1 | tf_op jit(solution)/shard_map/pallas_call | solution.py:572
  167.9 12.2 %collective-permute-done.29 = bf16[128,2048]{1,0:T(8,128)(2,1)S(1)} collective-permute-done((bf16[128,2048]{1,0:T(8,128)(2,1)S(1)}, bf16[128,2048]{1,0:T(8,128)(2,1)S(1)}, u32[]{:S(2)}, u32[]{:S(2)}) %collective-permute-start.29) | collective-permute-done | bytes 524320 | tf_op jit(solution)/shard_map/ppermute | solution.py:44
  186.5 21.5 %collective-permute-done.30 = bf16[256,2048]{1,0:T(8,128)(2,1)} collective-permute-done((bf16[256,2048]{1,0:T(8,128)(2,1)S(1)}, bf16[256,2048]{1,0:T(8,128)(2,1)}, u32[]{:S(2)}, u32[]{:S(2)}) %collective-permute-start.30) | collective-permute-done | bytes 1048608 | tf_op jit(solution)/shard_map/ppermute | solution.py:48
  217.5 10.6 %collective-permute-done.34.refs_5_ = bf16[128,2048]{1,0:T(8,128)(2,1)S(1)} collective-permute-done((bf16[128,2048]{1,0:T(8,128)(2,1)S(1)}, bf16[128,2048]{1,0:T(8,128)(2,1)S(1)}, u32[]{:S(2)}, u32[]{:S(2)}) %collective-permute-start.34) | collective-permute-done | bytes 524320 | tf_op jit(solution)/shard_map/ppermute | solution.py:48
  230.2 9.1 %collective-permute-done.33.refs_4_ = bf16[128,2048]{1,0:T(8,128)(2,1)S(1)} collective-permute-done((bf16[128,2048]{1,0:T(8,128)(2,1)S(1)}, bf16[128,2048]{1,0:T(8,128)(2,1)S(1)}, u32[]{:S(2)}, u32[]{:S(2)}) %collective-permute-start.33) | collective-permute-done | bytes 524320 | tf_op jit(solution)/shard_map/ppermute | solution.py:48
  241.5 8.3 %collective-permute-done.36.refs_7_ = bf16[128,2048]{1,0:T(8,128)(2,1)S(1)} collective-permute-done((bf16[128,2048]{1,0:T(8,128)(2,1)S(1)}, bf16[128,2048]{1,0:T(8,128)(2,1)S(1)}, u32[]{:S(2)}, u32[]{:S(2)}) %collective-permute-start.36) | collective-permute-done | bytes 524320 | tf_op jit(solution)/shard_map/ppermute | solution.py:48
  253.8 19.2 %all-gather.8.cloned.1.call-done = bf16[6144,704]{1,0:T(8,128)(2,1)} async-done(((bf16[1536,704]{1,0:T(8,128)(2,1)}), bf16[6144,704]{1,0:T(8,128)(2,1)}) %all-gather.8.cloned.1.call-update) | async-done | bytes 8650768 | tf_op jit(solution)/shard_map/all_gather | solution.py:56
  273.0 29.8 %shard_map.233 = (bf16[2048,2048]{1,0:T(8,128)(2,1)}, bf16[2048,2048]{1,0:T(8,128)(2,1)}, bf16[2048,704]{1,0:T(8,128)(2,1)}, bf16[2048,1408]{1,0:T(8,128)(2,1)},...) custom-call(bf16[128,2048]{1,0:T(8,128)(2,1)} %copy-done.38, bf16[128,2048]{1,0:T(8,128)(2,1)} %collective-permute-done.38.refs_1_, ...), custom_call_target="tpu_custom_call" | custom-call | flops 1 | bytes 1 | tf_op jit(solution)/shard_map/pallas_call | solution.py:572
  303.0 30.0 %shard_map.234 = (bf16[2048,2048]{1,0:T(8,128)(2,1)}, bf16[2048,2048]{1,0:T(8,128)(2,1)}, bf16[2048,704]{1,0:T(8,128)(2,1)}, bf16[2048,1408]{1,0:T(8,128)(2,1)},...) custom-call(bf16[128,2048]{1,0:T(8,128)(2,1)} %copy-done.13, ...), custom_call_target="tpu_custom_call", output_to_operand_aliasing={{0}: (14, {}), {1}: (15, {}), {2}: (16, {}), {3}: (17, {})} | custom-call | flops 1 | bytes 1 | tf_op jit(solution)/shard_map/pallas_call | solution.py:572
  340.9 9.9 %convolution_convert_fusion.2 = bf16[2048,704]{0,1:T(8,128)(2,1)} fusion(bf16[2048,2048]{1,0:T(8,128)(2,1)} %get-tuple-element.89, bf16[2048,704]{1,0:T(8,128)(2,1)S(1)} %copy-done.11), kind=kOutput, calls=%fused_computation.7 | convolution fusion | flops 5907021824 | bytes 14155776 | tf_op jit(solution)/shard_map/dot_general | solution.py:32
  362.2 17.2 %convolution_convert_fusion = bf16[2048,1408]{1,0:T(8,128)(2,1)} fusion(bf16[2048,2048]{1,0:T(8,128)(2,1)S(1)} %copy-done.4, bf16[2048,1408]{1,0:T(8,128)(2,1)} %get-tuple-element.95), kind=kOutput, calls=%fused_computation.2 | convolution fusion | flops 11814043648 | bytes 19922944 | tf_op jit(solution)/shard_map/dot_general | solution.py:32
  379.4 4.2 collective-permute-done.53
  397.0 12.3 %collective-permute-done.66.refs_5_ = bf16[128,2048]{1,0:T(8,128)(2,1)} collective-permute-done((bf16[128,2048]{1,0:T(8,128)(2,1)S(1)}, bf16[128,2048]{1,0:T(8,128)(2,1)}, u32[]{:S(2)}, u32[]{:S(2)}) %collective-permute-start.66) | collective-permute-done | bytes 524320 | tf_op jit(solution)/shard_map/ppermute | solution.py:48
  410.4 9.8 %collective-permute-done.64.refs_4_ = bf16[128,2048]{1,0:T(8,128)(2,1)} collective-permute-done((bf16[128,2048]{1,0:T(8,128)(2,1)}, bf16[128,2048]{1,0:T(8,128)(2,1)}, u32[]{:S(2)}, u32[]{:S(2)}) %collective-permute-start.64) | collective-permute-done | bytes 524320 | tf_op jit(solution)/shard_map/ppermute | solution.py:48
  428.7 5.3 collective-permute-done.70.refs_7_
  443.7 19.2 %shard_map.235 = (bf16[2048,2048]{1,0:T(8,128)(2,1)}, bf16[2048,768]{1,0:T(8,128)(2,1)}, bf16[512,2048]{1,0:T(8,128)(2,1)}, bf16[512,2048]{1,0:T(8,128)(2,1)}) custom-call(s32[8,6]{1,0:T(8,128)} %copy.96.marks_ref, bf16[128,2048]{1,0:T(8,128)(2,1)} %collective-permute-done.58.refs_0_, bf16[128,2048]{1,0:T(8,128)(2,1)} %copy-done.71, ...), custom_call_target="tpu_custom_call" | custom-call | flops 23622320128 | bytes 1 | tf_op jit(solution)/shard_map/pallas_call | solution.py:572
  472.7 18.1 %shard_map.236 = (bf16[2048,2048]{1,0:T(8,128)(2,1)}, bf16[2048,768]{1,0:T(8,128)(2,1)}, bf16[512,2048]{1,0:T(8,128)(2,1)}, bf16[512,2048]{1,0:T(8,128)(2,1)}) custom-call(s32[8,6]{1,0:T(8,128)} %copy.100.marks_ref, bf16[128,2048]{1,0:T(8,128)(2,1)} %get-tuple-element.194.refs_0_, ...), custom_call_target="tpu_custom_call", output_to_operand_aliasing={{0}: (15, {}), {1}: (16, {})} | custom-call | flops 23622320128 | bytes 1 | tf_op jit(solution)/shard_map/pallas_call | solution.py:572
  496.1 4.2 select_convert_fusion
  504.7 11.5 %fusion.1 = (f32[2048]{0:T(1024)S(1)}, f32[2048]{0:T(1024)S(1)}, bf16[2048,768]{1,0:T(8,128)(2,1)}) fusion(bf16[2048,768]{1,0:T(8,128)(2,1)S(1)} %copy-done.2, f32[768]{0:T(1024)S(1)} %copy-done.55, bf16[2048,2048]{1,0:T(8,128)(2,1)} %get-tuple-element.113, bf16[2048,768]{1,0:T(8,128)(2,1)S(1)} %copy-done.10), kind=kOutput, calls=%fused_computation.4 | convolution fusion | flops 6453456896 | bytes 17845248 | tf_op jit(solution)/shard_map/dot_general | solution.py:32
  532.5 3.9 collective-permute-done.88
  543.0 9.7 %collective-permute-done.90 = f32[4,448]{1,0:T(4,128)S(1)} collective-permute-done((f32[4,448]{1,0:T(4,128)S(1)}, f32[4,448]{1,0:T(4,128)S(1)}, u32[]{:S(2)}, u32[]{:S(2)}) %collective-permute-start.90) | collective-permute-done | bytes 7200 | tf_op jit(solution)/shard_map/ppermute | solution.py:215
  566.3 4.3 fusion.22
  570.5 4.9 reduce-scatter.9.cloned.1.call-done
  576.7 12.2 %collective-permute-done.82.refs_2_ = bf16[2,64,2112]{2,1,0:T(8,128)(2,1)S(1)} collective-permute-done((bf16[2,64,2112]{2,1,0:T(8,128)(2,1)}, bf16[2,64,2112]{2,1,0:T(8,128)(2,1)S(1)}, u32[]{:S(2)}, u32[]{:S(2)}) %collective-permute-start.82) | collective-permute-done | bytes 540704 | tf_op jit(solution)/shard_map/ppermute | solution.py:162
  601.6 5.1 collective-permute-done.86.refs_2_
  (510 shorter events, 227.6 us)
Async XLA Ops:
  7.2 121.1 %all-gather.6.cloned.1.call-start = ((), (), s32[]{:S(2)}) async-start(), calls=%async_computation.5 | async-start | bytes 1310720 | tf_op jit(solution)/shard_map/all_gather | solution.py:56
  7.9 120.4 %all-gather.4.cloned.1.call-start = ((), (), s32[]{:S(2)}) async-start(), calls=%async_computation.4 | async-start | bytes 3932160 | tf_op jit(solution)/shard_map/all_gather | solution.py:56
  31.5 241.5 %all-gather.8.cloned.1.call-start = ((), (), s32[]{:S(2)}) async-start(), calls=%async_computation.6 | async-start | bytes 11796480 | tf_op jit(solution)/shard_map/all_gather | solution.py:56
  31.6 38.0 %collective-permute-start.4 = (bf16[256,2048]{1,0:T(8,128)(2,1)S(1)}, bf16[256,2048]{1,0:T(8,128)(2,1)}, u32[]{:S(2)}, u32[]{:S(2)}) collective-permute-start(bf16[256,2048]{1,0:T(8,128)(2,1)S(1)} %copy-done), channel_id=1, source_target_pairs={{0,4},{4,0},{1,5},{5,1},{2,6},{6,2},{3,7},{7,3},{8,12},{12,8},{9,1... | collective-permute-start | bytes 3145736 | tf_op jit(solution)/shard_map/ppermute | solution.py:48
  33.2 39.3 %collective-permute-start.3 = (bf16[256,2048]{1,0:T(8,128)(2,1)S(1)}, bf16[256,2048]{1,0:T(8,128)(2,1)}, u32[]{:S(2)}, u32[]{:S(2)}) collective-permute-start(bf16[256,2048]{1,0:T(8,128)(2,1)S(1)} %copy-done), channel_id=1, source_target_pairs={{0,2},{2,0},{1,3},{3,1},{4,6},{6,4},{5,7},{7,5},{8,10},{10,8},{9,1... | collective-permute-start | bytes 3145736 | tf_op jit(solution)/shard_map/ppermute | solution.py:44
  47.7 28.8 %collective-permute-start.14 = (bf16[2,3,64,704]{3,2,1,0:T(8,128)(2,1)}, bf16[2,3,64,704]{3,2,1,0:T(8,128)(2,1)S(1)}, u32[]{:S(2)}, u32[]{:S(2)}) collective-permute-start(bf16[2,3,64,704]{3,2,1,0:T(8,128)(2,1)} %pad_maximum_fusion.12), channel_id=1, source_target_pairs={{0,2},{2,0},{4,6},{6,4},{1,3},{3,1},{5,7},{7,5},{8,10},{10,8},{12,... | collective-permute-start | bytes 1622024 | tf_op jit(solution)/shard_map/ppermute | solution.py:162
  50.1 26.5 %collective-permute-start.15 = (bf16[2,3,64,704]{3,2,1,0:T(8,128)(2,1)}, bf16[2,3,64,704]{3,2,1,0:T(8,128)(2,1)S(1)}, u32[]{:S(2)}, u32[]{:S(2)}) collective-permute-start(bf16[2,3,64,704]{3,2,1,0:T(8,128)(2,1)} %pad_maximum_fusion.13), channel_id=1, source_target_pairs={{0,4},{2,6},{4,0},{6,2},{1,5},{3,7},{5,1},{7,3},{8,12},{10,14},{12... | collective-permute-start | bytes 1622024 | tf_op jit(solution)/shard_map/ppermute | solution.py:162
  59.4 25.2 %collective-permute-start.16 = (bf16[2,3,64,704]{3,2,1,0:T(8,128)(2,1)}, bf16[2,3,64,704]{3,2,1,0:T(8,128)(2,1)S(1)}, u32[]{:S(2)}, u32[]{:S(2)}) collective-permute-start(bf16[2,3,64,704]{3,2,1,0:T(8,128)(2,1)} %pad_maximum_fusion.14), channel_id=1, source_target_pairs={{0,6},{2,4},{4,2},{6,0},{1,7},{3,5},{5,3},{7,1},{8,14},{10,12},{12... | collective-permute-start | bytes 1622024 | tf_op jit(solution)/shard_map/ppermute | solution.py:162
  76.5 47.0 %collective-permute-start.19 = (bf16[256,2048]{1,0:T(8,128)(2,1)S(1)}, bf16[256,2048]{1,0:T(8,128)(2,1)}, u32[]{:S(2)}, u32[]{:S(2)}) collective-permute-start(bf16[256,2048]{1,0:T(8,128)(2,1)S(1)} %copy-done), channel_id=1, source_target_pairs={{0,1},{1,0},{2,3},{3,2},{4,5},{5,4},{6,7},{7,6},{8,9},{9,8},{10,11... | collective-permute-start | bytes 3145736 | tf_op jit(solution)/shard_map/ppermute | solution.py:52
  86.2 339.7 %reduce-scatter.5.cloned.1.call-start = ((), (), s32[]{:S(2)}) async-start(), calls=%async_computation.7 | async-start | bytes 3604480 | tf_op jit(solution)/shard_map/reduce_scatter | solution.py:60
  86.4 38.6 %collective-permute-start.21 = (bf16[256,2048]{1,0:T(8,128)(2,1)}, bf16[256,2048]{1,0:T(8,128)(2,1)S(1)}, u32[]{:S(2)}, u32[]{:S(2)}) collective-permute-start(bf16[256,2048]{1,0:T(8,128)(2,1)} %collective-permute-done.4.refs_2_), channel_id=1, source_target_pairs={{0,1},{1,0},{2,3},{3,2},{4,5},{5,4},{6,7},{7,6},{8,9},{9,8},{10,11... | collective-permute-start | bytes 3145736 | tf_op jit(solution)/shard_map/ppermute | solution.py:52
  93.7 25.4 %collective-permute-start.18 = (bf16[256,2048]{1,0:T(8,128)(2,1)}, bf16[256,2048]{1,0:T(8,128)(2,1)}, u32[]{:S(2)}, u32[]{:S(2)}) collective-permute-start(bf16[256,2048]{1,0:T(8,128)(2,1)} %fusion.12.refs_8_), channel_id=1, source_target_pairs={{0,4},{4,0},{1,5},{5,1},{2,6},{6,2},{3,7},{7,3},{8,12},{12,8},{9,1... | collective-permute-start | bytes 3145736 | tf_op jit(solution)/shard_map/ppermute | solution.py:48
  95.2 25.9 %collective-permute-start.17 = (bf16[256,2048]{1,0:T(8,128)(2,1)}, bf16[256,2048]{1,0:T(8,128)(2,1)}, u32[]{:S(2)}, u32[]{:S(2)}) collective-permute-start(bf16[256,2048]{1,0:T(8,128)(2,1)} %fusion.12.refs_8_), channel_id=1, source_target_pairs={{0,2},{2,0},{1,3},{3,1},{4,6},{6,4},{5,7},{7,5},{8,10},{10,8},{9,1... | collective-permute-start | bytes 3145736 | tf_op jit(solution)/shard_map/ppermute | solution.py:44
  101.1 27.2 %collective-permute-start.20 = (bf16[256,2048]{1,0:T(8,128)(2,1)}, bf16[256,2048]{1,0:T(8,128)(2,1)S(1)}, u32[]{:S(2)}, u32[]{:S(2)}) collective-permute-start(bf16[256,2048]{1,0:T(8,128)(2,1)} %collective-permute-done.3.refs_1_), channel_id=1, source_target_pairs={{0,1},{1,0},{2,3},{3,2},{4,5},{5,4},{6,7},{7,6},{8,9},{9,8},{10,11... | collective-permute-start | bytes 3145736 | tf_op jit(solution)/shard_map/ppermute | solution.py:52
  186.0 26.9 %collective-permute-start.45 = (bf16[256,2048]{1,0:T(8,128)(2,1)}, bf16[256,2048]{1,0:T(8,128)(2,1)S(1)}, u32[]{:S(2)}, u32[]{:S(2)}) collective-permute-start(bf16[256,2048]{1,0:T(8,128)(2,1)} %fusion.12.refs_8_), channel_id=1, source_target_pairs={{0,1},{1,0},{2,3},{3,2},{4,5},{5,4},{6,7},{7,6},{8,9},{9,8},{10,11... | collective-permute-start | bytes 3145736 | tf_op jit(solution)/shard_map/ppermute | solution.py:52
  186.0 28.9 %collective-permute-start.47 = (bf16[256,2048]{1,0:T(8,128)(2,1)}, bf16[256,2048]{1,0:T(8,128)(2,1)S(1)}, u32[]{:S(2)}, u32[]{:S(2)}) collective-permute-start(bf16[256,2048]{1,0:T(8,128)(2,1)} %collective-permute-done.18.refs_10_), channel_id=1, source_target_pairs={{0,1},{1,0},{2,3},{3,2},{4,5},{5,4},{6,7},{7,6},{8,9},{9,8},{10,11... | collective-permute-start | bytes 3145736 | tf_op jit(solution)/shard_map/ppermute | solution.py:52
  186.5 30.4 %collective-permute-start.46 = (bf16[256,2048]{1,0:T(8,128)(2,1)}, bf16[256,2048]{1,0:T(8,128)(2,1)S(1)}, u32[]{:S(2)}, u32[]{:S(2)}) collective-permute-start(bf16[256,2048]{1,0:T(8,128)(2,1)} %collective-permute-done.17.refs_9_), channel_id=1, source_target_pairs={{0,1},{1,0},{2,3},{3,2},{4,5},{5,4},{6,7},{7,6},{8,9},{9,8},{10,11... | collective-permute-start | bytes 3145736 | tf_op jit(solution)/shard_map/ppermute | solution.py:52
  302.8 30.2 %collective-permute-start.50 = (bf16[1024,2048]{1,0:T(8,128)(2,1)}, bf16[1024,2048]{1,0:T(8,128)(2,1)S(1)}, u32[]{:S(2)}, u32[]{:S(2)}) collective-permute-start(bf16[1024,2048]{1,0:T(8,128)(2,1)} %get-tuple-element.87), channel_id=1, source_target_pairs={{0,1},{1,0},{2,3},{3,2},{4,5},{5,4},{6,7},{7,6},{8,9},{9,8},{10,11... | collective-permute-start | bytes 12582920 | tf_op jit(solution)/shard_map/ppermute | solution.py:52
  350.9 166.1 %reduce-scatter.7.cloned.1.call-start = ((), (), s32[]{:S(2)}) async-start(), calls=%async_computation.8 | async-start | bytes 7208960 | tf_op jit(solution)/shard_map/reduce_scatter | solution.py:60
  358.6 25.0 %collective-permute-start.53 = (bf16[256,2048]{1,0:T(8,128)(2,1)}, bf16[256,2048]{1,0:T(8,128)(2,1)}, u32[]{:S(2)}, u32[]{:S(2)}) collective-permute-start(bf16[256,2048]{1,0:T(8,128)(2,1)} %pad_maximum_fusion.5), channel_id=1, source_target_pairs={{0,2},{2,0},{1,3},{3,1},{4,6},{6,4},{5,7},{7,5},{8,10},{10,8},{9,1... | collective-permute-start | bytes 3145736 | tf_op jit(solution)/shard_map/ppermute | solution.py:44
  361.2 24.8 %collective-permute-start.54 = (bf16[256,2048]{1,0:T(8,128)(2,1)}, bf16[256,2048]{1,0:T(8,128)(2,1)}, u32[]{:S(2)}, u32[]{:S(2)}) collective-permute-start(bf16[256,2048]{1,0:T(8,128)(2,1)} %pad_maximum_fusion.6), channel_id=1, source_target_pairs={{0,4},{4,0},{1,5},{5,1},{2,6},{6,2},{3,7},{7,3},{8,12},{12,8},{9,1... | collective-permute-start | bytes 3145736 | tf_op jit(solution)/shard_map/ppermute | solution.py:48
  392.1 44.1 %collective-permute-start.55 = (bf16[1024,2048]{1,0:T(8,128)(2,1)}, bf16[1024,2048]{1,0:T(8,128)(2,1)}, u32[]{:S(2)}, u32[]{:S(2)}) collective-permute-start(bf16[1024,2048]{1,0:T(8,128)(2,1)} %get-tuple-element.98), channel_id=1, source_target_pairs={{0,1},{1,0},{2,3},{3,2},{4,5},{5,4},{6,7},{7,6},{8,9},{9,8},{10,11... | collective-permute-start | bytes 12582920 | tf_op jit(solution)/shard_map/ppermute | solution.py:52
  392.1 183.3 %reduce-scatter.9.cloned.1.call-start = ((), (), s32[]{:S(2)}) async-start(), calls=%async_computation.9 | async-start | bytes 3932160 | tf_op jit(solution)/shard_map/reduce_scatter | solution.py:60
  463.0 56.5 %collective-permute-start.74 = (bf16[512,2048]{1,0:T(8,128)(2,1)}, bf16[512,2048]{1,0:T(8,128)(2,1)}, u32[]{:S(2)}, u32[]{:S(2)}) collective-permute-start(bf16[512,2048]{1,0:T(8,128)(2,1)} %get-tuple-element.111), channel_id=1, source_target_pairs={{0,1},{1,0},{2,3},{3,2},{4,5},{5,4},{6,7},{7,6},{8,9},{9,8},{10,11... | collective-permute-start | bytes 6291464 | tf_op jit(solution)/shard_map/ppermute | solution.py:52
  463.0 37.2 %collective-permute-start.75 = (bf16[512,2048]{1,0:T(8,128)(2,1)}, bf16[512,2048]{1,0:T(8,128)(2,1)}, u32[]{:S(2)}, u32[]{:S(2)}) collective-permute-start(bf16[512,2048]{1,0:T(8,128)(2,1)} %get-tuple-element.101), channel_id=1, source_target_pairs={{0,1},{1,0},{2,3},{3,2},{4,5},{5,4},{6,7},{7,6},{8,9},{9,8},{10,11... | collective-permute-start | bytes 6291464 | tf_op jit(solution)/shard_map/ppermute | solution.py:52
  468.3 25.7 %collective-permute-start.72 = (bf16[256,2048]{1,0:T(8,128)(2,1)}, bf16[256,2048]{1,0:T(8,128)(2,1)}, u32[]{:S(2)}, u32[]{:S(2)}) collective-permute-start(bf16[256,2048]{1,0:T(8,128)(2,1)} %pad_maximum_fusion.7), channel_id=1, source_target_pairs={{0,2},{2,0},{1,3},{3,1},{4,6},{6,4},{5,7},{7,5},{8,10},{10,8},{9,1... | collective-permute-start | bytes 3145736 | tf_op jit(solution)/shard_map/ppermute | solution.py:44
  470.9 25.2 %collective-permute-start.73 = (bf16[256,2048]{1,0:T(8,128)(2,1)}, bf16[256,2048]{1,0:T(8,128)(2,1)}, u32[]{:S(2)}, u32[]{:S(2)}) collective-permute-start(bf16[256,2048]{1,0:T(8,128)(2,1)} %pad_maximum_fusion.8), channel_id=1, source_target_pairs={{0,4},{4,0},{1,5},{5,1},{2,6},{6,2},{3,7},{7,3},{8,12},{12,8},{9,1... | collective-permute-start | bytes 3145736 | tf_op jit(solution)/shard_map/ppermute | solution.py:48
  516.4 91.8 %reduce-scatter.11.cloned.1.call-start = ((), (), s32[]{:S(2)}) async-start(), calls=%async_computation.10 | async-start | bytes 1310720 | tf_op jit(solution)/shard_map/reduce_scatter | solution.py:60
  519.3 39.5 %collective-permute-start.80 = (bf16[4,64,2112]{2,1,0:T(8,128)(2,1)S(1)}, bf16[4,64,2112]{2,1,0:T(8,128)(2,1)}, u32[]{:S(2)}, u32[]{:S(2)}) collective-permute-start(bf16[4,64,2112]{2,1,0:T(8,128)(2,1)S(1)} %pad_maximum_fusion.2), channel_id=1, source_target_pairs={{0,1},{1,0},{2,3},{3,2},{4,5},{5,4},{6,7},{7,6},{8,9},{9,8},{10,11... | collective-permute-start | bytes 3244040 | tf_op jit(solution)/shard_map/ppermute | solution.py:52
  523.9 34.9 %collective-permute-start.78 = (bf16[256,2048]{1,0:T(8,128)(2,1)}, bf16[256,2048]{1,0:T(8,128)(2,1)}, u32[]{:S(2)}, u32[]{:S(2)}) collective-permute-start(bf16[256,2048]{1,0:T(8,128)(2,1)} %pad_maximum_fusion.9), channel_id=1, source_target_pairs={{0,2},{2,0},{1,3},{3,1},{4,6},{6,4},{5,7},{7,5},{8,10},{10,8},{9,1... | collective-permute-start | bytes 3145736 | tf_op jit(solution)/shard_map/ppermute | solution.py:44
  528.2 30.6 %collective-permute-start.79 = (bf16[256,2048]{1,0:T(8,128)(2,1)}, bf16[256,2048]{1,0:T(8,128)(2,1)}, u32[]{:S(2)}, u32[]{:S(2)}) collective-permute-start(bf16[256,2048]{1,0:T(8,128)(2,1)} %pad_maximum_fusion.10), channel_id=1, source_target_pairs={{0,4},{4,0},{1,5},{5,1},{2,6},{6,2},{3,7},{7,3},{8,12},{12,8},{9,1... | collective-permute-start | bytes 3145736 | tf_op jit(solution)/shard_map/ppermute | solution.py:48
  562.4 26.6 %collective-permute-start.82 = (bf16[2,64,2112]{2,1,0:T(8,128)(2,1)}, bf16[2,64,2112]{2,1,0:T(8,128)(2,1)S(1)}, u32[]{:S(2)}, u32[]{:S(2)}) collective-permute-start(bf16[2,64,2112]{2,1,0:T(8,128)(2,1)} %pad_maximum_fusion.16), channel_id=1, source_target_pairs={{0,4},{2,6},{4,0},{6,2},{1,5},{3,7},{5,1},{7,3},{8,12},{10,14},{12... | collective-permute-start | bytes 1622024 | tf_op jit(solution)/shard_map/ppermute | solution.py:162
  (143 other events, 1635.6 us)
Sparse Core Ops, SparseCore 0:
  9.6 30.6 all-gather.5
  42.4 63.6 all-gather.3
  107.6 165.3 all-gather.7
  351.0 52.5 reduce-scatter.4
  405.8 102.1 reduce-scatter.6
  516.5 58.8 reduce-scatter.8
  577.7 27.1 reduce-scatter.10

commit v7 on v6

--- a/solution.py
+++ b/solution.py
@@ -382,7 +382,7 @@
     tokens, refs = refs[:count], refs[count:]
     qkv_weight, out_weight, gain, shift, bias, cos_ref, ahead_ref, behind_ref = refs[:8]
     refs = refs[8 if first else 11 :]
-    normed_ref, qkv_ref, mixed_ref, part_ref, token_rows, line_sems = refs
+    standard_ref, qkv_ref, mixed_ref, part_ref, token_rows, line_sems = refs
     step = pl.program_id(0)
     group = half * GROUPS + step
     line = line_copies(tokens, token_rows, line_sems)
@@ -391,8 +391,9 @@
     values = token_rows[pl.ds(pl.multiple_of(step * rows, rows), rows), :].astype(f32)
     centre = values - jnp.mean(values, axis=1, keepdims=True)
     inverse = lax.rsqrt(jnp.mean(centre * centre, axis=1, keepdims=True) + eps_norm)
-    normed = (centre * inverse * gain[...] + shift[...]).astype(bf16)
-    normed_ref[...] = normed
+    standard = centre * inverse
+    standard_ref[...] = standard.astype(bf16)
+    normed = (standard * gain[...] + shift[...]).astype(bf16)
     width = heads * HEAD
     qkv = mat(normed, qkv_weight[...]) + bias[...]
     tables = [placed_table(ref, marks_ref, group, rows) for ref in (cos_ref, ahead_ref, behind_ref)]
@@ -716,7 +717,7 @@
         )
 
     *shared, out_sent = attention(1, None)
-    normed_one, saved, mixed, out_kept = attention(0, shared)
+    standard_rows, saved, mixed, out_kept = attention(0, shared)
     out_sent = after(out_sent, *grad_lines[0])
     inputs = tokens.astype(f32)
     middle = inputs + scatter_plane(out_kept, out_sent, rows)
@@ -811,13 +812,11 @@
     norm_one_grads = []
 
     def qkv_work(*far):
-        part = mat_rows(after(normed_one, *far), grad_qkv).astype(bf16)
+        along = mat_rows(after(standard_rows, *far), grad_qkv).astype(bf16).astype(f32)
         weight = qkv_full.astype(f32)
-        shift_grad = jnp.sum(weight * column_sums[None, :], axis=1)
-        along = jnp.sum(weight * part.astype(f32), axis=1)
-        norm_one_grads.append((along - shift_one[0] * shift_grad) / gain_one[0])
-        norm_one_grads.append(shift_grad)
-        return part
+        norm_one_grads.append(jnp.sum(weight * along, axis=1))
+        norm_one_grads.append(jnp.sum(weight * column_sums[None, :], axis=1))
+        return (gain_one.T * along + shift_one.T * column_sums[None, :]).astype(bf16)
 
     near_rows = []
 

time: 625 us -> 624 us (level)
  local copies, waits for them, and re-layouts: 56.6 us -> 48.4 us
  waiting for transfers between devices: 227 us -> 234 us
    ppermute x12, waiting for transfers between devices: 35.6 us -> 46 us  [send_pieces(): pair = lax.ppermute(pair, ('y', 'x'), [(i, i ^ away) for i in range(CHIPS)])]
    ppermute x18, waiting for transfers between devices: 102 us -> 110 us  [over_y(): return lax.ppermute(values, 'y', SWAP)]
  transfers between devices with their start and end apart: 100 -> 100, of which waited for: 39 -> 42; matrix products, arithmetic and copies ran while one was open for 26% -> 25% of each run, Pallas kernels for 17% -> 17%
where the time goes in v7:
time: 624 us; the launch traced here: 616 us
  waiting for transfers between devices  234 us (38%)
  Pallas kernels  136 us (22%)
  other arithmetic  73.5 us (12%)
  starting transfers between devices  65.4 us (10%)
  local copies, waits for them, and re-layouts  48.4 us (8%)
  matrix products  42.6 us (7%)
  between operations  16.7 us (3%)
    pallas_call x6, Pallas kernels, run_half(): pl.pallas_call(body, grid_spec=pltpu.PrefetchScalarGridSpec(num_scalar_pr...  130 us
    ppermute x18, waiting for transfers between devices, over_y(): return lax.ppermute(values, 'y', SWAP)  110 us
    ppermute x12, waiting for transfers between devices, send_pieces(): pair = lax.ppermute(pair, ('y', 'x'), [(i, i ^ away) for i in range(CHIPS)])  46 us
    dot_general x4, matrix products, mat_rows(): lax.dot_general(left, right, (((0,), (0,)), ((), ())), preferred_element_...  42.6 us
    ppermute x18, waiting for transfers between devices, over_x(): return lax.ppermute(values, 'x', SWAP)  27.2 us
    ppermute x5, waiting for transfers between devices, halved(): came = lax.ppermute(jnp.where(upper, low, high), axis, perm)  20.6 us
    ppermute x18, starting transfers between devices, over_y(): return lax.ppermute(values, 'y', SWAP)  20.5 us
    ppermute x18, starting transfers between devices, over_x(): return lax.ppermute(values, 'x', SWAP)  16.3 us
  transfers between devices with their start and end apart: 100, of which 42 were waited for; matrix products, arithmetic and copies ran while one was open for 25% of the time, Pallas kernels for 17%

profile of v7, /device:TPU:0, one launch (start us, length us, event | category | flops | bytes accessed | tf_op | source)
XLA Modules:
  0.0 616.4 jit_solution(14459053056052334516)
XLA Ops:
  25.2 5.3 collective-permute-done.10.refs_2_
  50.1 7.7 %collective-permute-done.4.refs_2_ = bf16[256,2048]{1,0:T(8,128)(2,1)} collective-permute-done((bf16[256,2048]{1,0:T(8,128)(2,1)S(1)}, bf16[256,2048]{1,0:T(8,128)(2,1)}, u32[]{:S(2)}, u32[]{:S(2)}) %collective-permute-start.4) | collective-permute-done | bytes 1048608 | tf_op jit(solution)/shard_map/ppermute | solution.py:48
  65.4 6.4 %collective-permute-done.14.refs_1_ = bf16[2,3,64,704]{3,2,1,0:T(8,128)(2,1)S(1)} collective-permute-done((bf16[2,3,64,704]{3,2,1,0:T(8,128)(2,1)}, bf16[2,3,64,704]{3,2,1,0:T(8,128)(2,1)S(1)}, u32[]{:S(2)}, u32[]{:S(2)}) %collective-permute-start.14) | collective-permute-done | bytes 540704 | tf_op jit(solution)/shard_map/ppermute | solution.py:162
  73.9 6.6 %collective-permute-done.15.refs_2_ = bf16[2,3,64,704]{3,2,1,0:T(8,128)(2,1)S(1)} collective-permute-done((bf16[2,3,64,704]{3,2,1,0:T(8,128)(2,1)}, bf16[2,3,64,704]{3,2,1,0:T(8,128)(2,1)S(1)}, u32[]{:S(2)}, u32[]{:S(2)}) %collective-permute-start.15) | collective-permute-done | bytes 540704 | tf_op jit(solution)/shard_map/ppermute | solution.py:162
  86.1 7.6 %collective-permute-done.1 = bf16[2,512]{1,0:T(2,128)(2,1)} collective-permute-done((bf16[2,512]{1,0:T(2,128)(2,1)}, bf16[2,512]{1,0:T(2,128)(2,1)}, u32[]{:S(2)}, u32[]{:S(2)}) %collective-permute-start.1) | collective-permute-done | bytes 2080 | tf_op jit(solution)/shard_map/ppermute | solution.py:204
  103.2 17.5 %collective-permute-done.18.refs_10_ = bf16[256,2048]{1,0:T(8,128)(2,1)} collective-permute-done((bf16[256,2048]{1,0:T(8,128)(2,1)}, bf16[256,2048]{1,0:T(8,128)(2,1)}, u32[]{:S(2)}, u32[]{:S(2)}) %collective-permute-start.18) | collective-permute-done | bytes 1048608 | tf_op jit(solution)/shard_map/ppermute | solution.py:48
  135.0 16.3 %shard_map.231 = (bf16[2048,2048]{1,0:T(8,128)(2,1)}, bf16[2048,768]{1,0:T(8,128)(2,1)}, bf16[2048,256]{1,0:T(8,128)(2,1)}, bf16[1024,2048]{1,0:T(8,128)(2,1)}) custom-call(s32[8,6]{1,0:T(8,128)} %copy.113.marks_ref, bf16[256,2048]{1,0:T(8,128)(2,1)} %collective-permute-done.19.refs_0_, bf16[256,2048]{1,0:T(8,128)(2,1)} %copy-done.22, ...), custom_call_target="tpu_custom_call" | custom-call | flops 1 | bytes 1 | tf_op jit(solution)/shard_map/pallas_call | solution.py:573
  152.3 16.3 %shard_map.232 = (bf16[2048,2048]{1,0:T(8,128)(2,1)}, bf16[2048,768]{1,0:T(8,128)(2,1)}, bf16[2048,256]{1,0:T(8,128)(2,1)}, bf16[1024,2048]{1,0:T(8,128)(2,1)}) custom-call(s32[8,6]{1,0:T(8,128)} %copy.117.marks_ref, bf16[256,2048]{1,0:T(8,128)(2,1)} %refs_0_.1, ...), custom_call_target="tpu_custom_call", output_to_operand_aliasing={{0}: (14, {}), {1}: (15, {}), {2}: (16, {})} | custom-call | flops 1 | bytes 1 | tf_op jit(solution)/shard_map/pallas_call | solution.py:573
  173.7 12.1 %collective-permute-done.29 = bf16[128,2048]{1,0:T(8,128)(2,1)S(1)} collective-permute-done((bf16[128,2048]{1,0:T(8,128)(2,1)S(1)}, bf16[128,2048]{1,0:T(8,128)(2,1)S(1)}, u32[]{:S(2)}, u32[]{:S(2)}) %collective-permute-start.29) | collective-permute-done | bytes 524320 | tf_op jit(solution)/shard_map/ppermute | solution.py:44
  191.5 21.4 %collective-permute-done.30 = bf16[256,2048]{1,0:T(8,128)(2,1)} collective-permute-done((bf16[256,2048]{1,0:T(8,128)(2,1)S(1)}, bf16[256,2048]{1,0:T(8,128)(2,1)}, u32[]{:S(2)}, u32[]{:S(2)}) %collective-permute-start.30) | collective-permute-done | bytes 1048608 | tf_op jit(solution)/shard_map/ppermute | solution.py:48
  223.4 10.6 %collective-permute-done.34.refs_5_ = bf16[128,2048]{1,0:T(8,128)(2,1)S(1)} collective-permute-done((bf16[128,2048]{1,0:T(8,128)(2,1)S(1)}, bf16[128,2048]{1,0:T(8,128)(2,1)S(1)}, u32[]{:S(2)}, u32[]{:S(2)}) %collective-permute-start.34) | collective-permute-done | bytes 524320 | tf_op jit(solution)/shard_map/ppermute | solution.py:48
  236.1 9.1 %collective-permute-done.33.refs_4_ = bf16[128,2048]{1,0:T(8,128)(2,1)S(1)} collective-permute-done((bf16[128,2048]{1,0:T(8,128)(2,1)S(1)}, bf16[128,2048]{1,0:T(8,128)(2,1)S(1)}, u32[]{:S(2)}, u32[]{:S(2)}) %collective-permute-start.33) | collective-permute-done | bytes 524320 | tf_op jit(solution)/shard_map/ppermute | solution.py:48
  246.5 9.1 %collective-permute-done.36.refs_7_ = bf16[128,2048]{1,0:T(8,128)(2,1)S(1)} collective-permute-done((bf16[128,2048]{1,0:T(8,128)(2,1)S(1)}, bf16[128,2048]{1,0:T(8,128)(2,1)S(1)}, u32[]{:S(2)}, u32[]{:S(2)}) %collective-permute-start.36) | collective-permute-done | bytes 524320 | tf_op jit(solution)/shard_map/ppermute | solution.py:48
  259.6 13.7 %all-gather.8.cloned.1.call-done = bf16[6144,704]{1,0:T(8,128)(2,1)} async-done(((bf16[1536,704]{1,0:T(8,128)(2,1)}), bf16[6144,704]{1,0:T(8,128)(2,1)}) %all-gather.8.cloned.1.call-update) | async-done | bytes 8650768 | tf_op jit(solution)/shard_map/all_gather | solution.py:56
  273.3 29.8 %shard_map.233 = (bf16[2048,2048]{1,0:T(8,128)(2,1)}, bf16[2048,2048]{1,0:T(8,128)(2,1)}, bf16[2048,704]{1,0:T(8,128)(2,1)}, bf16[2048,1408]{1,0:T(8,128)(2,1)},...) custom-call(bf16[128,2048]{1,0:T(8,128)(2,1)} %copy-done.36, bf16[128,2048]{1,0:T(8,128)(2,1)} %collective-permute-done.38.refs_1_, ...), custom_call_target="tpu_custom_call" | custom-call | flops 1 | bytes 1 | tf_op jit(solution)/shard_map/pallas_call | solution.py:573
  303.3 30.0 %shard_map.234 = (bf16[2048,2048]{1,0:T(8,128)(2,1)}, bf16[2048,2048]{1,0:T(8,128)(2,1)}, bf16[2048,704]{1,0:T(8,128)(2,1)}, bf16[2048,1408]{1,0:T(8,128)(2,1)},...) custom-call(bf16[128,2048]{1,0:T(8,128)(2,1)} %copy-done.13, ...), custom_call_target="tpu_custom_call", output_to_operand_aliasing={{0}: (14, {}), {1}: (15, {}), {2}: (16, {}), {3}: (17, {})} | custom-call | flops 1 | bytes 1 | tf_op jit(solution)/shard_map/pallas_call | solution.py:573
  341.2 9.9 %convolution_convert_fusion.2 = bf16[2048,704]{0,1:T(8,128)(2,1)} fusion(bf16[2048,2048]{1,0:T(8,128)(2,1)} %get-tuple-element.89, bf16[2048,704]{1,0:T(8,128)(2,1)S(1)} %copy-done.11), kind=kOutput, calls=%fused_computation.10 | convolution fusion | flops 5907021824 | bytes 14155776 | tf_op jit(solution)/shard_map/dot_general | solution.py:32
  362.4 17.3 %convolution_convert_fusion = bf16[2048,1408]{1,0:T(8,128)(2,1)} fusion(bf16[2048,2048]{1,0:T(8,128)(2,1)S(1)} %copy-done.4, bf16[2048,1408]{1,0:T(8,128)(2,1)} %get-tuple-element.95), kind=kOutput, calls=%fused_computation.3 | convolution fusion | flops 11814043648 | bytes 19922944 | tf_op jit(solution)/shard_map/dot_general | solution.py:32
  379.7 4.2 collective-permute-done.53
  396.0 12.2 %collective-permute-done.66.refs_5_ = bf16[128,2048]{1,0:T(8,128)(2,1)} collective-permute-done((bf16[128,2048]{1,0:T(8,128)(2,1)}, bf16[128,2048]{1,0:T(8,128)(2,1)}, u32[]{:S(2)}, u32[]{:S(2)}) %collective-permute-start.66) | collective-permute-done | bytes 524320 | tf_op jit(solution)/shard_map/ppermute | solution.py:48
  409.2 9.8 %collective-permute-done.64.refs_4_ = bf16[128,2048]{1,0:T(8,128)(2,1)} collective-permute-done((bf16[128,2048]{1,0:T(8,128)(2,1)}, bf16[128,2048]{1,0:T(8,128)(2,1)}, u32[]{:S(2)}, u32[]{:S(2)}) %collective-permute-start.64) | collective-permute-done | bytes 524320 | tf_op jit(solution)/shard_map/ppermute | solution.py:48
  427.1 5.8 collective-permute-done.70.refs_7_
  442.6 19.3 %shard_map.235 = (bf16[2048,2048]{1,0:T(8,128)(2,1)}, bf16[2048,768]{1,0:T(8,128)(2,1)}, bf16[512,2048]{1,0:T(8,128)(2,1)}, bf16[512,2048]{1,0:T(8,128)(2,1)}) custom-call(s32[8,6]{1,0:T(8,128)} %copy.121.marks_ref, bf16[128,2048]{1,0:T(8,128)(2,1)} %collective-permute-done.58.refs_0_, bf16[128,2048]{1,0:T(8,128)(2,1)} %copy-done.61, ...), custom_call_target="tpu_custom_call" | custom-call | flops 23622320128 | bytes 1 | tf_op jit(solution)/shard_map/pallas_call | solution.py:573
  471.7 17.9 %shard_map.236 = (bf16[2048,2048]{1,0:T(8,128)(2,1)}, bf16[2048,768]{1,0:T(8,128)(2,1)}, bf16[512,2048]{1,0:T(8,128)(2,1)}, bf16[512,2048]{1,0:T(8,128)(2,1)}) custom-call(s32[8,6]{1,0:T(8,128)} %copy.125.marks_ref, bf16[128,2048]{1,0:T(8,128)(2,1)} %get-tuple-element.195.refs_0_, ...), custom_call_target="tpu_custom_call", output_to_operand_aliasing={{0}: (15, {}), {1}: (16, {})} | custom-call | flops 23622320128 | bytes 1 | tf_op jit(solution)/shard_map/pallas_call | solution.py:573
  495.0 4.2 select_convert_fusion
  503.6 12.1 %fusion.3 = (f32[2048]{0:T(1024)S(1)}, f32[2048]{0:T(1024)S(1)}, bf16[2048,768]{1,0:T(8,128)(2,1)}) fusion(bf16[2048,768]{1,0:T(8,128)(2,1)S(1)} %copy-done.2, f32[768]{0:T(1024)S(1)} %convert_reduce_fusion, f32[2048]{0:T(1024)S(1)} %copy-done.50, f32[2048]{0:T(1024)S(1)} %reshape.346, bf16[2048,2048]{1,0:T(8,128)(2,1)} %get-tuple-element.113, ...), kind=kOutput, calls=%fused_computation.7 | convolution fusion | flops 6459748352 | bytes 17861632 | tf_op jit(solution)/shard_map/dot_general | solution.py:32
  531.5 4.1 collective-permute-done.88
  542.5 9.4 %collective-permute-done.90 = f32[4,448]{1,0:T(4,128)S(1)} collective-permute-done((f32[4,448]{1,0:T(4,128)S(1)}, f32[4,448]{1,0:T(4,128)S(1)}, u32[]{:S(2)}, u32[]{:S(2)}) %collective-permute-start.90) | collective-permute-done | bytes 7200 | tf_op jit(solution)/shard_map/ppermute | solution.py:215
  565.4 4.3 fusion.26
  569.7 5.1 reduce-scatter.9.cloned.1.call-done
  575.9 12.3 %collective-permute-done.82.refs_2_ = bf16[2,64,2112]{2,1,0:T(8,128)(2,1)S(1)} collective-permute-done((bf16[2,64,2112]{2,1,0:T(8,128)(2,1)}, bf16[2,64,2112]{2,1,0:T(8,128)(2,1)S(1)}, u32[]{:S(2)}, u32[]{:S(2)}) %collective-permute-start.82) | collective-permute-done | bytes 540704 | tf_op jit(solution)/shard_map/ppermute | solution.py:162
  600.8 5.1 collective-permute-done.86.refs_2_
  (489 shorter events, 227.2 us)
Async XLA Ops:
  7.2 126.9 %all-gather.6.cloned.1.call-start = ((), (), s32[]{:S(2)}) async-start(), calls=%async_computation.5 | async-start | bytes 1310720 | tf_op jit(solution)/shard_map/all_gather | solution.py:56
  7.9 126.2 %all-gather.4.cloned.1.call-start = ((), (), s32[]{:S(2)}) async-start(), calls=%async_computation.4 | async-start | bytes 3932160 | tf_op jit(solution)/shard_map/all_gather | solution.py:56
  31.5 241.9 %all-gather.8.cloned.1.call-start = ((), (), s32[]{:S(2)}) async-start(), calls=%async_computation.6 | async-start | bytes 11796480 | tf_op jit(solution)/shard_map/all_gather | solution.py:56
  31.5 26.3 %collective-permute-start.4 = (bf16[256,2048]{1,0:T(8,128)(2,1)S(1)}, bf16[256,2048]{1,0:T(8,128)(2,1)}, u32[]{:S(2)}, u32[]{:S(2)}) collective-permute-start(bf16[256,2048]{1,0:T(8,128)(2,1)S(1)} %copy-done), channel_id=1, source_target_pairs={{0,4},{4,0},{1,5},{5,1},{2,6},{6,2},{3,7},{7,3},{8,12},{12,8},{9,1... | collective-permute-start | bytes 3145736 | tf_op jit(solution)/shard_map/ppermute | solution.py:48
  33.1 26.6 %collective-permute-start.3 = (bf16[256,2048]{1,0:T(8,128)(2,1)S(1)}, bf16[256,2048]{1,0:T(8,128)(2,1)}, u32[]{:S(2)}, u32[]{:S(2)}) collective-permute-start(bf16[256,2048]{1,0:T(8,128)(2,1)S(1)} %copy-done), channel_id=1, source_target_pairs={{0,2},{2,0},{1,3},{3,1},{4,6},{6,4},{5,7},{7,5},{8,10},{10,8},{9,1... | collective-permute-start | bytes 3145736 | tf_op jit(solution)/shard_map/ppermute | solution.py:44
  43.6 28.3 %collective-permute-start.14 = (bf16[2,3,64,704]{3,2,1,0:T(8,128)(2,1)}, bf16[2,3,64,704]{3,2,1,0:T(8,128)(2,1)S(1)}, u32[]{:S(2)}, u32[]{:S(2)}) collective-permute-start(bf16[2,3,64,704]{3,2,1,0:T(8,128)(2,1)} %pad_maximum_fusion.12), channel_id=1, source_target_pairs={{0,2},{2,0},{4,6},{6,4},{1,3},{3,1},{5,7},{7,5},{8,10},{10,8},{12,... | collective-permute-start | bytes 1622024 | tf_op jit(solution)/shard_map/ppermute | solution.py:162
  45.9 34.5 %collective-permute-start.15 = (bf16[2,3,64,704]{3,2,1,0:T(8,128)(2,1)}, bf16[2,3,64,704]{3,2,1,0:T(8,128)(2,1)S(1)}, u32[]{:S(2)}, u32[]{:S(2)}) collective-permute-start(bf16[2,3,64,704]{3,2,1,0:T(8,128)(2,1)} %pad_maximum_fusion.13), channel_id=1, source_target_pairs={{0,4},{2,6},{4,0},{6,2},{1,5},{3,7},{5,1},{7,3},{8,12},{10,14},{12... | collective-permute-start | bytes 1622024 | tf_op jit(solution)/shard_map/ppermute | solution.py:162
  47.3 37.2 %collective-permute-start.16 = (bf16[2,3,64,704]{3,2,1,0:T(8,128)(2,1)}, bf16[2,3,64,704]{3,2,1,0:T(8,128)(2,1)S(1)}, u32[]{:S(2)}, u32[]{:S(2)}) collective-permute-start(bf16[2,3,64,704]{3,2,1,0:T(8,128)(2,1)} %pad_maximum_fusion.14), channel_id=1, source_target_pairs={{0,6},{2,4},{4,2},{6,0},{1,7},{3,5},{5,3},{7,1},{8,14},{10,12},{12... | collective-permute-start | bytes 1622024 | tf_op jit(solution)/shard_map/ppermute | solution.py:162
  62.7 35.0 %collective-permute-start.6 = (bf16[128,2048]{1,0:T(8,128)(2,1)}, bf16[128,2048]{1,0:T(8,128)(2,1)}, u32[]{:S(2)}, u32[]{:S(2)}) collective-permute-start(bf16[128,2048]{1,0:T(8,128)(2,1)} %slice.433), channel_id=1, source_target_pairs={{0,2},{2,0},{1,3},{3,1},{4,6},{6,4},{5,7},{7,5},{8,10},{10,8},{9,1... | collective-permute-start | bytes 1572872 | tf_op jit(solution)/shard_map/ppermute | solution.py:44
  63.9 33.8 %collective-permute-start.7 = (bf16[128,2048]{1,0:T(8,128)(2,1)}, bf16[128,2048]{1,0:T(8,128)(2,1)}, u32[]{:S(2)}, u32[]{:S(2)}) collective-permute-start(bf16[128,2048]{1,0:T(8,128)(2,1)} %slice.434), channel_id=1, source_target_pairs={{0,4},{4,0},{1,5},{5,1},{2,6},{6,2},{3,7},{7,3},{8,12},{12,8},{9,1... | collective-permute-start | bytes 1572872 | tf_op jit(solution)/shard_map/ppermute | solution.py:48
  80.5 48.6 %collective-permute-start.19 = (bf16[256,2048]{1,0:T(8,128)(2,1)S(1)}, bf16[256,2048]{1,0:T(8,128)(2,1)}, u32[]{:S(2)}, u32[]{:S(2)}) collective-permute-start(bf16[256,2048]{1,0:T(8,128)(2,1)S(1)} %copy-done), channel_id=1, source_target_pairs={{0,1},{1,0},{2,3},{3,2},{4,5},{5,4},{6,7},{7,6},{8,9},{9,8},{10,11... | collective-permute-start | bytes 3145736 | tf_op jit(solution)/shard_map/ppermute | solution.py:52
  86.1 338.2 %reduce-scatter.5.cloned.1.call-start = ((), (), s32[]{:S(2)}) async-start(), calls=%async_computation.7 | async-start | bytes 3604480 | tf_op jit(solution)/shard_map/reduce_scatter | solution.py:60
  100.8 28.8 %collective-permute-start.21 = (bf16[256,2048]{1,0:T(8,128)(2,1)}, bf16[256,2048]{1,0:T(8,128)(2,1)S(1)}, u32[]{:S(2)}, u32[]{:S(2)}) collective-permute-start(bf16[256,2048]{1,0:T(8,128)(2,1)} %collective-permute-done.4.refs_2_), channel_id=1, source_target_pairs={{0,1},{1,0},{2,3},{3,2},{4,5},{5,4},{6,7},{7,6},{8,9},{9,8},{10,11... | collective-permute-start | bytes 3145736 | tf_op jit(solution)/shard_map/ppermute | solution.py:52
  100.8 25.9 %collective-permute-start.17 = (bf16[256,2048]{1,0:T(8,128)(2,1)}, bf16[256,2048]{1,0:T(8,128)(2,1)}, u32[]{:S(2)}, u32[]{:S(2)}) collective-permute-start(bf16[256,2048]{1,0:T(8,128)(2,1)} %fusion.14.refs_8_), channel_id=1, source_target_pairs={{0,2},{2,0},{1,3},{3,1},{4,6},{6,4},{5,7},{7,5},{8,10},{10,8},{9,1... | collective-permute-start | bytes 3145736 | tf_op jit(solution)/shard_map/ppermute | solution.py:44
  102.9 31.2 %collective-permute-start.20 = (bf16[256,2048]{1,0:T(8,128)(2,1)}, bf16[256,2048]{1,0:T(8,128)(2,1)S(1)}, u32[]{:S(2)}, u32[]{:S(2)}) collective-permute-start(bf16[256,2048]{1,0:T(8,128)(2,1)} %collective-permute-done.3.refs_1_), channel_id=1, source_target_pairs={{0,1},{1,0},{2,3},{3,2},{4,5},{5,4},{6,7},{7,6},{8,9},{9,8},{10,11... | collective-permute-start | bytes 3145736 | tf_op jit(solution)/shard_map/ppermute | solution.py:52
  190.9 27.6 %collective-permute-start.45 = (bf16[256,2048]{1,0:T(8,128)(2,1)}, bf16[256,2048]{1,0:T(8,128)(2,1)S(1)}, u32[]{:S(2)}, u32[]{:S(2)}) collective-permute-start(bf16[256,2048]{1,0:T(8,128)(2,1)} %fusion.14.refs_8_), channel_id=1, source_target_pairs={{0,1},{1,0},{2,3},{3,2},{4,5},{5,4},{6,7},{7,6},{8,9},{9,8},{10,11... | collective-permute-start | bytes 3145736 | tf_op jit(solution)/shard_map/ppermute | solution.py:52
  190.9 28.7 %collective-permute-start.47 = (bf16[256,2048]{1,0:T(8,128)(2,1)}, bf16[256,2048]{1,0:T(8,128)(2,1)S(1)}, u32[]{:S(2)}, u32[]{:S(2)}) collective-permute-start(bf16[256,2048]{1,0:T(8,128)(2,1)} %collective-permute-done.18.refs_10_), channel_id=1, source_target_pairs={{0,1},{1,0},{2,3},{3,2},{4,5},{5,4},{6,7},{7,6},{8,9},{9,8},{10,11... | collective-permute-start | bytes 3145736 | tf_op jit(solution)/shard_map/ppermute | solution.py:52
  191.5 30.4 %collective-permute-start.46 = (bf16[256,2048]{1,0:T(8,128)(2,1)}, bf16[256,2048]{1,0:T(8,128)(2,1)S(1)}, u32[]{:S(2)}, u32[]{:S(2)}) collective-permute-start(bf16[256,2048]{1,0:T(8,128)(2,1)} %collective-permute-done.17.refs_9_), channel_id=1, source_target_pairs={{0,1},{1,0},{2,3},{3,2},{4,5},{5,4},{6,7},{7,6},{8,9},{9,8},{10,11... | collective-permute-start | bytes 3145736 | tf_op jit(solution)/shard_map/ppermute | solution.py:52
  303.1 30.1 %collective-permute-start.50 = (bf16[1024,2048]{1,0:T(8,128)(2,1)}, bf16[1024,2048]{1,0:T(8,128)(2,1)S(1)}, u32[]{:S(2)}, u32[]{:S(2)}) collective-permute-start(bf16[1024,2048]{1,0:T(8,128)(2,1)} %get-tuple-element.87), channel_id=1, source_target_pairs={{0,1},{1,0},{2,3},{3,2},{4,5},{5,4},{6,7},{7,6},{8,9},{9,8},{10,11... | collective-permute-start | bytes 12582920 | tf_op jit(solution)/shard_map/ppermute | solution.py:52
  351.2 164.9 %reduce-scatter.7.cloned.1.call-start = ((), (), s32[]{:S(2)}) async-start(), calls=%async_computation.8 | async-start | bytes 7208960 | tf_op jit(solution)/shard_map/reduce_scatter | solution.py:60
  392.0 43.0 %collective-permute-start.55 = (bf16[1024,2048]{1,0:T(8,128)(2,1)}, bf16[1024,2048]{1,0:T(8,128)(2,1)}, u32[]{:S(2)}, u32[]{:S(2)}) collective-permute-start(bf16[1024,2048]{1,0:T(8,128)(2,1)} %get-tuple-element.98), channel_id=1, source_target_pairs={{0,1},{1,0},{2,3},{3,2},{4,5},{5,4},{6,7},{7,6},{8,9},{9,8},{10,11... | collective-permute-start | bytes 12582920 | tf_op jit(solution)/shard_map/ppermute | solution.py:52
  393.9 180.9 %reduce-scatter.9.cloned.1.call-start = ((), (), s32[]{:S(2)}) async-start(), calls=%async_computation.9 | async-start | bytes 3932160 | tf_op jit(solution)/shard_map/reduce_scatter | solution.py:60
  461.9 56.6 %collective-permute-start.74 = (bf16[512,2048]{1,0:T(8,128)(2,1)}, bf16[512,2048]{1,0:T(8,128)(2,1)}, u32[]{:S(2)}, u32[]{:S(2)}) collective-permute-start(bf16[512,2048]{1,0:T(8,128)(2,1)} %get-tuple-element.111), channel_id=1, source_target_pairs={{0,1},{1,0},{2,3},{3,2},{4,5},{5,4},{6,7},{7,6},{8,9},{9,8},{10,11... | collective-permute-start | bytes 6291464 | tf_op jit(solution)/shard_map/ppermute | solution.py:52
  462.0 37.2 %collective-permute-start.75 = (bf16[512,2048]{1,0:T(8,128)(2,1)}, bf16[512,2048]{1,0:T(8,128)(2,1)}, u32[]{:S(2)}, u32[]{:S(2)}) collective-permute-start(bf16[512,2048]{1,0:T(8,128)(2,1)} %get-tuple-element.101), channel_id=1, source_target_pairs={{0,1},{1,0},{2,3},{3,2},{4,5},{5,4},{6,7},{7,6},{8,9},{9,8},{10,11... | collective-permute-start | bytes 6291464 | tf_op jit(solution)/shard_map/ppermute | solution.py:52
  467.2 25.5 %collective-permute-start.72 = (bf16[256,2048]{1,0:T(8,128)(2,1)}, bf16[256,2048]{1,0:T(8,128)(2,1)}, u32[]{:S(2)}, u32[]{:S(2)}) collective-permute-start(bf16[256,2048]{1,0:T(8,128)(2,1)} %pad_maximum_fusion.7), channel_id=1, source_target_pairs={{0,2},{2,0},{1,3},{3,1},{4,6},{6,4},{5,7},{7,5},{8,10},{10,8},{9,1... | collective-permute-start | bytes 3145736 | tf_op jit(solution)/shard_map/ppermute | solution.py:44
  469.8 25.2 %collective-permute-start.73 = (bf16[256,2048]{1,0:T(8,128)(2,1)}, bf16[256,2048]{1,0:T(8,128)(2,1)}, u32[]{:S(2)}, u32[]{:S(2)}) collective-permute-start(bf16[256,2048]{1,0:T(8,128)(2,1)} %pad_maximum_fusion.8), channel_id=1, source_target_pairs={{0,4},{4,0},{1,5},{5,1},{2,6},{6,2},{3,7},{7,3},{8,12},{12,8},{9,1... | collective-permute-start | bytes 3145736 | tf_op jit(solution)/shard_map/ppermute | solution.py:48
  515.9 91.4 %reduce-scatter.11.cloned.1.call-start = ((), (), s32[]{:S(2)}) async-start(), calls=%async_computation.10 | async-start | bytes 1310720 | tf_op jit(solution)/shard_map/reduce_scatter | solution.py:60
  518.4 39.6 %collective-permute-start.80 = (bf16[4,64,2112]{2,1,0:T(8,128)(2,1)S(1)}, bf16[4,64,2112]{2,1,0:T(8,128)(2,1)}, u32[]{:S(2)}, u32[]{:S(2)}) collective-permute-start(bf16[4,64,2112]{2,1,0:T(8,128)(2,1)S(1)} %pad_maximum_fusion.2), channel_id=1, source_target_pairs={{0,1},{1,0},{2,3},{3,2},{4,5},{5,4},{6,7},{7,6},{8,9},{9,8},{10,11... | collective-permute-start | bytes 3244040 | tf_op jit(solution)/shard_map/ppermute | solution.py:52
  523.0 35.0 %collective-permute-start.78 = (bf16[256,2048]{1,0:T(8,128)(2,1)}, bf16[256,2048]{1,0:T(8,128)(2,1)}, u32[]{:S(2)}, u32[]{:S(2)}) collective-permute-start(bf16[256,2048]{1,0:T(8,128)(2,1)} %pad_maximum_fusion.9), channel_id=1, source_target_pairs={{0,2},{2,0},{1,3},{3,1},{4,6},{6,4},{5,7},{7,5},{8,10},{10,8},{9,1... | collective-permute-start | bytes 3145736 | tf_op jit(solution)/shard_map/ppermute | solution.py:44
  527.3 30.7 %collective-permute-start.79 = (bf16[256,2048]{1,0:T(8,128)(2,1)}, bf16[256,2048]{1,0:T(8,128)(2,1)}, u32[]{:S(2)}, u32[]{:S(2)}) collective-permute-start(bf16[256,2048]{1,0:T(8,128)(2,1)} %pad_maximum_fusion.10), channel_id=1, source_target_pairs={{0,4},{4,0},{1,5},{5,1},{2,6},{6,2},{3,7},{7,3},{8,12},{12,8},{9,1... | collective-permute-start | bytes 3145736 | tf_op jit(solution)/shard_map/ppermute | solution.py:48
  561.6 26.6 %collective-permute-start.82 = (bf16[2,64,2112]{2,1,0:T(8,128)(2,1)}, bf16[2,64,2112]{2,1,0:T(8,128)(2,1)S(1)}, u32[]{:S(2)}, u32[]{:S(2)}) collective-permute-start(bf16[2,64,2112]{2,1,0:T(8,128)(2,1)} %pad_maximum_fusion.16), channel_id=1, source_target_pairs={{0,4},{2,6},{4,0},{6,2},{1,5},{3,7},{5,1},{7,3},{8,12},{10,14},{12... | collective-permute-start | bytes 1622024 | tf_op jit(solution)/shard_map/ppermute | solution.py:162
  563.2 25.0 %collective-permute-start.83 = (bf16[2,64,2112]{2,1,0:T(8,128)(2,1)}, bf16[2,64,2112]{2,1,0:T(8,128)(2,1)S(1)}, u32[]{:S(2)}, u32[]{:S(2)}) collective-permute-start(bf16[2,64,2112]{2,1,0:T(8,128)(2,1)} %pad_maximum_fusion.17), channel_id=1, source_target_pairs={{0,6},{2,4},{4,2},{6,0},{1,7},{3,5},{5,3},{7,1},{8,14},{10,12},{12... | collective-permute-start | bytes 1622024 | tf_op jit(solution)/shard_map/ppermute | solution.py:162
  (133 other events, 1529.6 us)
Sparse Core Ops, SparseCore 0:
  9.6 30.6 all-gather.5
  42.4 62.9 all-gather.3
  107.0 166.2 all-gather.7
  351.3 52.5 reduce-scatter.4
  406.0 102.0 reduce-scatter.6
  516.0 58.7 reduce-scatter.8
  577.2 27.1 reduce-scatter.10
